TPU v7x, 32 devices: a whole 2x2x4 slice. The times are simulated.
32 devices in a mesh: fsdp: 8 (over y, x, core), shard: 4 (over z).
Axes of the slice: x: 2, y: 2, z: 4, core: 2. Of those that a mesh axis runs over, the one named last changes fastest.
Arguments:
- tokens: bfloat16 [4096, 1024], P(('fsdp', 'shard')), may hold values from -6 to 6
- cotangent: bfloat16 [4096, 1024], P(('fsdp', 'shard')), may hold values from -6 to 6
- starts: int32 [4096], P(('fsdp', 'shard')), may hold values from 0 to 127, as said below
- counts: int32 [32], P(('fsdp', 'shard')), may hold values from 64 to 128, as said below
- attn_gain: bfloat16 [4, 256], P('shard', 'fsdp'), may hold values from 0.5 to 1.5
- attn_shift: bfloat16 [4, 256], P('shard', 'fsdp'), may hold values from -1.75 to 1.75
- w_qkv: bfloat16 [1024, 3, 1024], P('fsdp', None, 'shard'), may hold values from -0.1875 to 0.1875
- query_bias: bfloat16 [4, 256], P('shard', 'fsdp'), may hold values from -1.75 to 1.75
- value_bias: bfloat16 [4, 256], P('shard', 'fsdp'), may hold values from -1.75 to 1.75
- w_proj: bfloat16 [1024, 1024], P('shard', 'fsdp'), may hold values from -0.75 to 0.75
- proj_bias: bfloat16 [4, 256], P('shard', 'fsdp'), may hold values from -1.75 to 1.75
- mlp_gain: bfloat16 [4, 256], P('shard', 'fsdp'), may hold values from 0.5 to 1.5
- mlp_shift: bfloat16 [4, 256], P('shard', 'fsdp'), may hold values from -1.75 to 1.75
- w_up: bfloat16 [1024, 4096], P('fsdp', 'shard'), may hold values from -0.1875 to 0.1875
- up_bias: bfloat16 [4, 1024], P('shard', 'fsdp'), may hold values from -1.75 to 1.75
- w_down: bfloat16 [4096, 1024], P('shard', 'fsdp'), may hold values from -0.375 to 0.375
- down_bias: bfloat16 [4, 256], P('shard', 'fsdp'), may hold values from -1.75 to 1.75
Outputs:
- block_out: bfloat16 [4096, 1024], P(('fsdp', 'shard'))
- grad_tokens: float32 [4096, 1024], P(('fsdp', 'shard'))
- grad_attn_gain: float32 [4, 256], P('shard', 'fsdp')
- grad_attn_shift: float32 [4, 256], P('shard', 'fsdp')
- grad_w_qkv: float32 [1024, 3, 1024], P('fsdp', None, 'shard')
- grad_query_bias: float32 [4, 256], P('shard', 'fsdp')
- grad_value_bias: float32 [4, 256], P('shard', 'fsdp')
- grad_w_proj: float32 [1024, 1024], P('shard', 'fsdp')
- grad_proj_bias: float32 [4, 256], P('shard', 'fsdp')
- grad_mlp_gain: float32 [4, 256], P('shard', 'fsdp')
- grad_mlp_shift: float32 [4, 256], P('shard', 'fsdp')
- grad_w_up: float32 [1024, 4096], P('fsdp', 'shard')
- grad_up_bias: float32 [4, 1024], P('shard', 'fsdp')
- grad_w_down: float32 [4096, 1024], P('shard', 'fsdp')
- grad_down_bias: float32 [4, 256], P('shard', 'fsdp')
Inputs may be any that keep to these rules, and one draw needn't show every extreme that they name: starts[s] is the index, inside the block of 128 slots that holds slot s, of the first slot of s's sequence; a sequence's slots are consecutive in one block and never cross blocks; slots at or past the block's live count start themselves; in every draw some block holds one sequence over all 128 slots. The live slots are the first counts[b] of block b; some block is full in every draw.
All inputs are finite; a program needn't handle non-finite values.
Results may differ from a plain program's by a relative error of at most 0.012.
Values may be sent and summed in bfloat16 or wider, within the bound.
No kernel may reach another device: no remote copies, remote signals or barrier semaphores. Data moves between devices by JAX's collectives and lax.ppermute only.
A program may use at most 128 MiB of HBM per device.

v0:
```python
import jax
import jax.numpy as jnp
from jax import lax
from jax.sharding import PartitionSpec as P

HEAD_DIM = 64


NORM_EPS = 1e-05
NEG_FILL = -1e30


def layer_norm(inputs, norm_gain, norm_shift):
    center = inputs - jnp.mean(inputs, axis=-1, keepdims=True)
    variance = jnp.mean(center * center, axis=-1, keepdims=True)
    return center * lax.rsqrt(variance + NORM_EPS) * norm_gain + norm_shift


def gelu_tanh(values):
    return jax.nn.gelu(values, approximate=True)


def split_heads(qkv_full, quarter, slot_count):
    row_count = qkv_full.shape[0]
    grid = (row_count // slot_count, slot_count, quarter // HEAD_DIM, HEAD_DIM)
    query_part = qkv_full[:, :quarter].reshape(grid)
    key_part = qkv_full[:, quarter : 2 * quarter].reshape(grid)
    value_part = qkv_full[:, 2 * quarter :].reshape(grid)
    return (query_part, key_part, value_part)


def score_blocks(query_part, key_part, starts_grid):
    scores = jnp.einsum("bqhd,bkhd->bhqk", query_part, key_part, preferred_element_type=jnp.float32)
    scores = scores * HEAD_DIM ** (-0.5)
    positions = jnp.arange(scores.shape[2], dtype=jnp.int32)
    visible = (positions[None, None, :] >= starts_grid[:, :, None]) & (
        positions[None, None, :] <= positions[None, :, None]
    )
    return jnp.where(visible[:, None], scores, NEG_FILL)


def collect(params):
    over = (
        lax.all_gather(params[0], "fsdp", axis=1, tiled=True),
        lax.all_gather(params[1], "fsdp", axis=1, tiled=True),
        lax.all_gather(params[2], "fsdp", axis=0, tiled=True),
        lax.all_gather(params[3], "fsdp", axis=1, tiled=True),
        lax.all_gather(params[4], "fsdp", axis=1, tiled=True),
        lax.all_gather(params[5], "fsdp", axis=1, tiled=True),
        lax.all_gather(params[6], "fsdp", axis=1, tiled=True),
        lax.all_gather(params[7], "fsdp", axis=1, tiled=True),
        lax.all_gather(params[8], "fsdp", axis=1, tiled=True),
        lax.all_gather(params[9], "fsdp", axis=0, tiled=True),
        lax.all_gather(params[10], "fsdp", axis=1, tiled=True),
        lax.all_gather(params[11], "fsdp", axis=1, tiled=True),
        lax.all_gather(params[12], "fsdp", axis=1, tiled=True),
    )
    vectors = (
        lax.all_gather(over[0], "shard", axis=0, tiled=True),
        lax.all_gather(over[1], "shard", axis=0, tiled=True),
        lax.all_gather(over[6], "shard", axis=0, tiled=True),
        lax.all_gather(over[7], "shard", axis=0, tiled=True),
        lax.all_gather(over[8], "shard", axis=0, tiled=True),
        lax.all_gather(over[12], "shard", axis=0, tiled=True),
    )
    full = (
        vectors[0].reshape(-1),
        vectors[1].reshape(-1),
        over[2],
        over[3].reshape(-1),
        over[4].reshape(-1),
        over[5],
        vectors[2].reshape(-1),
        vectors[3].reshape(-1),
        vectors[4].reshape(-1),
        over[9],
        over[10].reshape(-1),
        over[11],
        vectors[5].reshape(-1),
    )
    return full


def spread(grads, shard_count):
    (
        g_attn_gain,
        g_attn_shift,
        g_qkv,
        g_query_bias,
        g_value_bias,
        g_proj,
        g_proj_bias,
        g_mlp_gain,
        g_mlp_shift,
        g_up,
        g_up_bias,
        g_down,
        g_down_bias,
    ) = grads
    summed = (
        lax.psum_scatter(
            g_attn_gain.reshape(shard_count, -1), "shard", scatter_dimension=0, tiled=True
        ),
        lax.psum_scatter(
            g_attn_shift.reshape(shard_count, -1), "shard", scatter_dimension=0, tiled=True
        ),
        lax.psum_scatter(
            g_proj_bias.reshape(shard_count, -1), "shard", scatter_dimension=0, tiled=True
        ),
        lax.psum_scatter(
            g_mlp_gain.reshape(shard_count, -1), "shard", scatter_dimension=0, tiled=True
        ),
        lax.psum_scatter(
            g_mlp_shift.reshape(shard_count, -1), "shard", scatter_dimension=0, tiled=True
        ),
        lax.psum_scatter(
            g_down_bias.reshape(shard_count, -1), "shard", scatter_dimension=0, tiled=True
        ),
    )
    pieces = (
        summed[0],
        summed[1],
        g_qkv,
        g_query_bias.reshape(1, -1),
        g_value_bias.reshape(1, -1),
        g_proj,
        summed[2],
        summed[3],
        summed[4],
        g_up,
        g_up_bias.reshape(1, -1),
        g_down,
        summed[5],
    )
    owned = (
        lax.psum_scatter(pieces[0], "fsdp", scatter_dimension=1, tiled=True),
        lax.psum_scatter(pieces[1], "fsdp", scatter_dimension=1, tiled=True),
        lax.psum_scatter(pieces[2], "fsdp", scatter_dimension=0, tiled=True),
        lax.psum_scatter(pieces[3], "fsdp", scatter_dimension=1, tiled=True),
        lax.psum_scatter(pieces[4], "fsdp", scatter_dimension=1, tiled=True),
        lax.psum_scatter(pieces[5], "fsdp", scatter_dimension=1, tiled=True),
        lax.psum_scatter(pieces[6], "fsdp", scatter_dimension=1, tiled=True),
        lax.psum_scatter(pieces[7], "fsdp", scatter_dimension=1, tiled=True),
        lax.psum_scatter(pieces[8], "fsdp", scatter_dimension=1, tiled=True),
        lax.psum_scatter(pieces[9], "fsdp", scatter_dimension=0, tiled=True),
        lax.psum_scatter(pieces[10], "fsdp", scatter_dimension=1, tiled=True),
        lax.psum_scatter(pieces[11], "fsdp", scatter_dimension=1, tiled=True),
        lax.psum_scatter(pieces[12], "fsdp", scatter_dimension=1, tiled=True),
    )
    return owned


def forward_pass(full, tokens, starts, live):
    (
        attn_gain,
        attn_shift,
        w_qkv,
        query_bias,
        value_bias,
        w_proj,
        proj_bias,
        mlp_gain,
        mlp_shift,
        w_up,
        up_bias,
        w_down,
        down_bias,
    ) = full
    slot_count = tokens.shape[0]
    width = tokens.shape[1]
    tokens_wide = tokens.astype(jnp.float32)
    normed_attn = layer_norm(
        tokens_wide, attn_gain.astype(jnp.float32), attn_shift.astype(jnp.float32)
    )
    act_attn = normed_attn.astype(jnp.bfloat16)
    act_rows, start_rows = (
        lax.all_gather(act_attn, "shard", axis=0, tiled=True),
        lax.all_gather(starts, "shard", axis=0, tiled=True),
    )
    quarter = w_qkv.shape[2]
    row_count = act_rows.shape[0]
    qkv_bias = jnp.concatenate([query_bias, jnp.zeros_like(query_bias), value_bias]).astype(
        jnp.float32
    )
    qkv_full = (
        jnp.dot(act_rows, w_qkv.reshape(width, 3 * quarter), preferred_element_type=jnp.float32)
        + qkv_bias
    ).astype(jnp.bfloat16)
    query_part, key_part, value_part = split_heads(qkv_full, quarter, slot_count)
    starts_grid = start_rows.reshape(row_count // slot_count, slot_count)
    scores = score_blocks(query_part, key_part, starts_grid)
    row_max = jnp.max(scores, axis=-1, keepdims=True)
    log_total = row_max + jnp.log(jnp.sum(jnp.exp(scores - row_max), axis=-1, keepdims=True))
    probs_low = jnp.exp(scores - log_total).astype(jnp.bfloat16)
    mixed = jnp.einsum("bhqk,bkhd->bqhd", probs_low, value_part, preferred_element_type=jnp.float32)
    mixed = mixed.reshape(row_count, quarter).astype(jnp.bfloat16)
    attn_term = lax.psum_scatter(
        jnp.dot(mixed, w_proj, preferred_element_type=jnp.float32),
        "shard",
        scatter_dimension=0,
        tiled=True,
    )
    hidden_one = tokens_wide + attn_term + proj_bias.astype(jnp.float32)
    normed_mlp = layer_norm(hidden_one, mlp_gain.astype(jnp.float32), mlp_shift.astype(jnp.float32))
    act_mlp = normed_mlp.astype(jnp.bfloat16)
    mlp_inputs = lax.all_gather(act_mlp, "shard", axis=0, tiled=True)
    pre_act = jnp.dot(mlp_inputs, w_up, preferred_element_type=jnp.float32) + up_bias.astype(
        jnp.float32
    )
    act_up = gelu_tanh(pre_act).astype(jnp.bfloat16)
    mlp_term = lax.psum_scatter(
        jnp.dot(act_up, w_down, preferred_element_type=jnp.float32),
        "shard",
        scatter_dimension=0,
        tiled=True,
    )
    block_out = (hidden_one + mlp_term + down_bias.astype(jnp.float32)) * live
    saved = (
        act_rows,
        starts_grid,
        qkv_full,
        log_total,
        mixed,
        hidden_one,
        mlp_inputs,
        pre_act,
        act_up,
    )
    return (block_out.astype(jnp.bfloat16), saved)


def backward_pass(full, saved, tokens, cotangent, live):
    (
        attn_gain,
        attn_shift,
        w_qkv,
        query_bias,
        value_bias,
        w_proj,
        proj_bias,
        mlp_gain,
        mlp_shift,
        w_up,
        up_bias,
        w_down,
        down_bias,
    ) = full
    act_rows, starts_grid, qkv_full, log_total, mixed, hidden_one, mlp_inputs, pre_act, act_up = (
        saved
    )
    slot_count = tokens.shape[0]
    width = tokens.shape[1]
    quarter = w_qkv.shape[2]
    row_count = act_rows.shape[0]
    tokens_wide = tokens.astype(jnp.float32)
    grad_out = cotangent.astype(jnp.float32) * live
    grad_low = grad_out.astype(jnp.bfloat16)
    grad_low_rows = lax.all_gather(grad_low, "shard", axis=0, tiled=True)
    g_down = jnp.dot(act_up.T, grad_low_rows, preferred_element_type=jnp.float32)
    g_down_bias = jnp.sum(grad_out, axis=0)
    grad_act = jnp.dot(grad_low_rows, w_down.T, preferred_element_type=jnp.float32)
    gelu_value, gelu_back = jax.vjp(gelu_tanh, pre_act)
    (grad_pre,) = gelu_back(grad_act)
    grad_pre_low = grad_pre.astype(jnp.bfloat16)
    g_up = jnp.dot(mlp_inputs.T, grad_pre_low, preferred_element_type=jnp.float32)
    g_up_bias = jnp.sum(grad_pre, axis=0)
    grad_normed = lax.psum_scatter(
        jnp.dot(grad_pre_low, w_up.T, preferred_element_type=jnp.float32),
        "shard",
        scatter_dimension=0,
        tiled=True,
    )
    norm_value, norm_back = jax.vjp(
        layer_norm, hidden_one, mlp_gain.astype(jnp.float32), mlp_shift.astype(jnp.float32)
    )
    grad_hidden_part, g_mlp_gain, g_mlp_shift = norm_back(grad_normed)
    grad_hidden = grad_out + grad_hidden_part
    grad_hidden_low = grad_hidden.astype(jnp.bfloat16)
    hidden_rows = lax.all_gather(grad_hidden_low, "shard", axis=0, tiled=True)
    g_proj = jnp.dot(mixed.T, hidden_rows, preferred_element_type=jnp.float32)
    g_proj_bias = jnp.sum(grad_hidden, axis=0)
    grad_mixed = jnp.dot(hidden_rows, w_proj.T, preferred_element_type=jnp.float32).astype(
        jnp.bfloat16
    )
    grad_mixed = grad_mixed.reshape(
        row_count // slot_count, slot_count, quarter // HEAD_DIM, HEAD_DIM
    )
    query_part, key_part, value_part = split_heads(qkv_full, quarter, slot_count)
    scores = score_blocks(query_part, key_part, starts_grid)
    attn_probs = jnp.exp(scores - log_total)
    probs_low = attn_probs.astype(jnp.bfloat16)
    grad_probs = jnp.einsum(
        "bqhd,bkhd->bhqk", grad_mixed, value_part, preferred_element_type=jnp.float32
    )
    grad_value = jnp.einsum(
        "bhqk,bqhd->bkhd", probs_low, grad_mixed, preferred_element_type=jnp.float32
    )
    row_dot = jnp.sum(attn_probs * grad_probs, axis=-1, keepdims=True)
    grad_scores = (attn_probs * (grad_probs - row_dot) * HEAD_DIM ** (-0.5)).astype(jnp.bfloat16)
    grad_query = jnp.einsum(
        "bhqk,bkhd->bqhd", grad_scores, key_part, preferred_element_type=jnp.float32
    )
    grad_key = jnp.einsum(
        "bhqk,bqhd->bkhd", grad_scores, query_part, preferred_element_type=jnp.float32
    )
    grad_query = grad_query.reshape(row_count, quarter)
    grad_key = grad_key.reshape(row_count, quarter)
    grad_value = grad_value.reshape(row_count, quarter)
    g_query_bias = jnp.sum(grad_query, axis=0)
    g_value_bias = jnp.sum(grad_value, axis=0)
    grad_qkv_low = jnp.concatenate([grad_query, grad_key, grad_value], axis=1).astype(jnp.bfloat16)
    g_qkv = jnp.dot(act_rows.T, grad_qkv_low, preferred_element_type=jnp.float32).reshape(
        width, 3, quarter
    )
    qkv_matrix = w_qkv.reshape(width, 3 * quarter)
    grad_normed_attn = lax.psum_scatter(
        jnp.dot(grad_qkv_low, qkv_matrix.T, preferred_element_type=jnp.float32),
        "shard",
        scatter_dimension=0,
        tiled=True,
    )
    first_value, first_back = jax.vjp(
        layer_norm, tokens_wide, attn_gain.astype(jnp.float32), attn_shift.astype(jnp.float32)
    )
    grad_in_part, g_attn_gain, g_attn_shift = first_back(grad_normed_attn)
    grad_in = grad_hidden + grad_in_part
    grads = (
        g_attn_gain,
        g_attn_shift,
        g_qkv,
        g_query_bias,
        g_value_bias,
        g_proj,
        g_proj_bias,
        g_mlp_gain,
        g_mlp_shift,
        g_up,
        g_up_bias,
        g_down,
        g_down_bias,
    )
    return (grad_in, grads)


def on_device(
    tokens,
    cotangent,
    starts,
    counts,
    attn_gain,
    attn_shift,
    w_qkv,
    query_bias,
    value_bias,
    w_proj,
    proj_bias,
    mlp_gain,
    mlp_shift,
    w_up,
    up_bias,
    w_down,
    down_bias,
):
    shard_count = lax.axis_size("shard")
    params = (
        attn_gain,
        attn_shift,
        w_qkv,
        query_bias,
        value_bias,
        w_proj,
        proj_bias,
        mlp_gain,
        mlp_shift,
        w_up,
        up_bias,
        w_down,
        down_bias,
    )
    full_forward = collect(params)
    live = (jnp.arange(tokens.shape[0], dtype=jnp.int32) < counts[0]).astype(jnp.float32)[:, None]
    output_low, saved = forward_pass(full_forward, tokens, starts, live)
    full_backward = collect(params)
    grad_in, grads = backward_pass(full_backward, saved, tokens, cotangent, live)
    owned = spread(grads, shard_count)
    return (
        output_low,
        grad_in,
        owned[0],
        owned[1],
        owned[2],
        owned[3],
        owned[4],
        owned[5],
        owned[6],
        owned[7],
        owned[8],
        owned[9],
        owned[10],
        owned[11],
        owned[12],
    )


def solution(mesh):
    in_specs = (
        P(("fsdp", "shard"), None),
        P(("fsdp", "shard"), None),
        P(("fsdp", "shard")),
        P(("fsdp", "shard")),
        P("shard", "fsdp"),
        P("shard", "fsdp"),
        P("fsdp", None, "shard"),
        P("shard", "fsdp"),
        P("shard", "fsdp"),
        P("shard", "fsdp"),
        P("shard", "fsdp"),
        P("shard", "fsdp"),
        P("shard", "fsdp"),
        P("fsdp", "shard"),
        P("shard", "fsdp"),
        P("shard", "fsdp"),
        P("shard", "fsdp"),
    )
    out_specs = (
        P(("fsdp", "shard"), None),
        P(("fsdp", "shard"), None),
        P("shard", "fsdp"),
        P("shard", "fsdp"),
        P("fsdp", None, "shard"),
        P("shard", "fsdp"),
        P("shard", "fsdp"),
        P("shard", "fsdp"),
        P("shard", "fsdp"),
        P("shard", "fsdp"),
        P("shard", "fsdp"),
        P("fsdp", "shard"),
        P("shard", "fsdp"),
        P("shard", "fsdp"),
        P("shard", "fsdp"),
    )
    return jax.shard_map(
        on_device, mesh=mesh, in_specs=in_specs, out_specs=out_specs, check_vma=False
    )
```

profile of v0, /device:TPU:0, one launch (start us, length us, event | category | flops | bytes accessed | tf_op | source)
XLA Modules:
  0.0 999.4 jit_solution(1785968189932253058)
XLA Ops:
  15.9 15.1 %all-reduce.15 = (bf16[256]{0:T(256)(128)(2,1)S(1)}, bf16[256]{0:T(256)(128)(2,1)S(1)}, bf16[256]{0:T(256)(128)(2,1)S(1)}, bf16[256]{0:T(256)(128)(2,1)S(1)}, bf...) all-reduce(bf16[256]{0:T(256)(128)(2,1)S(1)} %dynamic-update-slice., ...), channel_id=1, replica_groups=mesh['fsdp'=8,'shard'=4] {'fsdp'}, use_global_device_ids=true, to_apply=%add.1 | all-reduce | flops 2048 | bytes 8192
  79.9 27.8 %all-gather.17.cloned.1.call-done = bf16[1024,3,256]{0,2,1:T(8,128)(2,1)} async-done(((bf16[128,3,256]{0,2,1:T(8,128)(2,1)}), bf16[1024,3,256]{0,2,1:T(8,128)(2,1)}) %all-gather.17.cloned.1.call-update) | async-done | bytes 1572880 | tf_op jit(solution)/shard_map/all_gather | solution.py:46
  144.8 14.4 %reduce-scatter.36.cloned.1.call-done = f32[128,1024]{1,0:T(8,128)} async-done(((f32[512,1024]{1,0:T(8,128)}), f32[128,1024]{1,0:T(8,128)}) %reduce-scatter.36.cloned.1.call-update) | async-done | bytes 524304 | tf_op jit(solution)/shard_map/reduce_scatter | solution.py:197
  172.8 15.5 %all-gather.21.cloned.1.call-done = bf16[1024,1024]{1,0:T(8,128)(2,1)} async-done(((bf16[128,1024]{1,0:T(8,128)(2,1)}), bf16[1024,1024]{1,0:T(8,128)(2,1)}) %all-gather.21.cloned.1.call-update) | async-done | bytes 2097168 | tf_op jit(solution)/shard_map/all_gather | solution.py:53
  188.3 30.0 %all-gather.19.cloned.1.call-done = bf16[512,1024]{1,0:T(8,128)(2,1)} async-done(((bf16[128,1024]{1,0:T(8,128)(2,1)}), bf16[512,1024]{1,0:T(8,128)(2,1)}) %all-gather.19.cloned.1.call-update) | async-done | bytes 1048592 | tf_op jit(solution)/shard_map/all_gather | solution.py:206
  222.8 25.0 %all-gather.25.cloned.1.call-done = bf16[512,1024]{1,0:T(8,128)(2,1)} async-done(((bf16[128,1024]{1,0:T(8,128)(2,1)}), bf16[512,1024]{1,0:T(8,128)(2,1)}) %all-gather.25.cloned.1.call-update) | async-done | bytes 1048592 | tf_op jit(solution)/shard_map/all_gather | solution.py:258
  247.9 29.8 %all-gather.23.cloned.1.call-done = bf16[1024,1024]{1,0:T(8,128)(2,1)} async-done(((bf16[1024,128]{1,0:T(8,128)(2,1)}), bf16[1024,1024]{1,0:T(8,128)(2,1)}) %all-gather.23.cloned.1.call-update) | async-done | bytes 2097168 | tf_op jit(solution)/shard_map/all_gather | solution.py:55
  302.8 27.7 %reduce-scatter.40.cloned.1.call-done = f32[128,1024]{1,0:T(8,128)} async-done(((f32[512,1024]{1,0:T(8,128)}), f32[128,1024]{1,0:T(8,128)}) %reduce-scatter.40.cloned.1.call-update) | async-done | bytes 524304 | tf_op jit(solution)/shard_map/reduce_scatter | solution.py:267
  331.9 44.2 %reduce-scatter.38.cloned.1.call-done = f32[128,1024]{1,0:T(8,128)} async-done(((f32[512,1024]{1,0:T(8,128)}), f32[128,1024]{1,0:T(8,128)}) %reduce-scatter.38.cloned.1.call-update) | async-done | bytes 524304 | tf_op jit(solution)/shard_map/reduce_scatter | solution.py:211
  379.1 27.4 %all-gather.27.cloned.1.call-done = bf16[512,1024]{1,0:T(8,128)(2,1)} async-done(((bf16[128,1024]{1,0:T(8,128)(2,1)}), bf16[512,1024]{1,0:T(8,128)(2,1)}) %all-gather.27.cloned.1.call-update) | async-done | bytes 1048592 | tf_op jit(solution)/shard_map/all_gather | solution.py:279
  423.1 40.0 %reduce-scatter.42.cloned.1.call-done = f32[128,1024]{1,0:T(8,128)} async-done(((f32[512,1024]{1,0:T(8,128)}), f32[128,1024]{1,0:T(8,128)}) %reduce-scatter.42.cloned.1.call-update) | async-done | bytes 524304 | tf_op jit(solution)/shard_map/reduce_scatter | solution.py:316
  468.1 17.1 %all-reduce.14 = (f32[4,256]{1,0:T(4,128)S(1)}, f32[4,256]{1,0:T(4,128)S(1)}, f32[4,256]{1,0:T(4,128)S(1)}, f32[4,256]{1,0:T(4,128)S(1)}, f32[4,256]{1,0:T(4,128)S(1)}, /*index=5*/f32[4,256]{1,0:T(4,128)S(1)}) all-reduce(f32[4,256]{1,0:T(4,128)S(1)} %reshape.272, ...), channel_id=6, replica_groups=mesh['fsdp'=8,'shard'=4] {'shard'}, use_global_device_ids=true, to_apply=%region_16.17.clone | all-reduce | flops 6144 | bytes 49152
  511.4 24.8 %reduce-scatter.58.cloned.1.call-done = f32[32,1]{1,0:T(8,128)} async-done(((f32[256,1]{1,0:T(8,128)}), f32[32,1]{1,0:T(8,128)}) %reduce-scatter.58.cloned.1.call-update) | async-done | bytes 144
  537.5 35.0 %reduce-scatter.56.cloned.1.call-done = f32[32,1]{1,0:T(8,128)} async-done(((f32[256,1]{1,0:T(8,128)}), f32[32,1]{1,0:T(8,128)}) %reduce-scatter.56.cloned.1.call-update) | async-done | bytes 144
  573.8 35.2 %reduce-scatter.64.cloned.1.call-done = f32[32,1]{1,0:T(8,128)} async-done(((f32[256,1]{1,0:T(8,128)}), f32[32,1]{1,0:T(8,128)}) %reduce-scatter.64.cloned.1.call-update) | async-done | bytes 144
  610.3 35.0 %reduce-scatter.68.cloned.1.call-done = f32[32,1]{1,0:T(8,128)} async-done(((f32[256,1]{1,0:T(8,128)}), f32[32,1]{1,0:T(8,128)}) %reduce-scatter.68.cloned.1.call-update) | async-done | bytes 144
  646.6 35.2 %reduce-scatter.60.cloned.1.call-done = f32[32,1]{1,0:T(8,128)} async-done(((f32[256,1]{1,0:T(8,128)}), f32[32,1]{1,0:T(8,128)}) %reduce-scatter.60.cloned.1.call-update) | async-done | bytes 144
  683.1 35.0 %reduce-scatter.62.cloned.1.call-done = f32[32,1]{1,0:T(8,128)} async-done(((f32[256,1]{1,0:T(8,128)}), f32[32,1]{1,0:T(8,128)}) %reduce-scatter.62.cloned.1.call-update) | async-done | bytes 144
  719.4 35.3 %reduce-scatter.52.cloned.1.call-done = f32[32,1]{1,0:T(8,128)} async-done(((f32[256,1]{1,0:T(8,128)}), f32[32,1]{1,0:T(8,128)}) %reduce-scatter.52.cloned.1.call-update) | async-done | bytes 144
  756.0 35.0 %reduce-scatter.54.cloned.1.call-done = f32[32,1]{1,0:T(8,128)} async-done(((f32[256,1]{1,0:T(8,128)}), f32[32,1]{1,0:T(8,128)}) %reduce-scatter.54.cloned.1.call-update) | async-done | bytes 144
  792.3 54.4 %reduce-scatter.48.cloned.1.call-done = f32[128,1024]{1,0:T(8,128)} async-done(((f32[1024,1024]{1,0:T(8,128)}), f32[128,1024]{1,0:T(8,128)}) %reduce-scatter.48.cloned.1.call-update) | async-done | bytes 524304 | tf_op jit(solution)/shard_map/reduce_scatter | solution.py:145
  846.6 55.3 %reduce-scatter.50.cloned.1.call-done = f32[1024,128]{1,0:T(8,128)} async-done(((f32[1024,1024]{1,0:T(8,128)}), f32[1024,128]{1,0:T(8,128)}) %reduce-scatter.50.cloned.1.call-update) | async-done | bytes 524304 | tf_op jit(solution)/shard_map/reduce_scatter | solution.py:147
  901.9 40.2 %reduce-scatter.46.cloned.1.call-done = f32[256,128]{1,0:T(8,128)} async-done(((f32[256,1024]{1,0:T(8,128)}), f32[256,128]{1,0:T(8,128)}) %reduce-scatter.46.cloned.1.call-update) | async-done | bytes 131088 | tf_op jit(solution)/shard_map/reduce_scatter | solution.py:141
  942.1 50.5 %reduce-scatter.44.cloned.1.call-done = f32[128,3,256]{2,0,1:T(8,128)} async-done(((f32[1024,3,256]{2,0,1:T(8,128)}), f32[128,3,256]{2,0,1:T(8,128)}) %reduce-scatter.44.cloned.1.call-update) | async-done | bytes 393232 | tf_op jit(solution)/shard_map/reduce_scatter | solution.py:138
  (219 shorter events, 198.3 us)
Async XLA Ops:
  7.2 72.7 %all-gather.15.cloned.1.call-start = ((), (), s32[]{:S(2)}) async-start(), calls=%async_computation.17 | async-start | bytes 1310720 | tf_op jit(solution)/shard_map/all_gather | solution.py:177
  54.0 53.7 %all-gather.17.cloned.1.call-start = ((), (), s32[]{:S(2)}) async-start(), calls=%async_computation.18 | async-start | bytes 1769472 | tf_op jit(solution)/shard_map/all_gather | solution.py:46
  55.8 103.4 %reduce-scatter.36.cloned.1.call-start = ((), (), s32[]{:S(2)}) async-start(), calls=%async_computation.19 | async-start | bytes 2621440 | tf_op jit(solution)/shard_map/reduce_scatter | solution.py:197
  115.0 73.3 %all-gather.21.cloned.1.call-start = ((), (), s32[]{:S(2)}) async-start(), calls=%async_computation.21 | async-start | bytes 2359296 | tf_op jit(solution)/shard_map/all_gather | solution.py:53
  115.6 102.7 %all-gather.19.cloned.1.call-start = ((), (), s32[]{:S(2)}) async-start(), calls=%async_computation.20 | async-start | bytes 1310720 | tf_op jit(solution)/shard_map/all_gather | solution.py:206
  161.5 86.4 %all-gather.25.cloned.1.call-start = ((), (), s32[]{:S(2)}) async-start(), calls=%async_computation.24 | async-start | bytes 1310720 | tf_op jit(solution)/shard_map/all_gather | solution.py:258
  163.1 114.6 %all-gather.23.cloned.1.call-start = ((), (), s32[]{:S(2)}) async-start(), calls=%async_computation.22 | async-start | bytes 2359296 | tf_op jit(solution)/shard_map/all_gather | solution.py:55
  163.8 166.7 %reduce-scatter.40.cloned.1.call-start = ((), (), s32[]{:S(2)}) async-start(), calls=%async_computation.25 | async-start | bytes 2621440 | tf_op jit(solution)/shard_map/reduce_scatter | solution.py:267
  286.5 89.6 %reduce-scatter.38.cloned.1.call-start = ((), (), s32[]{:S(2)}) async-start(), calls=%async_computation.23 | async-start | bytes 2621440 | tf_op jit(solution)/shard_map/reduce_scatter | solution.py:211
  291.6 114.9 %all-gather.27.cloned.1.call-start = ((), (), s32[]{:S(2)}) async-start(), calls=%async_computation.26 | async-start | bytes 1310720 | tf_op jit(solution)/shard_map/all_gather | solution.py:279
  379.1 84.0 %reduce-scatter.42.cloned.1.call-start = ((), (), s32[]{:S(2)}) async-start(), calls=%async_computation.27 | async-start | bytes 2621440 | tf_op jit(solution)/shard_map/reduce_scatter | solution.py:316
  419.6 90.4 %reduce-scatter.66.cloned.1.call-start = ((), (), s32[]{:S(2)}) async-start(), calls=%async_computation.39 | async-start | bytes 589824
  420.7 115.5 %reduce-scatter.58.cloned.1.call-start = ((), (), s32[]{:S(2)}) async-start(), calls=%async_computation.35 | async-start | bytes 147456
  421.6 150.9 %reduce-scatter.56.cloned.1.call-start = ((), (), s32[]{:S(2)}) async-start(), calls=%async_computation.34 | async-start | bytes 147456
  423.1 186.0 %reduce-scatter.64.cloned.1.call-start = ((), (), s32[]{:S(2)}) async-start(), calls=%async_computation.38 | async-start | bytes 147456
  486.7 158.6 %reduce-scatter.68.cloned.1.call-start = ((), (), s32[]{:S(2)}) async-start(), calls=%async_computation.40 | async-start | bytes 147456
  487.5 194.2 %reduce-scatter.60.cloned.1.call-start = ((), (), s32[]{:S(2)}) async-start(), calls=%async_computation.36 | async-start | bytes 147456
  489.1 229.0 %reduce-scatter.62.cloned.1.call-start = ((), (), s32[]{:S(2)}) async-start(), calls=%async_computation.37 | async-start | bytes 147456
  489.9 264.8 %reduce-scatter.52.cloned.1.call-start = ((), (), s32[]{:S(2)}) async-start(), calls=%async_computation.32 | async-start | bytes 147456
  491.5 299.5 %reduce-scatter.54.cloned.1.call-start = ((), (), s32[]{:S(2)}) async-start(), calls=%async_computation.33 | async-start | bytes 147456
  492.3 354.3 %reduce-scatter.48.cloned.1.call-start = ((), (), s32[]{:S(2)}) async-start(), calls=%async_computation.30 | async-start | bytes 4718592 | tf_op jit(solution)/shard_map/reduce_scatter | solution.py:145
  496.9 405.0 %reduce-scatter.50.cloned.1.call-start = ((), (), s32[]{:S(2)}) async-start(), calls=%async_computation.31 | async-start | bytes 4718592 | tf_op jit(solution)/shard_map/reduce_scatter | solution.py:147
  502.4 439.7 %reduce-scatter.46.cloned.1.call-start = ((), (), s32[]{:S(2)}) async-start(), calls=%async_computation.29 | async-start | bytes 1179648 | tf_op jit(solution)/shard_map/reduce_scatter | solution.py:141
  505.0 487.6 %reduce-scatter.44.cloned.1.call-start = ((), (), s32[]{:S(2)}) async-start(), calls=%async_computation.28 | async-start | bytes 3538944 | tf_op jit(solution)/shard_map/reduce_scatter | solution.py:138
  (19 other events, 296.0 us)
Sparse Core Ops, SparseCore 0:
  54.1 25.7 all-gather.14
  82.3 25.3 all-gather.16
  115.1 44.0 reduce-scatter.35
  161.1 27.1 all-gather.20
  190.4 27.9 all-gather.18
  220.4 27.4 all-gather.24
  249.9 27.6 all-gather.22
  286.6 43.9 reduce-scatter.39
  332.8 43.1 reduce-scatter.37
  379.2 27.2 all-gather.26
  419.7 43.3 reduce-scatter.41
  466.0 33.4 reduce-scatter.65
  502.8 33.3 reduce-scatter.57
  539.1 33.3 reduce-scatter.55
  575.6 33.3 reduce-scatter.63
  611.9 33.3 reduce-scatter.67
  648.4 33.3 reduce-scatter.59
  684.6 33.3 reduce-scatter.61
  721.3 33.3 reduce-scatter.51
  757.6 33.3 reduce-scatter.53
  795.3 51.3 reduce-scatter.47
  850.6 51.2 reduce-scatter.49
  906.0 36.0 reduce-scatter.45
  946.3 46.2 reduce-scatter.43
where the time goes:
time: 1000 us; the launch traced here: 999 us
  waiting for transfers between devices  759 us (76%)
  blocking collectives  119 us (12%)
  matrix products  45.5 us (5%)
  local copies, waits for them, and re-layouts  41.7 us (4%)
  other arithmetic  16.8 us (2%)
  between operations  16.2 us (2%)
    unnamed x33, waiting for transfers between devices  272 us
    reduce_scatter x1, waiting for transfers between devices, spread(): lax.psum_scatter(pieces[11], 'fsdp', scatter_dimension=1, tiled=True)  55.3 us
    reduce_scatter x1, waiting for transfers between devices, spread(): lax.psum_scatter(pieces[9], 'fsdp', scatter_dimension=0, tiled=True)  54.4 us
    reduce_scatter x1, waiting for transfers between devices, spread(): lax.psum_scatter(pieces[2], 'fsdp', scatter_dimension=0, tiled=True)  50.5 us
    reduce_scatter x1, waiting for transfers between devices, forward_pass(): lax.psum_scatter(jnp.dot(act_up, w_down, preferred_element_type=jnp.float...  44.2 us
    reduce_scatter x1, waiting for transfers between devices, spread(): lax.psum_scatter(pieces[5], 'fsdp', scatter_dimension=1, tiled=True)  40.2 us
    reduce_scatter x1, waiting for transfers between devices, backward_pass(): lax.psum_scatter(jnp.dot(grad_qkv_low, qkv_matrix.T, preferred_element_ty...  40 us
    unnamed x85, local copies, waits for them, and re-layouts  34.7 us
  transfers between devices with their start and end apart: 24, of which 23 were waited for; matrix products, arithmetic and copies ran while one was open for 6% of the time, Pallas kernels for 0%

commit v1 on v0

v1 whole, which is shorter than its diff:
```python
import jax
import jax.numpy as jnp
from jax import lax
from jax.sharding import PartitionSpec as P

HEAD_DIM = 64


NORM_EPS = 1e-05
NEG_FILL = -1e30


def gelu_tanh(values):
    return jax.nn.gelu(values, approximate=True)


def split_heads(qkv_full, quarter, slot_count):
    row_count = qkv_full.shape[0]
    grid = (row_count // slot_count, slot_count, quarter // HEAD_DIM, HEAD_DIM)
    query_part = qkv_full[:, :quarter].reshape(grid)
    key_part = qkv_full[:, quarter : 2 * quarter].reshape(grid)
    value_part = qkv_full[:, 2 * quarter :].reshape(grid)
    return (query_part, key_part, value_part)


def score_blocks(query_part, key_part, starts_grid):
    scores = jnp.einsum("bqhd,bkhd->bhqk", query_part, key_part, preferred_element_type=jnp.float32)
    scores = scores * HEAD_DIM ** (-0.5)
    positions = jnp.arange(scores.shape[2], dtype=jnp.int32)
    visible = (positions[None, None, :] >= starts_grid[:, :, None]) & (
        positions[None, None, :] <= positions[None, :, None]
    )
    return jnp.where(visible[:, None], scores, NEG_FILL)


def core(array):
    count = lax.axis_size("fsdp")
    return lax.ppermute(array, "fsdp", [(index, index ^ 1) for index in range(count)])


def pair(array):
    count = lax.axis_size("shard")
    return lax.ppermute(array, "shard", [(index, index ^ 1) for index in range(count)])


def far(array):
    count = lax.axis_size("shard")
    return lax.ppermute(array, "shard", [(index, index ^ 2) for index in range(count)])


def plane_groups():
    count = lax.axis_size("fsdp")
    return [[2 * step + bit for step in range(count // 2)] for bit in range(2)]


def gather_blocks(array):
    across = pair(array)
    return jnp.concatenate([array, core(array), across, core(across)], axis=0)


def return_blocks(partial):
    count = partial.shape[0] // 4
    sent = jnp.concatenate([partial[count : 2 * count], partial[3 * count :]]).astype(jnp.bfloat16)
    received = core(sent).astype(jnp.float32)
    across = (partial[2 * count : 3 * count] + received[count:]).astype(jnp.bfloat16)
    return (partial[:count] + received[:count]) + pair(across).astype(jnp.float32)


def by_bit(bit, mine, other, axis):
    return jnp.where(
        bit == 0,
        jnp.concatenate([mine, other], axis=axis),
        jnp.concatenate([other, mine], axis=axis),
    )


def to_rows(piece, bit):
    mine = lax.dynamic_index_in_dim(piece, bit, axis=1, keepdims=False)
    other = core(lax.dynamic_index_in_dim(piece, 1 - bit, axis=1, keepdims=False))
    return by_bit(bit, mine, other, 0)


def from_rows(rows, bit):
    split = rows.reshape(2, rows.shape[0] // 2, rows.shape[1])
    mine = lax.dynamic_index_in_dim(split, bit, axis=0, keepdims=False)
    other = core(lax.dynamic_index_in_dim(split, 1 - bit, axis=0, keepdims=False))
    return by_bit(bit, mine[:, None], other[:, None], 1)


def widen(rows, lengths):
    other = far(rows)
    parts = []
    at = 0
    for length in lengths:
        parts += [rows[:, at : at + length], other[:, at : at + length]]
        at += length
    return jnp.concatenate(parts, axis=1)


def narrow(rows, lengths):
    own, other = [], []
    at = 0
    for length in lengths:
        own.append(rows[:, at : at + length])
        other.append(rows[:, at + length : at + 2 * length])
        at += 2 * length
    received = far(jnp.concatenate(other, axis=1))
    total = jnp.concatenate(own, axis=1).astype(jnp.float32) + received.astype(jnp.float32)
    return total.astype(jnp.bfloat16)


def gather_plane(rows):
    return lax.all_gather(rows, "fsdp", axis=0, axis_index_groups=plane_groups(), tiled=True)


def reduce_plane(whole):
    return lax.psum_scatter(
        whole, "fsdp", scatter_dimension=0, axis_index_groups=plane_groups(), tiled=True
    )


def gather_vectors(vectors, starts):
    fsdp_count = lax.axis_size("fsdp")
    shard_count = lax.axis_size("shard")
    packed = jnp.concatenate([v.reshape(-1) for v in vectors] + [starts.astype(jnp.bfloat16)])
    spread_out = jnp.broadcast_to(packed, (fsdp_count * shard_count, packed.shape[0]))
    every = lax.all_to_all(spread_out, ("fsdp", "shard"), 0, 0, tiled=True)
    every = every.reshape(fsdp_count, shard_count, -1)
    full = []
    at = 0
    for v in vectors:
        piece = every[:, :, at : at + v.size]
        full.append(jnp.transpose(piece, (1, 0, 2)).reshape(shard_count, -1).astype(jnp.float32))
        at += v.size
    fsdp, shard = lax.axis_index("fsdp"), lax.axis_index("shard")
    rows = [
        lax.dynamic_slice(every, (fsdp ^ f, shard ^ s, at), (1, 1, starts.shape[0]))[0]
        for s in range(2)
        for f in range(2)
    ]
    return full, jnp.concatenate(rows, axis=0).astype(jnp.int32)


def own_part(vector, bits):
    high, low, bit = bits
    split = vector.reshape(2, 2, 2, -1)
    split = lax.dynamic_index_in_dim(split, low, axis=1, keepdims=False)
    split = lax.dynamic_index_in_dim(split, bit, axis=1, keepdims=False)
    return by_bit(high, split[0], split[1], 0)


def whole_part(part, bits):
    high, low, bit = bits
    split = part.reshape(2, 1, 1, -1)
    split = jnp.where(high == 0, split, split[::-1])
    place = jnp.arange(2)
    mask = (place[:, None] == low) & (place[None, :] == bit)
    return jnp.where(mask[None, :, :, None], split, 0.0).reshape(-1)


def reduce_vectors(wholes):
    fsdp_count = lax.axis_size("fsdp")
    shard_count = lax.axis_size("shard")
    parts = [w.reshape(shard_count, fsdp_count, -1) for w in wholes]
    packed = jnp.transpose(jnp.concatenate(parts, axis=2), (1, 0, 2))
    packed = packed.reshape(fsdp_count * shard_count, -1)
    received = lax.all_to_all(packed, ("fsdp", "shard"), 0, 0, tiled=True)
    total = jnp.sum(received, axis=0)
    out = []
    at = 0
    for p in parts:
        out.append(total[at : at + p.shape[2]].reshape(1, -1))
        at += p.shape[2]
    return out


def norm_parts(inputs):
    center = inputs - jnp.mean(inputs, axis=-1, keepdims=True)
    variance = jnp.mean(center * center, axis=-1, keepdims=True)
    scale = lax.rsqrt(variance + NORM_EPS)
    return center * scale, scale


def norm_back(unit, scale, gain, grad):
    grad_unit = grad * gain
    mean_grad = jnp.mean(grad_unit, axis=-1, keepdims=True)
    mean_dot = jnp.mean(grad_unit * unit, axis=-1, keepdims=True)
    return (
        scale * (grad_unit - mean_grad - unit * mean_dot),
        jnp.sum(grad * unit, axis=0),
        jnp.sum(grad, axis=0),
    )


def dot(left, right, left_dim, right_dim):
    return lax.dot_general(
        left, right, (((left_dim,), (right_dim,)), ((), ())), preferred_element_type=jnp.float32
    )


def on_device(
    tokens,
    cotangent,
    starts,
    counts,
    attn_gain,
    attn_shift,
    w_qkv,
    query_bias,
    value_bias,
    w_proj,
    proj_bias,
    mlp_gain,
    mlp_shift,
    w_up,
    up_bias,
    w_down,
    down_bias,
):
    bf16, f32 = jnp.bfloat16, jnp.float32
    slot_count, width = tokens.shape
    shard = lax.axis_index("shard")
    bits = (shard // 2, shard % 2, lax.axis_index("fsdp") % 2)
    bit = bits[2]
    rows = w_qkv.shape[0]
    quarter = w_qkv.shape[2]
    half = quarter // 2
    up_half = w_up.shape[1] // 2

    attn_piece = jnp.concatenate(
        [
            jnp.transpose(w_qkv.reshape(rows, 3, 2, half), (0, 2, 1, 3)).reshape(rows, 2, 3 * half),
            w_proj.T.reshape(rows, 2, half),
        ],
        axis=2,
    )
    attn_rows = widen(to_rows(attn_piece, bit), (half,) * 4)
    attn_full = gather_plane(attn_rows)
    w_qkv_full, w_proj_full = attn_full[:, : 3 * quarter], attn_full[:, 3 * quarter :]
    vectors, starts_grid = gather_vectors(
        (
            attn_gain,
            attn_shift,
            proj_bias,
            mlp_gain,
            mlp_shift,
            down_bias,
            query_bias,
            value_bias,
            up_bias,
        ),
        starts,
    )
    a_gain, a_shift, p_bias, m_gain, m_shift, d_bias = [v.reshape(-1) for v in vectors[:6]]
    q_bias, v_bias, u_bias = [own_part(v, bits) for v in vectors[6:]]
    mlp_piece = jnp.concatenate(
        [w_up.reshape(rows, 2, up_half), w_down.T.reshape(rows, 2, up_half)], axis=2
    )
    mlp_rows = widen(to_rows(mlp_piece, bit), (up_half,) * 2)
    w_up_full = gather_plane(mlp_rows[:, : 2 * up_half])
    w_down_full = gather_plane(mlp_rows[:, 2 * up_half :])

    live = (jnp.arange(slot_count, dtype=jnp.int32) < counts[0]).astype(f32)[:, None]
    grad_out = cotangent.astype(f32) * live
    tokens_wide = tokens.astype(f32)
    attn_unit, attn_scale = norm_parts(tokens_wide)
    act_rows = gather_blocks((attn_unit * a_gain + a_shift).astype(bf16))
    grad_low_rows = gather_blocks(grad_out.astype(bf16))
    row_count = act_rows.shape[0]
    qkv_bias = jnp.concatenate([q_bias, jnp.zeros_like(q_bias), v_bias])
    qkv_full = (dot(act_rows, w_qkv_full, 1, 0) + qkv_bias).astype(bf16)
    query_part, key_part, value_part = split_heads(qkv_full, quarter, slot_count)
    scores = score_blocks(query_part, key_part, starts_grid)
    row_max = jnp.max(scores, axis=-1, keepdims=True)
    log_total = row_max + jnp.log(jnp.sum(jnp.exp(scores - row_max), axis=-1, keepdims=True))
    probs = jnp.exp(scores - log_total)
    probs_low = probs.astype(bf16)
    mixed = jnp.einsum("bhqk,bkhd->bqhd", probs_low, value_part, preferred_element_type=f32)
    mixed = mixed.reshape(row_count, quarter).astype(bf16)
    attn_term = return_blocks(dot(mixed, w_proj_full, 1, 1))
    hidden_one = tokens_wide + attn_term + p_bias
    mlp_unit, mlp_scale = norm_parts(hidden_one)
    mlp_inputs = gather_blocks((mlp_unit * m_gain + m_shift).astype(bf16))
    pre_act = dot(mlp_inputs, w_up_full, 1, 0) + u_bias
    act_up, gelu_back = jax.vjp(gelu_tanh, pre_act)
    act_up = act_up.astype(bf16)
    grad_act = dot(grad_low_rows, w_down_full, 1, 0)
    (grad_pre,) = gelu_back(grad_act)
    grad_pre_low = grad_pre.astype(bf16)
    grad_normed = return_blocks(dot(grad_pre_low, w_up_full, 1, 1))
    g_down = dot(grad_low_rows, act_up, 0, 0).astype(bf16)
    g_up = dot(mlp_inputs, grad_pre_low, 0, 0).astype(bf16)
    g_up_bias = jnp.sum(grad_pre, axis=0)
    g_down_bias = jnp.sum(grad_out, axis=0)
    grad_hidden_part, g_mlp_gain, g_mlp_shift = norm_back(
        mlp_unit, mlp_scale, m_gain, grad_normed
    )
    grad_hidden = grad_out + grad_hidden_part
    grad_hidden, g_down, g_up = lax.optimization_barrier((grad_hidden, g_down, g_up))
    g_down = reduce_plane(g_down)
    g_up = reduce_plane(g_up)
    hidden_rows = gather_blocks(grad_hidden.astype(bf16))
    mlp_term = return_blocks(dot(act_up, w_down_full, 1, 1))
    block_out = (hidden_one + mlp_term + d_bias) * live
    g_proj_bias = jnp.sum(grad_hidden, axis=0)
    g_proj = dot(hidden_rows, mixed, 0, 0).astype(bf16)
    grad_mixed = dot(hidden_rows, w_proj_full, 1, 0).astype(bf16)
    grad_mixed = grad_mixed.reshape(
        row_count // slot_count, slot_count, quarter // HEAD_DIM, HEAD_DIM
    )
    grad_probs = jnp.einsum("bqhd,bkhd->bhqk", grad_mixed, value_part, preferred_element_type=f32)
    grad_value = jnp.einsum("bhqk,bqhd->bkhd", probs_low, grad_mixed, preferred_element_type=f32)
    row_dot = jnp.sum(probs * grad_probs, axis=-1, keepdims=True)
    grad_scores = (probs * (grad_probs - row_dot) * HEAD_DIM ** (-0.5)).astype(bf16)
    grad_query = jnp.einsum("bhqk,bkhd->bqhd", grad_scores, key_part, preferred_element_type=f32)
    grad_key = jnp.einsum("bhqk,bqhd->bkhd", grad_scores, query_part, preferred_element_type=f32)
    grad_query = grad_query.reshape(row_count, quarter)
    grad_key = grad_key.reshape(row_count, quarter)
    grad_value = grad_value.reshape(row_count, quarter)
    g_query_bias = jnp.sum(grad_query, axis=0)
    g_value_bias = jnp.sum(grad_value, axis=0)
    grad_qkv_low = jnp.concatenate([grad_query, grad_key, grad_value], axis=1).astype(bf16)
    g_qkv = dot(act_rows, grad_qkv_low, 0, 0).astype(bf16)
    g_attn = reduce_plane(jnp.concatenate([g_qkv, g_proj], axis=1))
    grad_normed_attn = return_blocks(dot(grad_qkv_low, w_qkv_full, 1, 1))
    grad_in_part, g_attn_gain, g_attn_shift = norm_back(
        attn_unit, attn_scale, a_gain, grad_normed_attn
    )
    grad_in = grad_hidden + grad_in_part
    small = reduce_vectors(
        (
            g_attn_gain,
            g_attn_shift,
            g_proj_bias,
            g_mlp_gain,
            g_mlp_shift,
            g_down_bias,
            whole_part(g_query_bias, bits),
            whole_part(g_value_bias, bits),
            whole_part(g_up_bias, bits),
        )
    )
    g_mlp = narrow(jnp.concatenate([g_up, g_down], axis=1), (up_half,) * 2)
    g_mlp = from_rows(g_mlp, bit).astype(f32)
    g_attn = from_rows(narrow(g_attn, (half,) * 4), bit).astype(f32)
    g_qkv = jnp.transpose(g_attn[:, :, : 3 * half].reshape(rows, 2, 3, half), (0, 2, 1, 3))
    return (
        block_out.astype(bf16),
        grad_in,
        small[0],
        small[1],
        g_qkv.reshape(w_qkv.shape),
        small[6],
        small[7],
        g_attn[:, :, 3 * half :].reshape(rows, quarter).T,
        small[2],
        small[3],
        small[4],
        g_mlp[:, :, :up_half].reshape(w_up.shape),
        small[8],
        g_mlp[:, :, up_half:].reshape(rows, 2 * up_half).T,
        small[5],
    )


def solution(mesh):
    in_specs = (
        P(("fsdp", "shard"), None),
        P(("fsdp", "shard"), None),
        P(("fsdp", "shard")),
        P(("fsdp", "shard")),
        P("shard", "fsdp"),
        P("shard", "fsdp"),
        P("fsdp", None, "shard"),
        P("shard", "fsdp"),
        P("shard", "fsdp"),
        P("shard", "fsdp"),
        P("shard", "fsdp"),
        P("shard", "fsdp"),
        P("shard", "fsdp"),
        P("fsdp", "shard"),
        P("shard", "fsdp"),
        P("shard", "fsdp"),
        P("shard", "fsdp"),
    )
    out_specs = (
        P(("fsdp", "shard"), None),
        P(("fsdp", "shard"), None),
        P("shard", "fsdp"),
        P("shard", "fsdp"),
        P("fsdp", None, "shard"),
        P("shard", "fsdp"),
        P("shard", "fsdp"),
        P("shard", "fsdp"),
        P("shard", "fsdp"),
        P("shard", "fsdp"),
        P("shard", "fsdp"),
        P("fsdp", "shard"),
        P("shard", "fsdp"),
        P("shard", "fsdp"),
        P("shard", "fsdp"),
    )
    return jax.shard_map(
        on_device, mesh=mesh, in_specs=in_specs, out_specs=out_specs, check_vma=False
    )
```

time: 1000 us -> 318 us (0.32)
  waiting for transfers between devices: 759 us -> 175 us
  blocking collectives: 119 us -> 11.6 us
  starting transfers between devices: 0.99 us -> 25.1 us
  local copies, waits for them, and re-layouts: 41.7 us -> 22.2 us
  other arithmetic: 16.8 us -> 28.1 us
    reduce_scatter x8 -> x3, waiting for transfers between devices: 327 us -> 51 us  [reduce_plane(): lax.psum_scatter(whole, 'fsdp', scatter_dimension=0, axis_index_groups=pl...]
    unnamed x33 -> x6, waiting for transfers between devices: 272 us -> 0.62 us
    all_gather x7 -> x3, waiting for transfers between devices: 161 us -> 25.3 us  [gather_plane(): lax.all_gather(rows, 'fsdp', axis=0, axis_index_groups=plane_groups(), ti...]
    ppermute x0 -> x28, waiting for transfers between devices: none -> 91.5 us  [the longest x4 47.4 us: far(): lax.ppermute(array, 'shard', [(index, index ^ 2) for index in range(count)])]
    all_gather x9 -> x0, blocking collectives: 86.5 us -> none  [the longest x1 11.2 us: collect(): lax.all_gather(over[0], 'shard', axis=0, tiled=True)]
    unnamed x2 -> x0, blocking collectives: 32.2 us -> none
    unnamed x85 -> x120, local copies, waits for them, and re-layouts: 34.7 us -> 8.09 us
    ppermute x0 -> x28, starting transfers between devices: none -> 18.7 us  [the longest x4 9.52 us: far(): lax.ppermute(array, 'shard', [(index, index ^ 2) for index in range(count)])]
  transfers between devices with their start and end apart: 24 -> 35, of which waited for: 23 -> 19; matrix products, arithmetic and copies ran while one was open for 6% -> 23% of each run, Pallas kernels for 0% -> 0%
where the time goes in v1:
time: 318 us; the launch traced here: 317 us
  waiting for transfers between devices  175 us (55%)
  matrix products  39.2 us (12%)
  other arithmetic  28.1 us (9%)
  starting transfers between devices  25.1 us (8%)
  local copies, waits for them, and re-layouts  22.2 us (7%)
  between operations  16.3 us (5%)
  blocking collectives  11.6 us (4%)
    reduce_scatter x3, waiting for transfers between devices, reduce_plane(): lax.psum_scatter(whole, 'fsdp', scatter_dimension=0, axis_index_groups=pl...  51 us
    ppermute x4, waiting for transfers between devices, far(): lax.ppermute(array, 'shard', [(index, index ^ 2) for index in range(count)])  47.4 us
    ppermute x8, waiting for transfers between devices, pair(): lax.ppermute(array, 'shard', [(index, index ^ 1) for index in range(count)])  38.1 us
    dot_general x12, matrix products, dot(): lax.dot_general(left, right, (((left_dim,), (right_dim,)), ((), ())), pre...  32.5 us
    all_gather x3, waiting for transfers between devices, gather_plane(): lax.all_gather(rows, 'fsdp', axis=0, axis_index_groups=plane_groups(), ti...  25.3 us
    all_to_all x1, blocking collectives, reduce_vectors(): received = lax.all_to_all(packed, ('fsdp', 'shard'), 0, 0, tiled=True)  11.6 us
    ppermute x4, starting transfers between devices, far(): lax.ppermute(array, 'shard', [(index, index ^ 2) for index in range(count)])  9.52 us
    unnamed x120, local copies, waits for them, and re-layouts  8.09 us
  transfers between devices with their start and end apart: 35, of which 19 were waited for; matrix products, arithmetic and copies ran while one was open for 23% of the time, Pallas kernels for 0%

profile of v1, /device:TPU:0, one launch (start us, length us, event | category | flops | bytes accessed | tf_op | source)
XLA Modules:
  0.0 317.2 jit_solution(12860952454567908307)
XLA Ops:
  11.0 4.0 %collective-permute-start.4 = (bf16[256,512]{0,1:T(8,128)(2,1)S(1)}, bf16[256,512]{0,1:T(8,128)(2,1)S(1)}, u32[]{:S(2)}, u32[]{:S(2)}) collective-permute-start(bf16[256,512]{0,1:T(8,128)(2,1)S(1)} %maximum_select_fusion.2), channel_id=1, source_target_pairs={{0,2},{1,3},{2,0},{3,1},{4,6},{5,7},{6,4},{7,5},{8,10},{9,11},{10,... | collective-permute-start | bytes 786440 | tf_op jit(solution)/shard_map/ppermute | solution.py:48
  15.0 12.2 %collective-permute-done.4 = bf16[256,512]{0,1:T(8,128)(2,1)S(1)} collective-permute-done((bf16[256,512]{0,1:T(8,128)(2,1)S(1)}, bf16[256,512]{0,1:T(8,128)(2,1)S(1)}, u32[]{:S(2)}, u32[]{:S(2)}) %collective-permute-start.4) | collective-permute-done | bytes 262176 | tf_op jit(solution)/shard_map/ppermute | solution.py:48
  30.4 5.8 %all-to-all-start = ((bf16[32,2,256]{2,1,0:T(2,128)(2,1)}), bf16[32,2,256]{2,1,0:T(2,128)(2,1)S(1)}, u32[]{:S(2)}, u32[]{:S(2)}) async-start(bf16[32,2,256]{2,1,0:T(2,128)(2,1)} %reshape.517), calls=%async_computation | async-start | bytes 65536 | tf_op jit(solution)/shard_map/all_to_all | solution.py:127
  37.2 6.2 %all-to-all-done = bf16[32,2,256]{2,1,0:T(2,128)(2,1)S(1)} async-done(((bf16[32,2,256]{2,1,0:T(2,128)(2,1)}), bf16[32,2,256]{2,1,0:T(2,128)(2,1)S(1)}, u32[]{:S(2)}, u32[]{:S(2)}) %all-to-all-start) | async-done | bytes 32800 | tf_op jit(solution)/shard_map/all_to_all | solution.py:127
  46.6 23.3 %collective-permute-done.11 = bf16[256,1024]{0,1:T(8,128)(2,1)S(1)} collective-permute-done((bf16[256,1024]{0,1:T(8,128)(2,1)S(1)}, bf16[256,1024]{0,1:T(8,128)(2,1)S(1)}, u32[]{:S(2)}, u32[]{:S(2)}) %collective-permute-start.11) | collective-permute-done | bytes 524320 | tf_op jit(solution)/shard_map/ppermute | solution.py:48
  73.2 2.5 add_convert_fusion
  88.3 7.8 %collective-permute-done.6 = bf16[128,1024]{1,0:T(8,128)(2,1)} collective-permute-done((bf16[128,1024]{1,0:T(8,128)(2,1)}, bf16[128,1024]{1,0:T(8,128)(2,1)}, u32[]{:S(2)}, u32[]{:S(2)}) %collective-permute-start.6) | collective-permute-done | bytes 262176 | tf_op jit(solution)/shard_map/ppermute | solution.py:43
  100.7 6.5 %collective-permute-done.8 = bf16[128,1024]{1,0:T(8,128)(2,1)S(1)} collective-permute-done((bf16[128,1024]{1,0:T(8,128)(2,1)S(1)}, bf16[128,1024]{1,0:T(8,128)(2,1)S(1)}, u32[]{:S(2)}, u32[]{:S(2)}) %collective-permute-start.8) | collective-permute-done | bytes 262176 | tf_op jit(solution)/shard_map/ppermute | solution.py:43
  107.4 3.8 %collective-permute-done.15 = bf16[128,1024]{1,0:T(8,128)(2,1)} collective-permute-done((bf16[128,1024]{1,0:T(8,128)(2,1)S(1)}, bf16[128,1024]{1,0:T(8,128)(2,1)}, u32[]{:S(2)}, u32[]{:S(2)}) %collective-permute-start.15) | collective-permute-done | bytes 262176 | tf_op jit(solution)/shard_map/ppermute | solution.py:43
  111.3 4.5 %fusion.75 = f32[512,1024]{1,0:T(8,128)} fusion(bf16[1024,1024]{0,1:T(8,128)(2,1)} %all-gather.6.cloned.1.call-done, bf16[128,1024]{1,0:T(8,128)(2,1)S(1)} %collective-permute-done.9, bf16[128,1024]{1,0:T(8,128)(2,1)S(1)} %collective-permute-done.8, bf16[128,1024]{1,0:T(8,128)(2,1)S(1)} %collective-permute-done.7, bf16[128,1024]{1,0:T(8,128)(2,1)S(1)} %add_convert_fusion.3), kind=kOutput, calls=%fused_computation.141 | convolution fusion | flops 1077936128 | bytes 5242880 | tf_op jit(solution)/shard_map/dot_general | solution.py:196
  115.8 25.3 %all-gather.8.cloned.1.call-done = bf16[1024,1024]{0,1:T(8,128)(2,1)} async-done(((bf16[256,1024]{0,1:T(8,128)(2,1)}), bf16[1024,1024]{0,1:T(8,128)(2,1)}) %all-gather.8.cloned.1.call-update) | async-done | bytes 2097168 | tf_op jit(solution)/shard_map/all_gather | solution.py:113
  141.1 5.0 %fusion.128 = (f32[1024]{0:T(1024)S(1)}, bf16[512,1024]{1,0:T(8,128)(2,1)S(1)}) fusion(f32[512,1024]{1,0:T(8,128)} %fusion.75, f32[1024]{0:T(1024)S(1)} %maximum_select_fusion.4, bf16[1024,1024]{0,1:T(8,128)(2,1)} %all-gather.8.cloned.1.call-done, bf16[128,1024]{1,0:T(8,128)(2,1)S(1)} %collective-permute-done.16, ...), kind=kOutput, calls=%fused_computation.250 | convolution fusion | flops 1089469440 | bytes 6299648 | tf_op jit(solution)/shard_map/dot_general | solution.py:196
  146.2 2.7 fusion.123
  150.4 2.9 fusion.124
  154.2 3.8 %convolution_convert_fusion.1 = bf16[1024,1024]{1,0:T(8,128)(2,1)} fusion(bf16[128,1024]{1,0:T(8,128)(2,1)S(1)} %copy-done.46, bf16[128,1024]{1,0:T(8,128)(2,1)} %collective-permute-done.15, bf16[128,1024]{1,0:T(8,128)(2,1)} %collective-permute-done.14, bf16[128,1024]{1,0:T(8,128)(2,1)S(1)} %fusion.54, f32[512,1024]{1,0:T(8,128)S(1)} %copy-done.52, ...), kind=kOutput, calls=%fused_computation.12 | convolution fusion | flops 1084227584 | bytes 5246976 | tf_op jit(solution)/shard_map/dot_general | solution.py:196
  162.6 3.8 %convolution_convert_fusion = bf16[1024,1024]{1,0:T(8,128)(2,1)} fusion(bf16[512,1024]{1,0:T(8,128)(2,1)S(1)} %copy-done.51, bf16[128,1024]{1,0:T(8,128)(2,1)} %copy-done.40, bf16[128,1024]{1,0:T(8,128)(2,1)} %copy-done.38, bf16[128,1024]{1,0:T(8,128)(2,1)} %copy-done.39, bf16[128,1024]{1,0:T(8,128)(2,1)} %copy-done.20), kind=kOutput, calls=%fused_computation.11 | convolution fusion | flops 1078984704 | bytes 4194304 | tf_op jit(solution)/shard_map/dot_general | solution.py:196
  171.6 4.6 %collective-permute-done.13 = bf16[128,1024]{1,0:T(8,128)(2,1)S(1)} collective-permute-done((bf16[128,1024]{1,0:T(8,128)(2,1)S(1)}, bf16[128,1024]{1,0:T(8,128)(2,1)S(1)}, u32[]{:S(2)}, u32[]{:S(2)}) %collective-permute-start.13) | collective-permute-done | bytes 262176 | tf_op jit(solution)/shard_map/ppermute | solution.py:43
  180.1 6.6 %collective-permute-done.20 = bf16[128,1024]{1,0:T(8,128)(2,1)S(1)} collective-permute-done((bf16[128,1024]{1,0:T(8,128)(2,1)S(1)}, bf16[128,1024]{1,0:T(8,128)(2,1)S(1)}, u32[]{:S(2)}, u32[]{:S(2)}) %collective-permute-start.20) | collective-permute-done | bytes 262176 | tf_op jit(solution)/shard_map/ppermute | solution.py:43
  202.1 2.7 fusion.127
  211.5 7.0 %collective-permute-done.23 = bf16[128,1024]{1,0:T(8,128)(2,1)} collective-permute-done((bf16[128,1024]{1,0:T(8,128)(2,1)S(1)}, bf16[128,1024]{1,0:T(8,128)(2,1)}, u32[]{:S(2)}, u32[]{:S(2)}) %collective-permute-start.23) | collective-permute-done | bytes 262176 | tf_op jit(solution)/shard_map/ppermute | solution.py:43
  221.4 11.6 %all_to_all.16 = f32[32,1,384]{2,1,0:T(1,128)S(1)} all-to-all(f32[32,1,384]{2,1,0:T(1,128)S(1)} %all_to_all.13), channel_id=1, replica_groups=mesh['fsdp'=8,'shard'=4] {'fsdp','shard'}, dimensions={0} | all-to-all | bytes 98304 | tf_op jit(solution)/shard_map/all_to_all | solution.py:167
  234.8 17.1 %reduce-scatter.6.cloned.1.call-done = bf16[256,1024]{1,0:T(8,128)(2,1)} async-done(((bf16[1024,1024]{1,0:T(8,128)(2,1)}), bf16[256,1024]{1,0:T(8,128)(2,1)}) %reduce-scatter.6.cloned.1.call-update) | async-done | bytes 524304 | tf_op jit(solution)/shard_map/reduce_scatter | solution.py:117
  256.0 33.9 %reduce-scatter.4.cloned.1.call-done = bf16[256,1024]{0,1:T(8,128)(2,1)} async-done(((bf16[1024,1024]{0,1:T(8,128)(2,1)}), bf16[256,1024]{0,1:T(8,128)(2,1)}) %reduce-scatter.4.cloned.1.call-update) | async-done | bytes 524304 | tf_op jit(solution)/shard_map/reduce_scatter | solution.py:117
  293.8 11.9 %collective-permute-done.24 = bf16[256,512]{0,1:T(8,128)(2,1)S(1)} collective-permute-done((bf16[256,512]{0,1:T(8,128)(2,1)S(1)}, bf16[256,512]{0,1:T(8,128)(2,1)S(1)}, u32[]{:S(2)}, u32[]{:S(2)}) %collective-permute-start.24) | collective-permute-done | bytes 262176 | tf_op jit(solution)/shard_map/ppermute | solution.py:48
  (348 shorter events, 85.3 us)
Async XLA Ops:
  7.3 65.9 %all-gather.4.cloned.1.call-start = ((), (), s32[]{:S(2)}) async-start(), calls=%async_computation.5 | async-start | bytes 2621440 | tf_op jit(solution)/shard_map/all_gather | solution.py:113
  11.0 16.2 %collective-permute-start.4 = (bf16[256,512]{0,1:T(8,128)(2,1)S(1)}, bf16[256,512]{0,1:T(8,128)(2,1)S(1)}, u32[]{:S(2)}, u32[]{:S(2)}) collective-permute-start(bf16[256,512]{0,1:T(8,128)(2,1)S(1)} %maximum_select_fusion.2), channel_id=1, source_target_pairs={{0,2},{1,3},{2,0},{3,1},{4,6},{5,7},{6,4},{7,5},{8,10},{9,11},{10,... | collective-permute-start | bytes 786440 | tf_op jit(solution)/shard_map/ppermute | solution.py:48
  30.4 13.1 %all-to-all-start = ((bf16[32,2,256]{2,1,0:T(2,128)(2,1)}), bf16[32,2,256]{2,1,0:T(2,128)(2,1)S(1)}, u32[]{:S(2)}, u32[]{:S(2)}) async-start(bf16[32,2,256]{2,1,0:T(2,128)(2,1)} %reshape.517), calls=%async_computation | async-start | bytes 65536 | tf_op jit(solution)/shard_map/all_to_all | solution.py:127
  36.2 75.1 %all-gather.6.cloned.1.call-start = ((), (), s32[]{:S(2)}) async-start(), calls=%async_computation.6 | async-start | bytes 2621440 | tf_op jit(solution)/shard_map/all_gather | solution.py:113
  44.1 25.7 %collective-permute-start.11 = (bf16[256,1024]{0,1:T(8,128)(2,1)S(1)}, bf16[256,1024]{0,1:T(8,128)(2,1)S(1)}, u32[]{:S(2)}, u32[]{:S(2)}) collective-permute-start(bf16[256,1024]{0,1:T(8,128)(2,1)S(1)} %maximum_select_fusion), channel_id=1, source_target_pairs={{0,2},{1,3},{2,0},{3,1},{4,6},{5,7},{6,4},{7,5},{8,10},{9,11},{10,... | collective-permute-start | bytes 1572872 | tf_op jit(solution)/shard_map/ppermute | solution.py:48
  45.0 26.6 %collective-permute-start.1 = (bf16[128,1024]{1,0:T(8,128)(2,1)S(1)}, bf16[128,1024]{1,0:T(8,128)(2,1)S(1)}, u32[]{:S(2)}, u32[]{:S(2)}) collective-permute-start(bf16[128,1024]{1,0:T(8,128)(2,1)S(1)} %fusion.29), channel_id=1, source_target_pairs={{0,1},{1,0},{2,3},{3,2},{4,5},{5,4},{6,7},{7,6},{8,9},{9,8},{10,11... | collective-permute-start | bytes 786440 | tf_op jit(solution)/shard_map/ppermute | solution.py:43
  45.7 26.1 %collective-permute-start = (bf16[128,1024]{1,0:T(8,128)(2,1)S(1)}, bf16[128,1024]{1,0:T(8,128)(2,1)S(1)}, u32[]{:S(2)}, u32[]{:S(2)}) collective-permute-start(bf16[128,1024]{1,0:T(8,128)(2,1)S(1)} %fusion.29), channel_id=1, source_target_pairs={{0,4},{4,0},{8,12},{12,8},{16,20},{20,16},{24,28},{28,24},{1,5},{5... | collective-permute-start | bytes 786440 | tf_op jit(solution)/shard_map/ppermute | solution.py:38
  71.5 69.6 %all-gather.8.cloned.1.call-start = ((), (), s32[]{:S(2)}) async-start(), calls=%async_computation.7 | async-start | bytes 2621440 | tf_op jit(solution)/shard_map/all_gather | solution.py:113
  82.2 151.6 %reduce-scatter.8.cloned.1.call-start = ((), (), s32[]{:S(2)}) async-start(), calls=%async_computation.10 | async-start | bytes 2621440 | tf_op jit(solution)/shard_map/reduce_scatter | solution.py:117
  87.4 8.7 %collective-permute-start.6 = (bf16[128,1024]{1,0:T(8,128)(2,1)}, bf16[128,1024]{1,0:T(8,128)(2,1)}, u32[]{:S(2)}, u32[]{:S(2)}) collective-permute-start(bf16[128,1024]{1,0:T(8,128)(2,1)} %fusion.47), channel_id=1, source_target_pairs={{0,1},{1,0},{2,3},{3,2},{4,5},{5,4},{6,7},{7,6},{8,9},{9,8},{10,11... | collective-permute-start | bytes 786440 | tf_op jit(solution)/shard_map/ppermute | solution.py:43
  97.9 9.3 %collective-permute-start.8 = (bf16[128,1024]{1,0:T(8,128)(2,1)S(1)}, bf16[128,1024]{1,0:T(8,128)(2,1)S(1)}, u32[]{:S(2)}, u32[]{:S(2)}) collective-permute-start(bf16[128,1024]{1,0:T(8,128)(2,1)S(1)} %add_convert_fusion.3), channel_id=1, source_target_pairs={{0,1},{1,0},{2,3},{3,2},{4,5},{5,4},{6,7},{7,6},{8,9},{9,8},{10,11... | collective-permute-start | bytes 786440 | tf_op jit(solution)/shard_map/ppermute | solution.py:43
  98.4 12.8 %collective-permute-start.15 = (bf16[128,1024]{1,0:T(8,128)(2,1)S(1)}, bf16[128,1024]{1,0:T(8,128)(2,1)}, u32[]{:S(2)}, u32[]{:S(2)}) collective-permute-start(bf16[128,1024]{1,0:T(8,128)(2,1)S(1)} %fusion.54), channel_id=1, source_target_pairs={{0,1},{1,0},{2,3},{3,2},{4,5},{5,4},{6,7},{7,6},{8,9},{9,8},{10,11... | collective-permute-start | bytes 786440 | tf_op jit(solution)/shard_map/ppermute | solution.py:43
  100.2 15.6 %collective-permute-start.14 = (bf16[128,1024]{1,0:T(8,128)(2,1)S(1)}, bf16[128,1024]{1,0:T(8,128)(2,1)}, u32[]{:S(2)}, u32[]{:S(2)}) collective-permute-start(bf16[128,1024]{1,0:T(8,128)(2,1)S(1)} %fusion.54), channel_id=1, source_target_pairs={{0,4},{4,0},{8,12},{12,8},{16,20},{20,16},{24,28},{28,24},{1,5},{5... | collective-permute-start | bytes 786440 | tf_op jit(solution)/shard_map/ppermute | solution.py:38
  100.2 11.0 %collective-permute-start.7 = (bf16[128,1024]{1,0:T(8,128)(2,1)S(1)}, bf16[128,1024]{1,0:T(8,128)(2,1)S(1)}, u32[]{:S(2)}, u32[]{:S(2)}) collective-permute-start(bf16[128,1024]{1,0:T(8,128)(2,1)S(1)} %add_convert_fusion.3), channel_id=1, source_target_pairs={{0,4},{4,0},{8,12},{12,8},{16,20},{20,16},{24,28},{28,24},{1,5},{5... | collective-permute-start | bytes 786440 | tf_op jit(solution)/shard_map/ppermute | solution.py:38
  148.9 9.2 %collective-permute-start.17 = (bf16[256,1024]{1,0:T(8,128)(2,1)S(1)}, bf16[256,1024]{1,0:T(8,128)(2,1)}, u32[]{:S(2)}, u32[]{:S(2)}) collective-permute-start(bf16[256,1024]{1,0:T(8,128)(2,1)S(1)} %pad_maximum_fusion.9), channel_id=1, source_target_pairs={{0,4},{4,0},{8,12},{12,8},{16,20},{20,16},{24,28},{28,24},{1,5},{5... | collective-permute-start | bytes 1572872 | tf_op jit(solution)/shard_map/ppermute | solution.py:38
  154.2 12.3 %collective-permute-start.12 = (bf16[256,1024]{1,0:T(8,128)(2,1)}, bf16[256,1024]{1,0:T(8,128)(2,1)S(1)}, u32[]{:S(2)}, u32[]{:S(2)}) collective-permute-start(bf16[256,1024]{1,0:T(8,128)(2,1)} %pad_maximum_fusion.8), channel_id=1, source_target_pairs={{0,4},{4,0},{8,12},{12,8},{16,20},{20,16},{24,28},{28,24},{1,5},{5... | collective-permute-start | bytes 1572872 | tf_op jit(solution)/shard_map/ppermute | solution.py:38
  161.1 9.0 %collective-permute-start.18 = (bf16[128,1024]{1,0:T(8,128)(2,1)}, bf16[128,1024]{1,0:T(8,128)(2,1)}, u32[]{:S(2)}, u32[]{:S(2)}) collective-permute-start(bf16[128,1024]{1,0:T(8,128)(2,1)} %fusion.39), channel_id=1, source_target_pairs={{0,1},{1,0},{2,3},{3,2},{4,5},{5,4},{6,7},{7,6},{8,9},{9,8},{10,11... | collective-permute-start | bytes 786440 | tf_op jit(solution)/shard_map/ppermute | solution.py:43
  167.8 8.4 %collective-permute-start.13 = (bf16[128,1024]{1,0:T(8,128)(2,1)S(1)}, bf16[128,1024]{1,0:T(8,128)(2,1)S(1)}, u32[]{:S(2)}, u32[]{:S(2)}) collective-permute-start(bf16[128,1024]{1,0:T(8,128)(2,1)S(1)} %fusion.41), channel_id=1, source_target_pairs={{0,1},{1,0},{2,3},{3,2},{4,5},{5,4},{6,7},{7,6},{8,9},{9,8},{10,11... | collective-permute-start | bytes 786440 | tf_op jit(solution)/shard_map/ppermute | solution.py:43
  178.2 73.6 %reduce-scatter.6.cloned.1.call-start = ((), (), s32[]{:S(2)}) async-start(), calls=%async_computation.9 | async-start | bytes 2621440 | tf_op jit(solution)/shard_map/reduce_scatter | solution.py:117
  178.8 111.1 %reduce-scatter.4.cloned.1.call-start = ((), (), s32[]{:S(2)}) async-start(), calls=%async_computation.8 | async-start | bytes 2621440 | tf_op jit(solution)/shard_map/reduce_scatter | solution.py:117
  210.0 8.5 %collective-permute-start.23 = (bf16[128,1024]{1,0:T(8,128)(2,1)S(1)}, bf16[128,1024]{1,0:T(8,128)(2,1)}, u32[]{:S(2)}, u32[]{:S(2)}) collective-permute-start(bf16[128,1024]{1,0:T(8,128)(2,1)S(1)} %fusion.37), channel_id=1, source_target_pairs={{0,1},{1,0},{2,3},{3,2},{4,5},{5,4},{6,7},{7,6},{8,9},{9,8},{10,11... | collective-permute-start | bytes 786440 | tf_op jit(solution)/shard_map/ppermute | solution.py:43
  253.0 40.5 %collective-permute-start.26 = (bf16[256,1024]{1,0:T(8,128)(2,1)S(1)}, bf16[256,1024]{1,0:T(8,128)(2,1)S(1)}, u32[]{:S(2)}, u32[]{:S(2)}) collective-permute-start(bf16[256,1024]{1,0:T(8,128)(2,1)S(1)} %pad_maximum_fusion.11), channel_id=1, source_target_pairs={{0,2},{1,3},{2,0},{3,1},{4,6},{5,7},{6,4},{7,5},{8,10},{9,11},{10,... | collective-permute-start | bytes 1572872 | tf_op jit(solution)/shard_map/ppermute | solution.py:48
  291.0 14.6 %collective-permute-start.24 = (bf16[256,512]{0,1:T(8,128)(2,1)S(1)}, bf16[256,512]{0,1:T(8,128)(2,1)S(1)}, u32[]{:S(2)}, u32[]{:S(2)}) collective-permute-start(bf16[256,512]{0,1:T(8,128)(2,1)S(1)} %pad_maximum_fusion.12), channel_id=1, source_target_pairs={{0,2},{1,3},{2,0},{3,1},{4,6},{5,7},{6,4},{7,5},{8,10},{9,11},{10,... | collective-permute-start | bytes 786440 | tf_op jit(solution)/shard_map/ppermute | solution.py:48
  293.7 12.3 %collective-permute-start.27 = (bf16[128,1024]{1,0:T(8,128)(2,1)S(1)}, bf16[128,1024]{1,0:T(8,128)(2,1)S(1)}, u32[]{:S(2)}, u32[]{:S(2)}) collective-permute-start(bf16[128,1024]{1,0:T(8,128)(2,1)S(1)} %get-tuple-element.94), channel_id=1, source_target_pairs={{0,4},{4,0},{8,12},{12,8},{16,20},{20,16},{24,28},{28,24},{1,5},{5... | collective-permute-start | bytes 786440 | tf_op jit(solution)/shard_map/ppermute | solution.py:38
  (64 other events, 522.6 us)
Sparse Core Ops, SparseCore 0:
  28.3 36.3 all-gather.3
  71.6 31.8 all-gather.5
  105.9 35.1 all-gather.7
  178.4 34.6 reduce-scatter.7
  216.1 35.7 reduce-scatter.5
  254.7 35.1 reduce-scatter.3

commit v2 on v1

v2 whole, which is shorter than its diff:
```python
import functools

import jax
import jax.numpy as jnp
from jax import lax
from jax.experimental import pallas as pl
from jax.experimental.pallas import tpu as pltpu
from jax.sharding import PartitionSpec as P

HEAD_DIM = 64
PLANE = 4
BLOCKS = 4
NORM_EPS = 1e-05
NEG_FILL = -1e30
GELU_ROOT = 0.7978845608028654
GELU_CUBE = 0.044715
F32, BF16 = jnp.float32, jnp.bfloat16


def core(array):
    count = lax.axis_size("fsdp")
    return lax.ppermute(array, "fsdp", [(index, index ^ 1) for index in range(count)])


def pair(array):
    count = lax.axis_size("shard")
    return lax.ppermute(array, "shard", [(index, index ^ 1) for index in range(count)])


def far(array):
    count = lax.axis_size("shard")
    return lax.ppermute(array, "shard", [(index, index ^ 2) for index in range(count)])


def by_bit(bit, mine, other, axis):
    return jnp.where(
        bit == 0,
        jnp.concatenate([mine, other], axis=axis),
        jnp.concatenate([other, mine], axis=axis),
    )


def to_rows(piece, bit):
    mine = lax.dynamic_index_in_dim(piece, bit, axis=1, keepdims=False)
    other = core(lax.dynamic_index_in_dim(piece, 1 - bit, axis=1, keepdims=False))
    return by_bit(bit, mine, other, 0)


def from_rows(rows, bit):
    split = rows.reshape(2, rows.shape[0] // 2, rows.shape[1])
    mine = lax.dynamic_index_in_dim(split, bit, axis=0, keepdims=False)
    other = core(lax.dynamic_index_in_dim(split, 1 - bit, axis=0, keepdims=False))
    return by_bit(bit, mine[:, None], other[:, None], 1)


def plane_count():
    return lax.axis_size("fsdp") // 2


def plane_index():
    return lax.axis_index("fsdp") // 2


def plane(array, distance):
    count = lax.axis_size("fsdp")
    return lax.ppermute(
        array, "fsdp", [(index, index ^ (2 * distance)) for index in range(count)]
    )


def ring(array, distance):
    count = lax.axis_size("shard")
    return lax.ppermute(array, "shard", [(index, index ^ distance) for index in range(count)])


def gather_ring(array):
    others = {k: ring(array, k) for k in (3, 2, 1)}
    return [array] + [others[k] for k in range(1, BLOCKS)]


def return_ring(own, *sent):
    others = {k: ring(sent[k - 1], k) for k in (3, 2, 1)}
    return [own] + [others[k] for k in range(1, BLOCKS)]


def plane_groups():
    return [[2 * step + bit for step in range(plane_count())] for bit in range(2)]


def reorder(array):
    if plane_count() != PLANE:
        return array
    size = array.shape[-1] // PLANE
    index = plane_index()
    for step in (1, 2):
        blocks = [array[..., j * size : (j + 1) * size] for j in range(PLANE)]
        swapped = jnp.concatenate([blocks[j ^ step] for j in range(PLANE)], axis=-1)
        array = jnp.where((index & step) != 0, swapped, array)
    return array


def gather_pieces(rows):
    if plane_count() == PLANE:
        return [rows] + [plane(rows, k) for k in range(1, PLANE)]
    whole = lax.all_gather(rows, "fsdp", axis=0, axis_index_groups=plane_groups(), tiled=True)
    size = whole.shape[0] // PLANE
    return [whole[k * size : (k + 1) * size] for k in range(PLANE)]


def reduce_plane(whole):
    if plane_count() == PLANE:
        size = whole.shape[0] // PLANE
        total = whole[:size].astype(F32)
        for k in range(1, PLANE):
            total = total + plane(whole[k * size : (k + 1) * size], k).astype(F32)
        return total
    return scatter_plane(whole).astype(F32)


def scatter_plane(whole):
    return lax.psum_scatter(
        whole, "fsdp", scatter_dimension=0, axis_index_groups=plane_groups(), tiled=True
    )


def hold(*values):
    return lax.optimization_barrier(values)


def gather_blocks(array):
    across = pair(array)
    return [array, core(array), across, core(across)]


def return_blocks(own, kept, sent):
    received = core(sent)
    count = own.shape[0]
    across = (kept + received[count:].astype(F32)).astype(BF16)
    return own, received, pair(across)


def pack_rows(*refs):
    out, rows = refs[-2:]
    rows[...] = jnp.zeros(rows.shape, rows.dtype)
    for row, ref in enumerate(refs[:-2]):
        rows[row : row + 1, : ref.shape[1]] = ref[...].astype(F32)
    out[...] = jnp.broadcast_to(rows[...].astype(out.dtype)[None], out.shape)


def run(kernel, outs, *operands, scratch=(), flops=0):
    spec = pl.BlockSpec(memory_space=pltpu.VMEM)
    moved = sum(o.size * o.dtype.itemsize for o in operands)
    moved += sum(functools.reduce(lambda a, b: a * b, shape) * 4 for shape, _ in outs)
    body = kernel.func if isinstance(kernel, functools.partial) else kernel
    return pl.pallas_call(
        kernel,
        out_shape=[jax.ShapeDtypeStruct(shape, kind) for shape, kind in outs],
        in_specs=[pl.BlockSpec(memory_space=pltpu.SMEM)] + [spec] * (len(operands) - 1),
        out_specs=[spec] * len(outs),
        scratch_shapes=list(scratch),
        cost_estimate=pl.CostEstimate(flops=flops, bytes_accessed=moved, transcendentals=0),
        name=body.__name__,
    )(*operands)


AT_PLANE, AT_SHARD, AT_FSDP, AT_COUNT = 0, 1, 2, 3


def mm(left, right, left_dim=1, right_dim=0):
    return lax.dot_general(
        left, right, (((left_dim,), (right_dim,)), ((), ())), preferred_element_type=F32
    )


def ordered(place, vec, row, swap):
    size = vec.shape[1] // PLANE
    blocks = []
    for j in range(PLANE):
        block = (place[AT_PLANE] ^ j) if swap else j
        blocks.append(vec[row : row + 1, pl.ds(pl.multiple_of(block * size, size), size)])
    return jnp.concatenate(blocks, axis=1)


def quarter_at(place, size, far_side):
    shard = place[AT_SHARD] ^ (2 if far_side else 0)
    return pl.multiple_of((shard * 2 + (place[AT_FSDP] & 1)) * size, size)


def unit_rows(values):
    center = values - jnp.mean(values, axis=-1, keepdims=True)
    scale = lax.rsqrt(jnp.mean(center * center, axis=-1, keepdims=True) + NORM_EPS)
    return center * scale, scale


def unit_back(unit, scale, grad_unit):
    mean_grad = jnp.mean(grad_unit, axis=-1, keepdims=True)
    mean_dot = jnp.mean(grad_unit * unit, axis=-1, keepdims=True)
    return scale * (grad_unit - mean_grad - unit * mean_dot)


def attn_forward(swap, place, vec, every, t0, t1, t2, t3, n0, n1, n2, n3, f0, f1, f2, f3,
                 act, qkv, probs, mixed, own, kept, sent):
    count = t0.shape[0]
    half = n0.shape[1] // 4
    width = vec.shape[1]
    size = width // PLANE
    gain, shift = ordered(place, vec, 0, swap), ordered(place, vec, 1, swap)
    for b, ref in enumerate((t0, t1, t2, t3)):
        unit, _ = unit_rows(ref[...].astype(F32))
        act[b * count : (b + 1) * count] = (unit * gain + shift).astype(BF16)
    for side, pieces in enumerate(((n0, n1, n2, n3), (f0, f1, f2, f3))):
        total = mm(act[:, :size], pieces[0][:, : 3 * half])
        for k in range(1, PLANE):
            total = total + mm(act[:, k * size : (k + 1) * size], pieces[k][:, : 3 * half])
        at = quarter_at(place, half, side == 1)
        bias = [vec[6:7, pl.ds(at, half)], jnp.zeros((1, half), F32), vec[7:8, pl.ds(at, half)]]
        total = total + jnp.concatenate(bias, axis=1)
        qkv[:, side * 3 * half : (side + 1) * 3 * half] = total.astype(BF16)
    keys = lax.broadcasted_iota(jnp.int32, (count, count), 0)
    queries = lax.broadcasted_iota(jnp.int32, (count, count), 1)

    def block(b, carry):
        rows = pl.ds(pl.multiple_of(b * count, count), count)
        device = (place[AT_FSDP] ^ (b & 1)) * place[AT_COUNT] + (place[AT_SHARD] ^ (b >> 1))
        starts = every[device].astype(F32)[9:10, :count].astype(jnp.int32)
        seen = (keys >= starts) & (keys <= queries)
        outs = []
        for h in range(BLOCKS):
            base = (h // 2) * 3 * half + (h % 2) * HEAD_DIM
            query = qkv[rows, base : base + HEAD_DIM]
            key = qkv[rows, base + half : base + half + HEAD_DIM]
            value = qkv[rows, base + 2 * half : base + 2 * half + HEAD_DIM]
            scores = jnp.where(seen, mm(key, query, 1, 1) * HEAD_DIM**-0.5, NEG_FILL)
            grown = jnp.exp(scores - jnp.max(scores, axis=0, keepdims=True))
            prob = grown / jnp.sum(grown, axis=0, keepdims=True)
            probs[b, h] = prob
            outs.append(mm(prob.astype(BF16), value, 0, 0))
        mixed[rows, :] = jnp.concatenate(outs, axis=1).astype(BF16)
        return carry

    lax.fori_loop(0, BLOCKS, block, 0)
    for k, (near, far_) in enumerate(zip((n0, n1, n2, n3), (f0, f1, f2, f3))):
        cols = slice(k * size, (k + 1) * size)
        part = mm(mixed[:, :half], near[:, 3 * half :], 1, 1)
        part = part + mm(mixed[:, half:], far_[:, 3 * half :], 1, 1)
        split_blocks(part, cols, count, own, kept, sent)


def split_blocks(part, cols, count, own, kept, sent):
    own[:, cols] = part[:count]
    kept[:, cols] = part[2 * count : 3 * count]
    sent[:count, cols] = part[count : 2 * count].astype(BF16)
    sent[count:, cols] = part[3 * count :].astype(BF16)


def natural(place, j, size, swap):
    return pl.ds(pl.multiple_of(((place[AT_PLANE] ^ j) if swap else j) * size, size), size)


def mlp_norm(swap, place, vec, tokens, own, received, across, hidden, hidden_natural, act):
    count, width = tokens.shape
    size = width // PLANE
    total = tokens[...].astype(F32) + ordered(place, vec, 2, swap)
    total = total + (own[...] + received[:count].astype(F32) + across[...].astype(F32))
    hidden[...] = total
    unit, _ = unit_rows(total)
    low = (unit * ordered(place, vec, 3, swap) + ordered(place, vec, 4, swap)).astype(BF16)
    for j in range(PLANE):
        there = natural(place, j, size, swap)
        act[:, there] = low[:, j * size : (j + 1) * size]
        hidden_natural[:, there] = total[:, j * size : (j + 1) * size]


def split_ring(part, cols, count, own, s1, s2, s3):
    own[:, cols] = part[:count]
    for k, ref in enumerate((s1, s2, s3)):
        ref[:, cols] = part[(k + 1) * count : (k + 2) * count].astype(BF16)


def mlp_forward(place, up_bias, up, down, a0, a1, a2, a3, g0, g1, g2, g3, act_up, grad_pre,
                bias_sum, own, s1, s2, s3, act, grad):
    count, width = a0.shape
    units = up.shape[1]
    tile = min(256, units)
    for b, (act_ref, grad_ref) in enumerate(zip((a0, a1, a2, a3), (g0, g1, g2, g3))):
        act[b * count : (b + 1) * count] = act_ref[...]
        grad[b * count : (b + 1) * count] = grad_ref[...]
    bias_sum[...] = jnp.zeros(bias_sum.shape, F32)
    start = place[AT_SHARD] * units

    def step(j, carry):
        inner = pl.ds(pl.multiple_of(j * tile, tile), tile)
        whole = pl.ds(pl.multiple_of(start + j * tile, tile), tile)
        pre = mm(act[...], up[:, inner]) + up_bias[:, whole]
        square = pre * pre
        bend = jnp.tanh(GELU_ROOT * (pre + GELU_CUBE * square * pre))
        half_in = 0.5 * (1.0 + bend)
        act_up[:, inner] = (pre * half_in).astype(BF16)
        slope = half_in + 0.5 * pre * (1.0 - bend * bend) * (
            GELU_ROOT * (1.0 + 3.0 * GELU_CUBE * square)
        )
        back = mm(grad[...], down[:, inner]) * slope
        grad_pre[:, inner] = back.astype(BF16)
        bias_sum[:, whole] = jnp.sum(back, axis=0, keepdims=True)
        return carry

    lax.fori_loop(0, units // tile, step, 0)
    size = width // PLANE
    for k in range(PLANE):
        cols = slice(k * size, (k + 1) * size)
        split_ring(mm(grad_pre[...], up[cols], 1, 1), cols, count, own, s1, s2, s3)


def unit_grads(swap, place, act_up, grad_pre, down, a0, a1, a2, a3, g0, g1, g2, g3,
               g_down, g_up, own, s1, s2, s3, rows):
    count, width = a0.shape
    half_units = g_up.shape[1] // 2
    size = width // PLANE
    for b, ref in enumerate((g0, g1, g2, g3)):
        rows[b * count : (b + 1) * count] = ref[...]
    for side in range(2):
        cols = slice(side * half_units, (side + 1) * half_units)
        g_down[:, cols] = mm(rows[...], act_up[:, cols], 0, 0).astype(BF16)
    for b, ref in enumerate((a0, a1, a2, a3)):
        rows[b * count : (b + 1) * count] = ref[...]
    if swap:
        size = width // (2 * PLANE)
        for far_core in range(2):
            for k in range(PLANE):
                block = (place[AT_FSDP] ^ (2 * k)) ^ far_core
                there = pl.ds(pl.multiple_of(block * size, size), size)
                at = (far_core * PLANE + k) * size
                g_up[at : at + size] = mm(rows[:, there], grad_pre[...], 0, 0).astype(BF16)
    else:
        for side in range(2):
            cols = slice(side * half_units, (side + 1) * half_units)
            g_up[:, cols] = mm(rows[...], grad_pre[:, cols], 0, 0).astype(BF16)
    size = width // PLANE
    for k in range(PLANE):
        cols = slice(k * size, (k + 1) * size)
        split_ring(mm(act_up[...], down[cols], 1, 1), cols, count, own, s1, s2, s3)


def norm_back(swap, place, vec, hidden, grad_out, own, r1, r2, r3, grad_hidden, low, sums):
    width = hidden.shape[1]
    size = width // PLANE
    unit, scale = unit_rows(hidden[...])
    blocks = []
    for j in range(PLANE):
        there = natural(place, j, size, swap)
        block = own[:, there]
        for ref in (r1, r2, r3):
            block = block + ref[:, there].astype(F32)
        blocks.append(block)
    grad = jnp.concatenate(blocks, axis=1)
    total = grad_out[...] + unit_back(unit, scale, grad * ordered(place, vec, 3, swap))
    grad_hidden[...] = total
    low[...] = total.astype(BF16)
    sums[0:1] = jnp.sum(grad * unit, axis=0, keepdims=True)
    sums[1:2] = jnp.sum(grad, axis=0, keepdims=True)
    sums[2:3] = jnp.sum(total, axis=0, keepdims=True)
    sums[3:4] = jnp.sum(grad_out[...], axis=0, keepdims=True)


def attn_backward(place, qkv, probs, mixed, act, h0, h1, h2, h3, n0, n1, n2, n3, f0, f1, f2, f3,
                  far_out, near_out, low, bias_sum, grad, grad_mixed):
    count, width = h0.shape
    size = width // PLANE
    half = n0.shape[1] // 4
    for b, ref in enumerate((h0, h1, h2, h3)):
        grad[b * count : (b + 1) * count] = ref[...]
    sides = ((n0, n1, n2, n3), (f0, f1, f2, f3))
    for side, pieces in enumerate(sides):
        total = mm(grad[:, :size], pieces[0][:, 3 * half :])
        for k in range(1, PLANE):
            total = total + mm(grad[:, k * size : (k + 1) * size], pieces[k][:, 3 * half :])
        grad_mixed[:, side * half : (side + 1) * half] = total.astype(BF16)
    bias_sum[...] = jnp.zeros(bias_sum.shape, F32)

    def block(b, sums):
        rows = pl.ds(pl.multiple_of(b * count, count), count)
        parts = [[], [], []]
        for h in range(BLOCKS):
            base = (h // 2) * 3 * half + (h % 2) * HEAD_DIM
            query = qkv[rows, base : base + HEAD_DIM]
            key = qkv[rows, base + half : base + half + HEAD_DIM]
            value = qkv[rows, base + 2 * half : base + 2 * half + HEAD_DIM]
            out = grad_mixed[rows, h * HEAD_DIM : (h + 1) * HEAD_DIM]
            prob = probs[b, h]
            back = mm(value, out, 1, 1)
            mean = jnp.sum(prob * back, axis=0, keepdims=True)
            scores = (prob * (back - mean) * HEAD_DIM**-0.5).astype(BF16)
            parts[0].append(mm(scores, key, 0, 0))
            parts[1].append(mm(scores, query, 1, 0))
            parts[2].append(mm(prob.astype(BF16), out, 1, 0))
        new = []
        for side in range(2):
            for which in range(3):
                joined = jnp.concatenate(parts[which][2 * side : 2 * side + 2], axis=1)
                base = (side * 3 + which) * half
                low[rows, base : base + half] = joined.astype(BF16)
                if which != 1:
                    new.append(jnp.sum(joined, axis=0, keepdims=True))
        return tuple(a + c for a, c in zip(sums, new))

    zero = jnp.zeros((1, half), F32)
    sums = lax.fori_loop(0, BLOCKS, block, (zero,) * 4)
    for side in range(2):
        at = quarter_at(place, half, side == 1)
        bias_sum[0:1, pl.ds(at, half)] = sums[2 * side]
        bias_sum[1:2, pl.ds(at, half)] = sums[2 * side + 1]
    for side, out in ((1, far_out), (0, near_out)):
        out[:, : 3 * half] = mm(
            act[...], low[:, side * 3 * half : (side + 1) * 3 * half], 0, 0
        ).astype(BF16)
        out[:, 3 * half :] = mm(
            grad[...], mixed[:, side * half : (side + 1) * half], 0, 0
        ).astype(BF16)


def attn_return(place, low, n0, n1, n2, n3, f0, f1, f2, f3, own, kept, sent):
    count = own.shape[0]
    half = n0.shape[1] // 4
    size = own.shape[1] // PLANE
    for k, (near, far_) in enumerate(zip((n0, n1, n2, n3), (f0, f1, f2, f3))):
        part = mm(low[:, : 3 * half], near[:, : 3 * half], 1, 1)
        part = part + mm(low[:, 3 * half :], far_[:, : 3 * half], 1, 1)
        split_blocks(part, slice(k * size, (k + 1) * size), count, own, kept, sent)


def input_back(swap, place, vec, tokens, grad_hidden, own, received, across, grad_in, sums):
    count = tokens.shape[0]
    unit, scale = unit_rows(tokens[...].astype(F32))
    grad = own[...] + received[:count].astype(F32) + across[...].astype(F32)
    gain = ordered(place, vec, 0, swap)
    grad_in[...] = grad_hidden[...] + unit_back(unit, scale, grad * gain)
    sums[0:1] = jnp.sum(grad * unit, axis=0, keepdims=True)
    sums[1:2] = jnp.sum(grad, axis=0, keepdims=True)


def on_device(
    tokens,
    cotangent,
    starts,
    counts,
    attn_gain,
    attn_shift,
    w_qkv,
    query_bias,
    value_bias,
    w_proj,
    proj_bias,
    mlp_gain,
    mlp_shift,
    w_up,
    up_bias,
    w_down,
    down_bias,
):
    slot_count, width = tokens.shape
    shard, fsdp = lax.axis_index("shard"), lax.axis_index("fsdp")
    shard_count, fsdp_count = lax.axis_size("shard"), lax.axis_size("fsdp")
    devices = shard_count * fsdp_count
    bit = fsdp % 2
    swap = plane_count() == PLANE
    place = jnp.stack([plane_index(), shard, fsdp, jnp.int32(shard_count)]).astype(jnp.int32)
    rows = w_qkv.shape[0]
    quarter = w_qkv.shape[2]
    half = quarter // 2
    units = w_up.shape[1]
    row_count = BLOCKS * slot_count

    with jax.named_scope("attn_weights"):
        attn_piece = jnp.concatenate(
            [
                jnp.transpose(w_qkv.reshape(rows, 3, 2, half), (0, 2, 1, 3)).reshape(
                    rows, 2, 3 * half
                ),
                w_proj.T.reshape(rows, 2, half),
            ],
            axis=2,
        )
        attn_near = to_rows(attn_piece, bit)
    with jax.named_scope("token_rows"):
        first, attn_near = hold(tokens, attn_near)
        token_low = reorder(first)
        token_across = pair(token_low)
    with jax.named_scope("attn_weights"):
        attn_far = far(attn_near)
        near = gather_pieces(attn_near)
    with jax.named_scope("vectors"):
        pieces = [
            v.reshape(1, -1)
            for v in (
                attn_gain,
                attn_shift,
                proj_bias,
                mlp_gain,
                mlp_shift,
                down_bias,
                query_bias,
                value_bias,
                up_bias,
                starts,
            )
        ]
        lanes = max(piece.shape[1] for piece in pieces)
        packed = pl.pallas_call(
            pack_rows,
            out_shape=jax.ShapeDtypeStruct((devices, 16, lanes), BF16),
            scratch_shapes=[pltpu.VMEM((16, lanes), F32)],
            name="pack_rows",
        )(*pieces)
    live = (jnp.arange(slot_count, dtype=jnp.int32) < counts[0]).astype(F32)[:, None]
    grad_natural = cotangent.astype(F32) * live
    grad_low = grad_natural.astype(BF16)
    grad_out = reorder(cotangent).astype(F32) * live
    grad_low, attn_far, token_low, token_across, packed, place, up, *near = hold(
        grad_low, attn_far, token_low, token_across, packed, place, w_up, *near
    )
    with jax.named_scope("mlp_weights"):
        up = lax.all_gather(up, "fsdp", axis=0, tiled=True)
    with jax.named_scope("attn_weights"):
        away = gather_pieces(attn_far)
    with jax.named_scope("token_rows"):
        token_rows = [token_low, core(token_low), token_across, core(token_across)]
    with jax.named_scope("vectors"):
        every = lax.all_to_all(packed, ("fsdp", "shard"), 0, 0, tiled=True)
        grid = every.reshape(fsdp_count, shard_count, 16, lanes)
        size = attn_gain.shape[1]
        vec = jnp.transpose(grid[:, :, :8, :size], (2, 1, 0, 3)).reshape(8, -1).astype(F32)
        size = up_bias.shape[1]
        up_vec = jnp.transpose(grid[:, :, 8, :size], (1, 0, 2)).reshape(1, -1).astype(F32)
    with jax.named_scope("grad_rows"):
        grad_rows = [grad_low, ring(grad_low, 1), ring(grad_low, 2), None]
    every, vec, up_vec, down, *held = hold(
        every, vec, up_vec, w_down.T, *grad_rows[:3], *token_rows, *away
    )
    grad_rows, token_rows, away = held[:3], held[3 : 3 + BLOCKS], held[3 + BLOCKS :]
    with jax.named_scope("mlp_weights"):
        down = lax.all_gather(down, "fsdp", axis=0, tiled=True)
    with jax.named_scope("grad_rows"):
        grad_rows.append(ring(grad_rows[0], 3))
    block = (slot_count, width)
    parts = [(block, F32), (block, F32), ((2 * slot_count, width), BF16)]
    act, qkv, probs, mixed, *attn_parts = run(
        functools.partial(attn_forward, swap),
        [
            ((row_count, width), BF16),
            ((row_count, 3 * quarter), BF16),
            ((BLOCKS, BLOCKS, slot_count, slot_count), F32),
            ((row_count, quarter), BF16),
            *parts,
        ],
        place,
        vec,
        every,
        *token_rows,
        *near,
        *away,
    )
    held = hold(*attn_parts, *grad_rows)
    attn_parts, grad_rows = held[:3], held[3:]
    with jax.named_scope("attn_return"):
        attn_term = return_blocks(*attn_parts)
    hidden, hidden_natural, mlp_act = run(
        functools.partial(mlp_norm, swap),
        [(block, F32), (block, F32), (block, BF16)],
        place,
        vec,
        token_low,
        *attn_term,
    )
    with jax.named_scope("mlp_inputs"):
        mlp_rows = gather_ring(mlp_act)
    whole = pltpu.VMEM((row_count, width), BF16)
    ring_parts = [(block, F32)] + [(block, BF16)] * (BLOCKS - 1)
    act_up, grad_pre, up_bias_sum, *normed_parts = run(
        mlp_forward,
        [((row_count, units), BF16), ((row_count, units), BF16), (up_vec.shape, F32), *ring_parts],
        place,
        up_vec,
        up,
        down,
        *mlp_rows,
        *grad_rows,
        scratch=[whole, whole],
    )
    with jax.named_scope("normed_return"):
        grad_normed = return_ring(*normed_parts)
    g_down, g_up, *mlp_parts = run(
        functools.partial(unit_grads, swap),
        [((width, units), BF16)] * 2 + ring_parts,
        place,
        act_up,
        grad_pre,
        down,
        *mlp_rows,
        *grad_rows,
        scratch=[whole],
    )
    with jax.named_scope("down_grads"):
        g_down_own = lax.psum_scatter(g_down, "fsdp", scatter_dimension=0, tiled=True)
    g_down, g_up, *held = hold(g_down, g_up, *mlp_parts, *grad_normed)
    mlp_parts, grad_normed = held[:BLOCKS], held[BLOCKS:]
    grad_hidden, hidden_low, sums = run(
        functools.partial(norm_back, swap),
        [(block, F32), (block, BF16), ((4, width), F32)],
        place,
        vec,
        hidden,
        grad_out,
        *grad_normed,
    )
    with jax.named_scope("hidden_rows"):
        hidden_rows = gather_blocks(hidden_low)
    with jax.named_scope("up_grads"):
        if swap:
            mid = width // 2
            g_up_half = (g_up[:mid].astype(F32) + core(g_up[mid:]).astype(F32)).astype(BF16)
        else:
            g_up_half = g_up
    g_up_half, *hidden_rows = hold(g_up_half, *hidden_rows)
    with jax.named_scope("mlp_return"):
        mlp_own, *mlp_others = return_ring(*mlp_parts)
    with jax.named_scope("up_grads"):
        if swap:
            g_up = reduce_plane(g_up_half)
        else:
            g_up = lax.psum_scatter(g_up, "fsdp", scatter_dimension=0, tiled=True).astype(F32)
    side = ((width, 4 * half), BF16)
    g_attn_far, g_attn_near, low, bias_sum = run(
        attn_backward,
        [side, side, ((row_count, 3 * quarter), BF16), ((2, width), F32)],
        place,
        qkv,
        probs,
        mixed,
        act,
        *hidden_rows,
        *near,
        *away,
        scratch=[whole, pltpu.VMEM((row_count, quarter), BF16)],
    )
    back_parts = run(attn_return, parts, place, low, *near, *away)
    g_attn_far, g_attn_near, g_up, *held = hold(
        g_attn_far, g_attn_near, g_up, *back_parts, *mlp_others[:2]
    )
    back_parts, mlp_others = held[:3], held[3:] + mlp_others[2:]
    with jax.named_scope("attn_grads"):
        g_attn_far = reduce_plane(g_attn_far).astype(BF16)
    with jax.named_scope("attn_back"):
        grad_attn = return_blocks(*back_parts)
    g_attn_far, g_attn_near, g_down_own, *held = hold(
        g_attn_far, g_attn_near, g_down_own, *grad_attn, *mlp_others
    )
    grad_attn, mlp_others = held[:3], held[3:]
    with jax.named_scope("attn_grads"):
        g_attn_near = reduce_plane(g_attn_near)
        g_attn_far = far(g_attn_far)
    with jax.named_scope("mlp_return"):
        mlp_term = mlp_own + sum(part.astype(F32) for part in mlp_others)
    block_out = ((hidden_natural + mlp_term + vec[5:6]) * live).astype(BF16)
    grad_in, in_sums = run(
        functools.partial(input_back, swap),
        [(block, F32), ((2, width), F32)],
        place,
        vec,
        token_low,
        grad_hidden,
        *grad_attn,
    )
    with jax.named_scope("small_grads"):
        flat = jnp.concatenate([reorder(jnp.concatenate([in_sums, sums], axis=0)), bias_sum])
        flat = flat.reshape(8, shard_count, fsdp_count, -1)
        flat = jnp.transpose(flat, (2, 1, 0, 3)).reshape(devices, -1)
        size = up_bias.shape[1]
        upper = jnp.transpose(up_bias_sum.reshape(shard_count, fsdp_count, size), (1, 0, 2))
        small = jnp.concatenate([flat, upper.reshape(devices, size)], axis=1)
        small, g_attn_near = hold(small, g_attn_near)
        small = jnp.sum(lax.all_to_all(small, ("fsdp", "shard"), 0, 0, tiled=True), axis=0)
        size = attn_gain.shape[1]
        g_vec = small[: 8 * size].reshape(8, 1, size)
        g_up_bias = small[8 * size :].reshape(1, -1)
    with jax.named_scope("attn_grads"):
        g_attn = from_rows((g_attn_near + g_attn_far.astype(F32)).astype(BF16), bit).astype(F32)
    g_qkv = jnp.transpose(g_attn[:, :, : 3 * half].reshape(rows, 2, 3, half), (0, 2, 1, 3))
    return (
        block_out,
        reorder(grad_in),
        g_vec[0],
        g_vec[1],
        g_qkv.reshape(w_qkv.shape),
        g_vec[6],
        g_vec[7],
        g_attn[:, :, 3 * half :].reshape(rows, quarter).T,
        g_vec[4],
        g_vec[2],
        g_vec[3],
        g_up,
        g_up_bias,
        g_down_own.astype(F32).T,
        g_vec[5],
    )


def solution(mesh):
    in_specs = (
        P(("fsdp", "shard"), None),
        P(("fsdp", "shard"), None),
        P(("fsdp", "shard")),
        P(("fsdp", "shard")),
        P("shard", "fsdp"),
        P("shard", "fsdp"),
        P("fsdp", None, "shard"),
        P("shard", "fsdp"),
        P("shard", "fsdp"),
        P("shard", "fsdp"),
        P("shard", "fsdp"),
        P("shard", "fsdp"),
        P("shard", "fsdp"),
        P("fsdp", "shard"),
        P("shard", "fsdp"),
        P("shard", "fsdp"),
        P("shard", "fsdp"),
    )
    out_specs = (
        P(("fsdp", "shard"), None),
        P(("fsdp", "shard"), None),
        P("shard", "fsdp"),
        P("shard", "fsdp"),
        P("fsdp", None, "shard"),
        P("shard", "fsdp"),
        P("shard", "fsdp"),
        P("shard", "fsdp"),
        P("shard", "fsdp"),
        P("shard", "fsdp"),
        P("shard", "fsdp"),
        P("fsdp", "shard"),
        P("shard", "fsdp"),
        P("shard", "fsdp"),
        P("shard", "fsdp"),
    )
    return jax.shard_map(
        on_device, mesh=mesh, in_specs=in_specs, out_specs=out_specs, check_vma=False
    )
```

time: 318 us -> 244 us (0.77)
  waiting for transfers between devices: 175 us -> 80.6 us
  Pallas kernels: 0 us -> 53.1 us
  matrix products: 39.2 us -> 0 us
  starting transfers between devices: 25.1 us -> 62.3 us
  other arithmetic: 28.1 us -> 14.8 us
  blocking collectives: 11.6 us -> 0 us
  local copies, waits for them, and re-layouts: 22.2 us -> 16.7 us
    pallas_call x0 -> x9, Pallas kernels: none -> 53.1 us  [the longest x8 51.6 us: run(): pl.pallas_call(kernel, out_shape=[jax.ShapeDtypeStruct(shape, kind) for s...]
    reduce_scatter x3 -> x1, waiting for transfers between devices: 51 us -> 0.01 us  [on_device(): lax.psum_scatter(g_down, 'fsdp', scatter_dimension=0, tiled=True)]
    ppermute x0 -> x27, waiting for transfers between devices: none -> 47.6 us  [the longest x12 34.2 us: ring(): lax.ppermute(array, 'shard', [(index, index ^ distance) for index in rang...]
    ppermute x4 -> x2, waiting for transfers between devices: 47.4 us -> 2.17 us  [far(): lax.ppermute(array, 'shard', [(index, index ^ 2) for index in range(count)])]
    ppermute x0 -> x27, starting transfers between devices: none -> 42.1 us  [the longest x12 22.2 us: ring(): lax.ppermute(array, 'shard', [(index, index ^ distance) for index in rang...]
    dot_general x18 -> x0, matrix products: 39.2 us -> none  [the longest x12 32.5 us: dot(): lax.dot_general(left, right, (((left_dim,), (right_dim,)), ((), ())), pre...]
    all_gather x3 -> x2, waiting for transfers between devices: 25.3 us -> 0.04 us  [the longest x1 0.02 us: on_device(): down = lax.all_gather(down, 'fsdp', axis=0, tiled=True)]
    ppermute x8 -> x4, waiting for transfers between devices: 38.1 us -> 23.4 us  [pair(): lax.ppermute(array, 'shard', [(index, index ^ 1) for index in range(count)])]
  transfers between devices with their start and end apart: 35 -> 47, of which waited for: 19 -> 17; matrix products, arithmetic and copies ran while one was open for 23% -> 9% of each run, Pallas kernels for 0% -> 18%
where the time goes in v2:
time: 244 us; the launch traced here: 243 us
  waiting for transfers between devices  80.6 us (33%)
  starting transfers between devices  62.3 us (26%)
  Pallas kernels  53.1 us (22%)
  local copies, waits for them, and re-layouts  16.7 us (7%)
  between operations  15.3 us (6%)
  other arithmetic  14.8 us (6%)
    pallas_call x8, Pallas kernels, run(): pl.pallas_call(kernel, out_shape=[jax.ShapeDtypeStruct(shape, kind) for s...  51.6 us
    ppermute x12, waiting for transfers between devices, ring(): lax.ppermute(array, 'shard', [(index, index ^ distance) for index in rang...  34.2 us
    ppermute x4, waiting for transfers between devices, pair(): lax.ppermute(array, 'shard', [(index, index ^ 1) for index in range(count)])  23.4 us
    ppermute x12, starting transfers between devices, ring(): lax.ppermute(array, 'shard', [(index, index ^ distance) for index in rang...  22.2 us
    ppermute x15, starting transfers between devices, plane(): lax.ppermute(array, 'fsdp', [(index, index ^ 2 * distance) for index in r...  19.9 us
    ppermute x15, waiting for transfers between devices, plane(): lax.ppermute(array, 'fsdp', [(index, index ^ 2 * distance) for index in r...  13.4 us
    unnamed x92, local copies, waits for them, and re-layouts  6.4 us
    ppermute x4, starting transfers between devices, pair(): lax.ppermute(array, 'shard', [(index, index ^ 1) for index in range(count)])  6.32 us
  transfers between devices with their start and end apart: 47, of which 17 were waited for; matrix products, arithmetic and copies ran while one was open for 9% of the time, Pallas kernels for 18%

profile of v2, /device:TPU:0, one launch (start us, length us, event | category | flops | bytes accessed | tf_op | source)
XLA Modules:
  0.0 242.7 jit_solution(11376442400957679609)
XLA Ops:
  11.8 3.7 %collective-permute-start.1 = (bf16[256,512]{1,0:T(8,128)(2,1)S(1)}, bf16[256,512]{1,0:T(8,128)(2,1)S(1)}, u32[]{:S(2)}, u32[]{:S(2)}) collective-permute-start(bf16[256,512]{1,0:T(8,128)(2,1)S(1)} %maximum_select_fusion.2.n0), channel_id=1, source_target_pairs={{0,2},{1,3},{2,0},{3,1},{4,6},{5,7},{6,4},{7,5},{8,10},{9,11},{10,... | collective-permute-start | bytes 786440 | tf_op jit(solution)/shard_map/attn_weights/ppermute | solution.py:32
  23.8 7.5 %collective-permute-done.2.t2 = bf16[128,1024]{1,0:T(8,128)(2,1)S(1)} collective-permute-done((bf16[128,1024]{1,0:T(8,128)(2,1)S(1)}, bf16[128,1024]{1,0:T(8,128)(2,1)S(1)}, u32[]{:S(2)}, u32[]{:S(2)}) %collective-permute-start.2) | collective-permute-done | bytes 262176 | tf_op jit(solution)/shard_map/token_rows/ppermute | solution.py:27
  34.5 2.8 %all-to-all-start = ((bf16[32,16,128]{2,1,0:T(8,128)(2,1)}), bf16[32,16,128]{2,1,0:T(8,128)(2,1)S(1)}, u32[]{:S(2)}, u32[]{:S(2)}) async-start(bf16[32,16,128]{2,1,0:T(8,128)(2,1)} %pack_rows.1), calls=%async_computation | async-start | bytes 262144 | tf_op jit(solution)/shard_map/vectors/all_to_all | solution.py:528
  38.2 2.7 %collective-permute-start.12 = (bf16[256,512]{1,0:T(8,128)(2,1)S(1)}, bf16[256,512]{1,0:T(8,128)(2,1)S(1)}, u32[]{:S(2)}, u32[]{:S(2)}) collective-permute-start(bf16[256,512]{1,0:T(8,128)(2,1)S(1)} %collective-permute-done.1.f0), channel_id=1, source_target_pairs={{0,24},{4,28},{8,16},{12,20},{16,8},{20,12},{24,0},{28,4},{1,25},{... | collective-permute-start | bytes 786440 | tf_op jit(solution)/shard_map/attn_weights/ppermute | solution.py:66
  47.9 3.5 %collective-permute-done.12.f3 = bf16[256,512]{1,0:T(8,128)(2,1)S(1)} collective-permute-done((bf16[256,512]{1,0:T(8,128)(2,1)S(1)}, bf16[256,512]{1,0:T(8,128)(2,1)S(1)}, u32[]{:S(2)}, u32[]{:S(2)}) %collective-permute-start.12) | collective-permute-done | bytes 262176 | tf_op jit(solution)/shard_map/attn_weights/ppermute | solution.py:66
  51.4 3.2 %collective-permute-done.6.g1 = bf16[128,1024]{1,0:T(8,128)(2,1)S(1)} collective-permute-done((bf16[128,1024]{1,0:T(8,128)(2,1)S(1)}, bf16[128,1024]{1,0:T(8,128)(2,1)S(1)}, u32[]{:S(2)}, u32[]{:S(2)}) %collective-permute-start.6) | collective-permute-done | bytes 262176 | tf_op jit(solution)/shard_map/grad_rows/ppermute | solution.py:73
  59.4 10.7 %attn_forward.1 = (bf16[512,1024]{1,0:T(8,128)(2,1)}, bf16[512,768]{1,0:T(8,128)(2,1)}, f32[4,4,128,128]{3,2,1,0:T(8,128)}, bf16[512,256]{1,0:T(8,128)(2,1)}, f3...) custom-call(s32[4]{0:T(128)} %pad_add_fusion.place, f32[8,1024]{1,0:T(8,128)} %reshape.131.vec, ...), custom_call_target="tpu_custom_call" | custom-call | bytes 10649616 | tf_op jit(solution)/shard_map/attn_forward/pallas_call | solution.py:155
  73.7 8.3 %collective-permute-done.15.across = bf16[128,1024]{1,0:T(8,128)(2,1)S(1)} collective-permute-done((bf16[128,1024]{1,0:T(8,128)(2,1)S(1)}, bf16[128,1024]{1,0:T(8,128)(2,1)S(1)}, u32[]{:S(2)}, u32[]{:S(2)}) %collective-permute-start.15) | collective-permute-done | bytes 262176 | tf_op jit(solution)/shard_map/attn_return/ppermute | solution.py:27
  89.7 7.6 %collective-permute-done.16.a1 = bf16[128,1024]{1,0:T(8,128)(2,1)S(1)} collective-permute-done((bf16[128,1024]{1,0:T(8,128)(2,1)}, bf16[128,1024]{1,0:T(8,128)(2,1)S(1)}, u32[]{:S(2)}, u32[]{:S(2)}) %collective-permute-start.16) | collective-permute-done | bytes 262176 | tf_op jit(solution)/shard_map/mlp_inputs/ppermute | solution.py:73
  97.3 9.9 %collective-permute-done.17.a2 = bf16[128,1024]{1,0:T(8,128)(2,1)S(1)} collective-permute-done((bf16[128,1024]{1,0:T(8,128)(2,1)}, bf16[128,1024]{1,0:T(8,128)(2,1)S(1)}, u32[]{:S(2)}, u32[]{:S(2)}) %collective-permute-start.17) | collective-permute-done | bytes 262176 | tf_op jit(solution)/shard_map/mlp_inputs/ppermute | solution.py:73
  108.0 9.1 %mlp_forward.1 = (bf16[512,1024]{1,0:T(8,128)(2,1)}, bf16[512,1024]{1,0:T(8,128)(2,1)}, f32[1,4096]{1,0:T(1,128)}, f32[128,1024]{1,0:T(8,128)}, bf16[128,1024]{1...) custom-call(s32[4]{0:T(128)} %pad_add_fusion.place, f32[1,4096]{1,0:T(1,128)} %bitcast.87, ...), custom_call_target="tpu_custom_call" | custom-call | bytes 12615696 | tf_op jit(solution)/shard_map/mlp_forward/pallas_call | solution.py:155
  117.1 4.5 %collective-permute-start.19 = (bf16[128,1024]{1,0:T(8,128)(2,1)}, bf16[128,1024]{1,0:T(8,128)(2,1)S(1)}, u32[]{:S(2)}, u32[]{:S(2)}) collective-permute-start(bf16[128,1024]{1,0:T(8,128)(2,1)} %get-tuple-element.167), channel_id=1, source_target_pairs={{0,1},{1,0},{2,3},{3,2},{4,5},{5,4},{6,7},{7,6},{8,9},{9,8},{10,11... | collective-permute-start | bytes 786440 | tf_op jit(solution)/shard_map/normed_return/ppermute | solution.py:73
  124.1 7.3 %unit_grads.1 = (bf16[1024,1024]{1,0:T(8,128)(2,1)}, bf16[1024,1024]{1,0:T(8,128)(2,1)}, f32[128,1024]{1,0:T(8,128)}, bf16[128,1024]{1,0:T(8,128)(2,1)}, bf16[12...) custom-call(s32[4]{0:T(128)} %pad_add_fusion.place, bf16[512,1024]{1,0:T(8,128)(2,1)} %get-tuple-element.158.act_up, ...), custom_call_target="tpu_custom_call" | custom-call | bytes 16777232 | tf_op jit(solution)/shard_map/unit_grads/pallas_call | solution.py:155
  131.4 11.5 %collective-permute-done.20.r2 = bf16[128,1024]{1,0:T(8,128)(2,1)S(1)} collective-permute-done((bf16[128,1024]{1,0:T(8,128)(2,1)}, bf16[128,1024]{1,0:T(8,128)(2,1)S(1)}, u32[]{:S(2)}, u32[]{:S(2)}) %collective-permute-start.20) | collective-permute-done | bytes 262176 | tf_op jit(solution)/shard_map/normed_return/ppermute | solution.py:73
  145.1 3.2 %norm_back.1 = (f32[128,1024]{1,0:T(8,128)}, bf16[128,1024]{1,0:T(8,128)(2,1)}, f32[4,1024]{1,0:T(4,128)}) custom-call(s32[4]{0:T(128)} %pad_add_fusion.place, f32[8,1024]{1,0:T(8,128)} %reshape.131.vec, f32[128,1024]{1,0:T(8,128)} %get-tuple-element.176.hidden, f32[128,1024]{1,0:T(8,128)} %get-tuple-element.341.grad_out, ...), custom_call_target="tpu_custom_call" | custom-call | bytes 3457040 | tf_op jit(solution)/shard_map/norm_back/pallas_call | solution.py:155
  148.3 3.8 %collective-permute-start.24 = (bf16[128,1024]{1,0:T(8,128)(2,1)}, bf16[128,1024]{1,0:T(8,128)(2,1)S(1)}, u32[]{:S(2)}, u32[]{:S(2)}) collective-permute-start(bf16[128,1024]{1,0:T(8,128)(2,1)} %get-tuple-element.182.h0), channel_id=1, source_target_pairs={{0,1},{1,0},{2,3},{3,2},{4,5},{5,4},{6,7},{7,6},{8,9},{9,8},{10,11... | collective-permute-start | bytes 786440 | tf_op jit(solution)/shard_map/hidden_rows/ppermute | solution.py:27
  152.2 7.0 %collective-permute-done.24.h2 = bf16[128,1024]{1,0:T(8,128)(2,1)S(1)} collective-permute-done((bf16[128,1024]{1,0:T(8,128)(2,1)}, bf16[128,1024]{1,0:T(8,128)(2,1)S(1)}, u32[]{:S(2)}, u32[]{:S(2)}) %collective-permute-start.24) | collective-permute-done | bytes 262176 | tf_op jit(solution)/shard_map/hidden_rows/ppermute | solution.py:27
  167.3 11.7 %attn_backward.1 = (bf16[1024,512]{1,0:T(8,128)(2,1)}, bf16[1024,512]{1,0:T(8,128)(2,1)}, bf16[512,768]{1,0:T(8,128)(2,1)}, f32[2,1024]{1,0:T(2,128)}) custom-call(s32[4]{0:T(128)} %pad_add_fusion.place, bf16[512,768]{1,0:T(8,128)(2,1)} %get-tuple-element.171.qkv, f32[4,4,128,128]{3,2,1,0:T(8,128)} %get-tuple-element.172.probs, ...), custom_call_target="tpu_custom_call" | custom-call | bytes 12066832 | tf_op jit(solution)/shard_map/attn_backward/pallas_call | solution.py:155
  179.0 4.2 %attn_return.1 = (f32[128,1024]{1,0:T(8,128)}, f32[128,1024]{1,0:T(8,128)}, bf16[256,1024]{1,0:T(8,128)(2,1)}) custom-call(s32[4]{0:T(128)} %pad_add_fusion.place, bf16[512,768]{1,0:T(8,128)(2,1)} %get-tuple-element.189.low, bf16[256,512]{1,0:T(8,128)(2,1)} %copy-done, bf16[256,512]{1,0:T(8,128)(2,1)} %copy-done.4, bf16[256,512]{1,0:T(8,128)(2,1)} %copy-done.5, ...), custom_call_target="tpu_custom_call" | custom-call | bytes 4980752 | tf_op jit(solution)/shard_map/attn_return/pallas_call | solution.py:155
  193.1 4.2 %collective-permute-done.31 = bf16[256,512]{1,0:T(8,128)(2,1)S(1)} collective-permute-done((bf16[256,512]{1,0:T(8,128)(2,1)S(1)}, bf16[256,512]{1,0:T(8,128)(2,1)S(1)}, u32[]{:S(2)}, u32[]{:S(2)}) %collective-permute-start.31) | collective-permute-done | bytes 262176 | tf_op jit(solution)/shard_map/attn_grads/ppermute | solution.py:66
  197.3 5.5 %collective-permute-done.32 = bf16[256,512]{1,0:T(8,128)(2,1)S(1)} collective-permute-done((bf16[256,512]{1,0:T(8,128)(2,1)S(1)}, bf16[256,512]{1,0:T(8,128)(2,1)S(1)}, u32[]{:S(2)}, u32[]{:S(2)}) %collective-permute-start.32) | collective-permute-done | bytes 262176 | tf_op jit(solution)/shard_map/attn_grads/ppermute | solution.py:66
  208.8 2.8 %input_back.1 = (f32[128,1024]{1,0:T(8,128)}, f32[2,1024]{1,0:T(2,128)}) custom-call(s32[4]{0:T(128)} %pad_add_fusion.place, f32[8,1024]{1,0:T(8,128)} %reshape.131.vec, bf16[128,1024]{1,0:T(8,128)(2,1)} %copy-done.1, f32[128,1024]{1,0:T(8,128)} %get-tuple-element.206.grad_hidden, f32[128,1024]{1,0:T(8,128)} %get-tuple-element.207.own, ...), custom_call_target="tpu_custom_call" | custom-call | bytes 2662416 | tf_op jit(solution)/shard_map/input_back/pallas_call | solution.py:155
  221.8 3.8 %all-to-all-start.1 = ((f32[32,1,384]{2,1,0:T(1,128)}), f32[32,1,384]{2,1,0:T(1,128)S(1)}, u32[]{:S(2)}, u32[]{:S(2)}) async-start(f32[32,1,384]{2,1,0:T(1,128)} %copy.83), calls=%async_computation.2 | async-start | bytes 98304 | tf_op jit(solution)/shard_map/small_grads/all_to_all | solution.py:681
  228.9 4.1 %all-to-all-done.1 = f32[32,1,384]{2,1,0:T(1,128)S(1)} async-done(((f32[32,1,384]{2,1,0:T(1,128)}), f32[32,1,384]{2,1,0:T(1,128)S(1)}, u32[]{:S(2)}, u32[]{:S(2)}) %all-to-all-start.1) | async-done | bytes 49184 | tf_op jit(solution)/shard_map/small_grads/all_to_all | solution.py:681
  (233 shorter events, 84.8 us)
Async XLA Ops:
  7.2 100.1 %all-gather.3.cloned.1.call-start = ((), (), s32[]{:S(2)}) async-start(), calls=%async_computation.3 | async-start | bytes 2359296 | tf_op jit(solution)/shard_map/mlp_weights/all_gather | solution.py:522
  11.8 19.5 %collective-permute-start.1 = (bf16[256,512]{1,0:T(8,128)(2,1)S(1)}, bf16[256,512]{1,0:T(8,128)(2,1)S(1)}, u32[]{:S(2)}, u32[]{:S(2)}) collective-permute-start(bf16[256,512]{1,0:T(8,128)(2,1)S(1)} %maximum_select_fusion.2.n0), channel_id=1, source_target_pairs={{0,2},{1,3},{2,0},{3,1},{4,6},{5,7},{6,4},{7,5},{8,10},{9,11},{10,... | collective-permute-start | bytes 786440 | tf_op jit(solution)/shard_map/attn_weights/ppermute | solution.py:32
  15.5 15.8 %collective-permute-start.3 = (bf16[256,512]{1,0:T(8,128)(2,1)S(1)}, bf16[256,512]{1,0:T(8,128)(2,1)S(1)}, u32[]{:S(2)}, u32[]{:S(2)}) collective-permute-start(bf16[256,512]{1,0:T(8,128)(2,1)S(1)} %maximum_select_fusion.2.n0), channel_id=1, source_target_pairs={{0,8},{4,12},{8,0},{12,4},{16,24},{20,28},{24,16},{28,20},{1,9},{5... | collective-permute-start | bytes 786440 | tf_op jit(solution)/shard_map/attn_weights/ppermute | solution.py:66
  17.0 14.3 %collective-permute-start.4 = (bf16[256,512]{1,0:T(8,128)(2,1)S(1)}, bf16[256,512]{1,0:T(8,128)(2,1)S(1)}, u32[]{:S(2)}, u32[]{:S(2)}) collective-permute-start(bf16[256,512]{1,0:T(8,128)(2,1)S(1)} %maximum_select_fusion.2.n0), channel_id=1, source_target_pairs={{0,16},{4,20},{8,24},{12,28},{16,0},{20,4},{24,8},{28,12},{1,17},{... | collective-permute-start | bytes 786440 | tf_op jit(solution)/shard_map/attn_weights/ppermute | solution.py:66
  31.4 14.6 %collective-permute-start.10 = (bf16[256,512]{1,0:T(8,128)(2,1)S(1)}, bf16[256,512]{1,0:T(8,128)(2,1)S(1)}, u32[]{:S(2)}, u32[]{:S(2)}) collective-permute-start(bf16[256,512]{1,0:T(8,128)(2,1)S(1)} %collective-permute-done.1.f0), channel_id=1, source_target_pairs={{0,8},{4,12},{8,0},{12,4},{16,24},{20,28},{24,16},{28,20},{1,9},{5... | collective-permute-start | bytes 786440 | tf_op jit(solution)/shard_map/attn_weights/ppermute | solution.py:66
  37.3 70.0 %all-gather.5.cloned.1.call-start = ((), (), s32[]{:S(2)}) async-start(), calls=%async_computation.4 | async-start | bytes 2359296 | tf_op jit(solution)/shard_map/mlp_weights/all_gather | solution.py:541
  42.3 14.4 %collective-permute-start.7 = (bf16[128,1024]{1,0:T(8,128)(2,1)S(1)}, bf16[128,1024]{1,0:T(8,128)(2,1)S(1)}, u32[]{:S(2)}, u32[]{:S(2)}) collective-permute-start(bf16[128,1024]{1,0:T(8,128)(2,1)S(1)} %get-tuple-element.154.g0), channel_id=1, source_target_pairs={{0,2},{1,3},{2,0},{3,1},{4,6},{5,7},{6,4},{7,5},{8,10},{9,11},{10,... | collective-permute-start | bytes 786440 | tf_op jit(solution)/shard_map/grad_rows/ppermute | solution.py:73
  56.7 147.6 %reduce-scatter.2.cloned.1.call-start = ((), (), s32[]{:S(2)}) async-start(), calls=%async_computation.5 | async-start | bytes 2359296 | tf_op jit(solution)/shard_map/down_grads/reduce_scatter | solution.py:603
  85.6 21.6 %collective-permute-start.17 = (bf16[128,1024]{1,0:T(8,128)(2,1)}, bf16[128,1024]{1,0:T(8,128)(2,1)S(1)}, u32[]{:S(2)}, u32[]{:S(2)}) collective-permute-start(bf16[128,1024]{1,0:T(8,128)(2,1)} %get-tuple-element.153.a0), channel_id=1, source_target_pairs={{0,2},{1,3},{2,0},{3,1},{4,6},{5,7},{6,4},{7,5},{8,10},{9,11},{10,... | collective-permute-start | bytes 786440 | tf_op jit(solution)/shard_map/mlp_inputs/ppermute | solution.py:73
  87.3 20.0 %collective-permute-start.18 = (bf16[128,1024]{1,0:T(8,128)(2,1)}, bf16[128,1024]{1,0:T(8,128)(2,1)S(1)}, u32[]{:S(2)}, u32[]{:S(2)}) collective-permute-start(bf16[128,1024]{1,0:T(8,128)(2,1)} %get-tuple-element.153.a0), channel_id=1, source_target_pairs={{0,3},{1,2},{2,1},{3,0},{4,7},{5,6},{6,5},{7,4},{8,11},{9,10},{10,... | collective-permute-start | bytes 786440 | tf_op jit(solution)/shard_map/mlp_inputs/ppermute | solution.py:73
  117.1 14.3 %collective-permute-start.19 = (bf16[128,1024]{1,0:T(8,128)(2,1)}, bf16[128,1024]{1,0:T(8,128)(2,1)S(1)}, u32[]{:S(2)}, u32[]{:S(2)}) collective-permute-start(bf16[128,1024]{1,0:T(8,128)(2,1)} %get-tuple-element.167), channel_id=1, source_target_pairs={{0,1},{1,0},{2,3},{3,2},{4,5},{5,4},{6,7},{7,6},{8,9},{9,8},{10,11... | collective-permute-start | bytes 786440 | tf_op jit(solution)/shard_map/normed_return/ppermute | solution.py:73
  121.7 21.2 %collective-permute-start.20 = (bf16[128,1024]{1,0:T(8,128)(2,1)}, bf16[128,1024]{1,0:T(8,128)(2,1)S(1)}, u32[]{:S(2)}, u32[]{:S(2)}) collective-permute-start(bf16[128,1024]{1,0:T(8,128)(2,1)} %get-tuple-element.168), channel_id=1, source_target_pairs={{0,2},{1,3},{2,0},{3,1},{4,6},{5,7},{6,4},{7,5},{8,10},{9,11},{10,... | collective-permute-start | bytes 786440 | tf_op jit(solution)/shard_map/normed_return/ppermute | solution.py:73
  121.7 21.2 %collective-permute-start.21 = (bf16[128,1024]{1,0:T(8,128)(2,1)}, bf16[128,1024]{1,0:T(8,128)(2,1)S(1)}, u32[]{:S(2)}, u32[]{:S(2)}) collective-permute-start(bf16[128,1024]{1,0:T(8,128)(2,1)} %get-tuple-element.169), channel_id=1, source_target_pairs={{0,3},{1,2},{2,1},{3,0},{4,7},{5,6},{6,5},{7,4},{8,11},{9,10},{10,... | collective-permute-start | bytes 786440 | tf_op jit(solution)/shard_map/normed_return/ppermute | solution.py:73
  145.0 14.1 %collective-permute-start.22 = (bf16[512,1024]{1,0:T(8,128)(2,1)S(1)}, bf16[512,1024]{1,0:T(8,128)(2,1)}, u32[]{:S(2)}, u32[]{:S(2)}) collective-permute-start(bf16[512,1024]{1,0:T(8,128)(2,1)S(1)} %slice.205), channel_id=1, source_target_pairs={{0,4},{4,0},{8,12},{12,8},{16,20},{20,16},{24,28},{28,24},{1,5},{5... | collective-permute-start | bytes 3145736 | tf_op jit(solution)/shard_map/up_grads/ppermute | solution.py:22
  161.8 21.3 %collective-permute-start.26 = (bf16[128,1024]{1,0:T(8,128)(2,1)}, bf16[128,1024]{1,0:T(8,128)(2,1)S(1)}, u32[]{:S(2)}, u32[]{:S(2)}) collective-permute-start(bf16[128,1024]{1,0:T(8,128)(2,1)} %get-tuple-element.302), channel_id=1, source_target_pairs={{0,8},{4,12},{8,0},{12,4},{16,24},{20,28},{24,16},{28,20},{1,9},{5... | collective-permute-start | bytes 786440 | tf_op jit(solution)/shard_map/up_grads/ppermute | solution.py:66
  162.3 20.9 %collective-permute-start.27 = (bf16[128,1024]{1,0:T(8,128)(2,1)}, bf16[128,1024]{1,0:T(8,128)(2,1)S(1)}, u32[]{:S(2)}, u32[]{:S(2)}) collective-permute-start(bf16[128,1024]{1,0:T(8,128)(2,1)} %get-tuple-element.304), channel_id=1, source_target_pairs={{0,16},{4,20},{8,24},{12,28},{16,0},{20,4},{24,8},{28,12},{1,17},{... | collective-permute-start | bytes 786440 | tf_op jit(solution)/shard_map/up_grads/ppermute | solution.py:66
  163.2 20.0 %collective-permute-start.28 = (bf16[128,1024]{1,0:T(8,128)(2,1)S(1)}, bf16[128,1024]{1,0:T(8,128)(2,1)}, u32[]{:S(2)}, u32[]{:S(2)}) collective-permute-start(bf16[128,1024]{1,0:T(8,128)(2,1)S(1)} %get-tuple-element.303), channel_id=1, source_target_pairs={{0,24},{4,28},{8,16},{12,20},{16,8},{20,12},{24,0},{28,4},{1,25},{... | collective-permute-start | bytes 786440 | tf_op jit(solution)/shard_map/up_grads/ppermute | solution.py:66
  165.3 19.8 %collective-permute-start.29 = (bf16[128,1024]{1,0:T(8,128)(2,1)}, bf16[128,1024]{1,0:T(8,128)(2,1)S(1)}, u32[]{:S(2)}, u32[]{:S(2)}) collective-permute-start(bf16[128,1024]{1,0:T(8,128)(2,1)} %get-tuple-element.193), channel_id=1, source_target_pairs={{0,1},{1,0},{2,3},{3,2},{4,5},{5,4},{6,7},{7,6},{8,9},{9,8},{10,11... | collective-permute-start | bytes 786440 | tf_op jit(solution)/shard_map/mlp_return/ppermute | solution.py:73
  167.1 18.1 %collective-permute-start.30 = (bf16[128,1024]{1,0:T(8,128)(2,1)}, bf16[128,1024]{1,0:T(8,128)(2,1)S(1)}, u32[]{:S(2)}, u32[]{:S(2)}) collective-permute-start(bf16[128,1024]{1,0:T(8,128)(2,1)} %get-tuple-element.194), channel_id=1, source_target_pairs={{0,2},{1,3},{2,0},{3,1},{4,6},{5,7},{6,4},{7,5},{8,10},{9,11},{10,... | collective-permute-start | bytes 786440 | tf_op jit(solution)/shard_map/mlp_return/ppermute | solution.py:73
  186.0 16.8 %collective-permute-start.32 = (bf16[256,512]{1,0:T(8,128)(2,1)S(1)}, bf16[256,512]{1,0:T(8,128)(2,1)S(1)}, u32[]{:S(2)}, u32[]{:S(2)}) collective-permute-start(bf16[256,512]{1,0:T(8,128)(2,1)S(1)} %get-tuple-element.301), channel_id=1, source_target_pairs={{0,16},{4,20},{8,24},{12,28},{16,0},{20,4},{24,8},{28,12},{1,17},{... | collective-permute-start | bytes 786440 | tf_op jit(solution)/shard_map/attn_grads/ppermute | solution.py:66
  187.0 15.9 %collective-permute-start.33 = (bf16[256,512]{1,0:T(8,128)(2,1)S(1)}, bf16[256,512]{1,0:T(8,128)(2,1)S(1)}, u32[]{:S(2)}, u32[]{:S(2)}) collective-permute-start(bf16[256,512]{1,0:T(8,128)(2,1)S(1)} %get-tuple-element.300), channel_id=1, source_target_pairs={{0,24},{4,28},{8,16},{12,20},{16,8},{20,12},{24,0},{28,4},{1,25},{... | collective-permute-start | bytes 786440 | tf_op jit(solution)/shard_map/attn_grads/ppermute | solution.py:66
  188.9 14.8 %collective-permute-start.36 = (bf16[128,1024]{1,0:T(8,128)(2,1)S(1)}, bf16[128,1024]{1,0:T(8,128)(2,1)S(1)}, u32[]{:S(2)}, u32[]{:S(2)}) collective-permute-start(bf16[128,1024]{1,0:T(8,128)(2,1)S(1)} %copy-done.43), channel_id=1, source_target_pairs={{0,3},{1,2},{2,1},{3,0},{4,7},{5,6},{6,5},{7,4},{8,11},{9,10},{10,... | collective-permute-start | bytes 786440 | tf_op jit(solution)/shard_map/mlp_return/ppermute | solution.py:73
  205.3 14.5 %collective-permute-start.37 = (bf16[256,512]{1,0:T(8,128)(2,1)}, bf16[256,512]{1,0:T(8,128)(2,1)}, u32[]{:S(2)}, u32[]{:S(2)}) collective-permute-start(bf16[256,512]{1,0:T(8,128)(2,1)} %get-tuple-element.296), channel_id=1, source_target_pairs={{0,8},{4,12},{8,0},{12,4},{16,24},{20,28},{24,16},{28,20},{1,9},{5... | collective-permute-start | bytes 786440 | tf_op jit(solution)/shard_map/attn_grads/ppermute | solution.py:66
  213.5 14.3 %collective-permute-start.40 = (bf16[256,512]{1,0:T(8,128)(2,1)}, bf16[256,512]{1,0:T(8,128)(2,1)}, u32[]{:S(2)}, u32[]{:S(2)}) collective-permute-start(bf16[256,512]{1,0:T(8,128)(2,1)} %add_convert_fusion.3), channel_id=1, source_target_pairs={{0,2},{1,3},{2,0},{3,1},{4,6},{5,7},{6,4},{7,5},{8,10},{9,11},{10,... | collective-permute-start | bytes 786440 | tf_op jit(solution)/shard_map/attn_grads/ppermute | solution.py:32
  (67 other events, 796.4 us)
Sparse Core Ops, SparseCore 0:
  31.5 34.0 all-gather.2
  67.5 27.8 all-gather.4
  145.2 50.5 reduce-scatter.1

commit v3 on v2

--- a/solution.py
+++ b/solution.py
@@ -107,14 +107,13 @@
     return [whole[k * size : (k + 1) * size] for k in range(PLANE)]
 
 
-def reduce_plane(whole):
+def reduce_pieces(pieces):
     if plane_count() == PLANE:
-        size = whole.shape[0] // PLANE
-        total = whole[:size].astype(F32)
+        total = pieces[0].astype(F32)
         for k in range(1, PLANE):
-            total = total + plane(whole[k * size : (k + 1) * size], k).astype(F32)
+            total = total + plane(pieces[k], k).astype(F32)
         return total
-    return scatter_plane(whole).astype(F32)
+    return scatter_plane(jnp.concatenate(pieces, axis=0)).astype(F32)
 
 
 def scatter_plane(whole):
@@ -238,7 +237,7 @@
         mixed[rows, :] = jnp.concatenate(outs, axis=1).astype(BF16)
         return carry
 
-    lax.fori_loop(0, BLOCKS, block, 0)
+    lax.fori_loop(0, BLOCKS, block, 0, unroll=True)
     for k, (near, far_) in enumerate(zip((n0, n1, n2, n3), (f0, f1, f2, f3))):
         cols = slice(k * size, (k + 1) * size)
         part = mm(mixed[:, :half], near[:, 3 * half :], 1, 1)
@@ -277,21 +276,26 @@
         ref[:, cols] = part[(k + 1) * count : (k + 2) * count].astype(BF16)
 
 
-def mlp_forward(place, up_bias, up, down, a0, a1, a2, a3, g0, g1, g2, g3, act_up, grad_pre,
+def shard_block(place, ref, distance, count):
+    return ref[pl.ds(pl.multiple_of((place[AT_SHARD] ^ distance) * count, count), count)]
+
+
+def mlp_forward(place, up_bias, both, a0, a1, a2, a3, grads, act_up, grad_pre,
                 bias_sum, own, s1, s2, s3, act, grad):
     count, width = a0.shape
-    units = up.shape[1]
+    units = both.shape[1] // 2
     tile = min(256, units)
-    for b, (act_ref, grad_ref) in enumerate(zip((a0, a1, a2, a3), (g0, g1, g2, g3))):
+    for b, act_ref in enumerate((a0, a1, a2, a3)):
         act[b * count : (b + 1) * count] = act_ref[...]
-        grad[b * count : (b + 1) * count] = grad_ref[...]
+        grad[b * count : (b + 1) * count] = shard_block(place, grads, b, count)
     bias_sum[...] = jnp.zeros(bias_sum.shape, F32)
     start = place[AT_SHARD] * units
 
     def step(j, carry):
         inner = pl.ds(pl.multiple_of(j * tile, tile), tile)
         whole = pl.ds(pl.multiple_of(start + j * tile, tile), tile)
-        pre = mm(act[...], up[:, inner]) + up_bias[:, whole]
+        second = pl.ds(pl.multiple_of(units + j * tile, tile), tile)
+        pre = mm(act[...], both[:, inner]) + up_bias[:, whole]
         square = pre * pre
         bend = jnp.tanh(GELU_ROOT * (pre + GELU_CUBE * square * pre))
         half_in = 0.5 * (1.0 + bend)
@@ -299,7 +303,7 @@
         slope = half_in + 0.5 * pre * (1.0 - bend * bend) * (
             GELU_ROOT * (1.0 + 3.0 * GELU_CUBE * square)
         )
-        back = mm(grad[...], down[:, inner]) * slope
+        back = mm(grad[...], both[:, second]) * slope
         grad_pre[:, inner] = back.astype(BF16)
         bias_sum[:, whole] = jnp.sum(back, axis=0, keepdims=True)
         return carry
@@ -308,16 +312,16 @@
     size = width // PLANE
     for k in range(PLANE):
         cols = slice(k * size, (k + 1) * size)
-        split_ring(mm(grad_pre[...], up[cols], 1, 1), cols, count, own, s1, s2, s3)
-
-
-def unit_grads(swap, place, act_up, grad_pre, down, a0, a1, a2, a3, g0, g1, g2, g3,
-               g_down, g_up, own, s1, s2, s3, rows):
+        split_ring(mm(grad_pre[...], both[cols, :units], 1, 1), cols, count, own, s1, s2, s3)
+
+
+def unit_grads(swap, place, act_up, grad_pre, both, a0, a1, a2, a3, grads,
+               g_down, g_up, g_up_sent, own, s1, s2, s3, rows):
     count, width = a0.shape
     half_units = g_up.shape[1] // 2
     size = width // PLANE
-    for b, ref in enumerate((g0, g1, g2, g3)):
-        rows[b * count : (b + 1) * count] = ref[...]
+    for b in range(BLOCKS):
+        rows[b * count : (b + 1) * count] = shard_block(place, grads, b, count)
     for side in range(2):
         cols = slice(side * half_units, (side + 1) * half_units)
         g_down[:, cols] = mm(rows[...], act_up[:, cols], 0, 0).astype(BF16)
@@ -329,16 +333,16 @@
             for k in range(PLANE):
                 block = (place[AT_FSDP] ^ (2 * k)) ^ far_core
                 there = pl.ds(pl.multiple_of(block * size, size), size)
-                at = (far_core * PLANE + k) * size
-                g_up[at : at + size] = mm(rows[:, there], grad_pre[...], 0, 0).astype(BF16)
+                part = mm(rows[:, there], grad_pre[...], 0, 0).astype(BF16)
+                (g_up_sent if far_core else g_up)[k * size : (k + 1) * size] = part
     else:
-        for side in range(2):
-            cols = slice(side * half_units, (side + 1) * half_units)
-            g_up[:, cols] = mm(rows[...], grad_pre[:, cols], 0, 0).astype(BF16)
+        for side, out in enumerate((g_up, g_up_sent)):
+            cols = slice(side * width // 2, (side + 1) * width // 2)
+            out[...] = mm(rows[:, cols], grad_pre[...], 0, 0).astype(BF16)
     size = width // PLANE
     for k in range(PLANE):
         cols = slice(k * size, (k + 1) * size)
-        split_ring(mm(act_up[...], down[cols], 1, 1), cols, count, own, s1, s2, s3)
+        split_ring(mm(act_up[...], both[cols, act_up.shape[1] :], 1, 1), cols, count, own, s1, s2, s3)
 
 
 def norm_back(swap, place, vec, hidden, grad_out, own, r1, r2, r3, grad_hidden, low, sums):
@@ -363,7 +367,8 @@
 
 
 def attn_backward(place, qkv, probs, mixed, act, h0, h1, h2, h3, n0, n1, n2, n3, f0, f1, f2, f3,
-                  far_out, near_out, low, bias_sum, grad, grad_mixed):
+                  far0, far1, far2, far3, near0, near1, near2, near3, low, bias_sum, grad,
+                  grad_mixed):
     count, width = h0.shape
     size = width // PLANE
     half = n0.shape[1] // 4
@@ -404,18 +409,20 @@
         return tuple(a + c for a, c in zip(sums, new))
 
     zero = jnp.zeros((1, half), F32)
-    sums = lax.fori_loop(0, BLOCKS, block, (zero,) * 4)
+    sums = lax.fori_loop(0, BLOCKS, block, (zero,) * 4, unroll=True)
     for side in range(2):
         at = quarter_at(place, half, side == 1)
         bias_sum[0:1, pl.ds(at, half)] = sums[2 * side]
         bias_sum[1:2, pl.ds(at, half)] = sums[2 * side + 1]
-    for side, out in ((1, far_out), (0, near_out)):
-        out[:, : 3 * half] = mm(
-            act[...], low[:, side * 3 * half : (side + 1) * 3 * half], 0, 0
-        ).astype(BF16)
-        out[:, 3 * half :] = mm(
-            grad[...], mixed[:, side * half : (side + 1) * half], 0, 0
-        ).astype(BF16)
+    for side, outs in ((1, (far0, far1, far2, far3)), (0, (near0, near1, near2, near3))):
+        for k, out in enumerate(outs):
+            cols = slice(k * size, (k + 1) * size)
+            out[:, : 3 * half] = mm(
+                act[:, cols], low[:, side * 3 * half : (side + 1) * 3 * half], 0, 0
+            ).astype(BF16)
+            out[:, 3 * half :] = mm(
+                grad[:, cols], mixed[:, side * half : (side + 1) * half], 0, 0
+            ).astype(BF16)
 
 
 def attn_return(place, low, n0, n1, n2, n3, f0, f1, f2, f3, own, kept, sent):
@@ -515,11 +522,12 @@
     grad_natural = cotangent.astype(F32) * live
     grad_low = grad_natural.astype(BF16)
     grad_out = reorder(cotangent).astype(F32) * live
-    grad_low, attn_far, token_low, token_across, packed, place, up, *near = hold(
-        grad_low, attn_far, token_low, token_across, packed, place, w_up, *near
-    )
-    with jax.named_scope("mlp_weights"):
-        up = lax.all_gather(up, "fsdp", axis=0, tiled=True)
+    mlp_piece = jnp.concatenate([w_up, w_down.T], axis=1)
+    grad_low, attn_far, token_low, token_across, packed, place, mlp_piece, *near = hold(
+        grad_low, attn_far, token_low, token_across, packed, place, mlp_piece, *near
+    )
+    with jax.named_scope("grad_rows"):
+        grad_rows = lax.all_gather(grad_low, "shard", axis=0, tiled=True)
     with jax.named_scope("attn_weights"):
         away = gather_pieces(attn_far)
     with jax.named_scope("token_rows"):
@@ -531,16 +539,12 @@
         vec = jnp.transpose(grid[:, :, :8, :size], (2, 1, 0, 3)).reshape(8, -1).astype(F32)
         size = up_bias.shape[1]
         up_vec = jnp.transpose(grid[:, :, 8, :size], (1, 0, 2)).reshape(1, -1).astype(F32)
-    with jax.named_scope("grad_rows"):
-        grad_rows = [grad_low, ring(grad_low, 1), ring(grad_low, 2), None]
-    every, vec, up_vec, down, *held = hold(
-        every, vec, up_vec, w_down.T, *grad_rows[:3], *token_rows, *away
-    )
-    grad_rows, token_rows, away = held[:3], held[3 : 3 + BLOCKS], held[3 + BLOCKS :]
+    every, vec, up_vec, mlp_piece, *held = hold(
+        every, vec, up_vec, mlp_piece, *token_rows, *away
+    )
+    token_rows, away = held[:BLOCKS], held[BLOCKS:]
     with jax.named_scope("mlp_weights"):
-        down = lax.all_gather(down, "fsdp", axis=0, tiled=True)
-    with jax.named_scope("grad_rows"):
-        grad_rows.append(ring(grad_rows[0], 3))
+        both = lax.all_gather(mlp_piece, "fsdp", axis=0, tiled=True)
     block = (slot_count, width)
     parts = [(block, F32), (block, F32), ((2 * slot_count, width), BF16)]
     act, qkv, probs, mixed, *attn_parts = run(
@@ -559,8 +563,6 @@
         *near,
         *away,
     )
-    held = hold(*attn_parts, *grad_rows)
-    attn_parts, grad_rows = held[:3], held[3:]
     with jax.named_scope("attn_return"):
         attn_term = return_blocks(*attn_parts)
     hidden, hidden_natural, mlp_act = run(
@@ -580,28 +582,28 @@
         [((row_count, units), BF16), ((row_count, units), BF16), (up_vec.shape, F32), *ring_parts],
         place,
         up_vec,
-        up,
-        down,
+        both,
         *mlp_rows,
-        *grad_rows,
+        grad_rows,
         scratch=[whole, whole],
     )
     with jax.named_scope("normed_return"):
         grad_normed = return_ring(*normed_parts)
-    g_down, g_up, *mlp_parts = run(
+    half_rows = ((width // 2, units), BF16)
+    g_down, g_up, g_up_sent, *mlp_parts = run(
         functools.partial(unit_grads, swap),
-        [((width, units), BF16)] * 2 + ring_parts,
+        [((width, units), BF16), half_rows, half_rows, *ring_parts],
         place,
         act_up,
         grad_pre,
-        down,
+        both,
         *mlp_rows,
-        *grad_rows,
+        grad_rows,
         scratch=[whole],
     )
     with jax.named_scope("down_grads"):
         g_down_own = lax.psum_scatter(g_down, "fsdp", scatter_dimension=0, tiled=True)
-    g_down, g_up, *held = hold(g_down, g_up, *mlp_parts, *grad_normed)
+    g_down, g_up, g_up_sent, *held = hold(g_down, g_up, g_up_sent, *mlp_parts, *grad_normed)
     mlp_parts, grad_normed = held[:BLOCKS], held[BLOCKS:]
     grad_hidden, hidden_low, sums = run(
         functools.partial(norm_back, swap),
@@ -612,26 +614,26 @@
         grad_out,
         *grad_normed,
     )
-    with jax.named_scope("hidden_rows"):
-        hidden_rows = gather_blocks(hidden_low)
     with jax.named_scope("up_grads"):
         if swap:
-            mid = width // 2
-            g_up_half = (g_up[:mid].astype(F32) + core(g_up[mid:]).astype(F32)).astype(BF16)
+            g_up_half = (g_up.astype(F32) + core(g_up_sent).astype(F32)).astype(BF16)
         else:
-            g_up_half = g_up
-    g_up_half, *hidden_rows = hold(g_up_half, *hidden_rows)
+            g_up_half = jnp.concatenate([g_up, g_up_sent], axis=0)
+    with jax.named_scope("hidden_rows"):
+        across, g_up_half = hold(pair(hidden_low), g_up_half)
+        hidden_rows = [hidden_low, core(hidden_low), across, core(across)]
+    with jax.named_scope("up_grads"):
+        if swap:
+            g_up_parts = [g_up_half[k * rows : (k + 1) * rows] for k in range(PLANE)]
+            g_up_parts = g_up_parts[:1] + [plane(g_up_parts[k], k) for k in range(1, PLANE)]
+        else:
+            g_up_parts = [lax.psum_scatter(g_up_half, "fsdp", scatter_dimension=0, tiled=True)]
     with jax.named_scope("mlp_return"):
         mlp_own, *mlp_others = return_ring(*mlp_parts)
-    with jax.named_scope("up_grads"):
-        if swap:
-            g_up = reduce_plane(g_up_half)
-        else:
-            g_up = lax.psum_scatter(g_up, "fsdp", scatter_dimension=0, tiled=True).astype(F32)
-    side = ((width, 4 * half), BF16)
-    g_attn_far, g_attn_near, low, bias_sum = run(
+    side = ((width // PLANE, 4 * half), BF16)
+    *held, low, bias_sum = run(
         attn_backward,
-        [side, side, ((row_count, 3 * quarter), BF16), ((2, width), F32)],
+        [side] * (2 * PLANE) + [((row_count, 3 * quarter), BF16), ((2, width), F32)],
         place,
         qkv,
         probs,
@@ -642,21 +644,30 @@
         *away,
         scratch=[whole, pltpu.VMEM((row_count, quarter), BF16)],
     )
+    g_attn_far, g_attn_near = held[:PLANE], held[PLANE:]
     back_parts = run(attn_return, parts, place, low, *near, *away)
-    g_attn_far, g_attn_near, g_up, *held = hold(
-        g_attn_far, g_attn_near, g_up, *back_parts, *mlp_others[:2]
-    )
-    back_parts, mlp_others = held[:3], held[3:] + mlp_others[2:]
+    m1, m2, *held = hold(
+        *mlp_others[:2], *back_parts, *g_up_parts, *g_attn_far, *g_attn_near
+    )
+    mlp_others = [m1, m2, *mlp_others[2:]]
+    back_parts, g_up_parts, held = held[:3], held[3 : -2 * PLANE], held[-2 * PLANE :]
+    g_attn_far, g_attn_near = held[:PLANE], held[PLANE:]
     with jax.named_scope("attn_grads"):
-        g_attn_far = reduce_plane(g_attn_far).astype(BF16)
+        g_attn_far = reduce_pieces(g_attn_far).astype(BF16)
     with jax.named_scope("attn_back"):
         grad_attn = return_blocks(*back_parts)
-    g_attn_far, g_attn_near, g_down_own, *held = hold(
-        g_attn_far, g_attn_near, g_down_own, *grad_attn, *mlp_others
-    )
+    g_attn_far, g_down_own, *held = hold(
+        g_attn_far, g_down_own, *g_attn_near, *grad_attn, *mlp_others
+    )
+    g_attn_near, held = held[:PLANE], held[PLANE:]
     grad_attn, mlp_others = held[:3], held[3:]
+    with jax.named_scope("up_grads"):
+        g_up = sum(part.astype(F32) for part in g_up_parts)
     with jax.named_scope("attn_grads"):
-        g_attn_near = reduce_plane(g_attn_near)
+        if swap:
+            near_parts = g_attn_near[:1] + [plane(g_attn_near[k], k) for k in range(1, PLANE)]
+        else:
+            near_parts = [scatter_plane(jnp.concatenate(g_attn_near, axis=0))]
         g_attn_far = far(g_attn_far)
     with jax.named_scope("mlp_return"):
         mlp_term = mlp_own + sum(part.astype(F32) for part in mlp_others)
@@ -677,12 +688,13 @@
         size = up_bias.shape[1]
         upper = jnp.transpose(up_bias_sum.reshape(shard_count, fsdp_count, size), (1, 0, 2))
         small = jnp.concatenate([flat, upper.reshape(devices, size)], axis=1)
-        small, g_attn_near = hold(small, g_attn_near)
+        small, near_parts[-1] = hold(small, near_parts[-1])
         small = jnp.sum(lax.all_to_all(small, ("fsdp", "shard"), 0, 0, tiled=True), axis=0)
         size = attn_gain.shape[1]
         g_vec = small[: 8 * size].reshape(8, 1, size)
         g_up_bias = small[8 * size :].reshape(1, -1)
     with jax.named_scope("attn_grads"):
+        g_attn_near = sum(part.astype(F32) for part in near_parts)
         g_attn = from_rows((g_attn_near + g_attn_far.astype(F32)).astype(BF16), bit).astype(F32)
     g_qkv = jnp.transpose(g_attn[:, :, : 3 * half].reshape(rows, 2, 3, half), (0, 2, 1, 3))
     return (

time: 244 us -> 233 us (0.955)
  starting transfers between devices: 62.3 us -> 55.9 us
  local copies, waits for them, and re-layouts: 16.7 us -> 13.9 us
    ppermute x12 -> x9, starting transfers between devices: 22.2 us -> 14.2 us  [ring(): lax.ppermute(array, 'shard', [(index, index ^ distance) for index in rang...]
    ppermute x15, waiting for transfers between devices: 13.4 us -> 18.8 us  [plane(): lax.ppermute(array, 'fsdp', [(index, index ^ 2 * distance) for index in r...]
    ppermute x12 -> x9, waiting for transfers between devices: 34.2 us -> 29.4 us  [ring(): lax.ppermute(array, 'shard', [(index, index ^ distance) for index in rang...]
    all_to_all x1, waiting for transfers between devices: 1.11 us -> 4.34 us  [on_device(): every = lax.all_to_all(packed, ('fsdp', 'shard'), 0, 0, tiled=True)]
    ppermute x4, waiting for transfers between devices: 23.4 us -> 20.3 us  [pair(): lax.ppermute(array, 'shard', [(index, index ^ 1) for index in range(count)])]
    slice x4 -> x1, local copies, waits for them, and re-layouts: 3.2 us -> 0.07 us  [on_device(): g_up_parts = [g_up_half[k * rows:(k + 1) * rows] for k in range(PLANE)]]
    unnamed x92 -> x86, local copies, waits for them, and re-layouts: 6.4 us -> 6.69 us
  transfers between devices with their start and end apart: 47 -> 44, of which waited for: 17 -> 17; matrix products, arithmetic and copies ran while one was open for 9% -> 8% of each run, Pallas kernels for 18% -> 17%
where the time goes in v3:
time: 233 us; the launch traced here: 232 us
  waiting for transfers between devices  81.1 us (35%)
  starting transfers between devices  55.9 us (24%)
  Pallas kernels  51.8 us (22%)
  between operations  15.2 us (7%)
  other arithmetic  14 us (6%)
  local copies, waits for them, and re-layouts  13.9 us (6%)
    pallas_call x8, Pallas kernels, run(): pl.pallas_call(kernel, out_shape=[jax.ShapeDtypeStruct(shape, kind) for s...  50.3 us
    ppermute x9, waiting for transfers between devices, ring(): lax.ppermute(array, 'shard', [(index, index ^ distance) for index in rang...  29.4 us
    ppermute x4, waiting for transfers between devices, pair(): lax.ppermute(array, 'shard', [(index, index ^ 1) for index in range(count)])  20.3 us
    ppermute x15, waiting for transfers between devices, plane(): lax.ppermute(array, 'fsdp', [(index, index ^ 2 * distance) for index in r...  18.8 us
    ppermute x15, starting transfers between devices, plane(): lax.ppermute(array, 'fsdp', [(index, index ^ 2 * distance) for index in r...  17.9 us
    ppermute x9, starting transfers between devices, ring(): lax.ppermute(array, 'shard', [(index, index ^ distance) for index in rang...  14.2 us
    ppermute x4, starting transfers between devices, pair(): lax.ppermute(array, 'shard', [(index, index ^ 1) for index in range(count)])  8.34 us
    unnamed x86, local copies, waits for them, and re-layouts  6.69 us
  transfers between devices with their start and end apart: 44, of which 17 were waited for; matrix products, arithmetic and copies ran while one was open for 8% of the time, Pallas kernels for 17%

profile of v3, /device:TPU:0, one launch (start us, length us, event | category | flops | bytes accessed | tf_op | source)
XLA Modules:
  0.0 231.9 jit_solution(564310729774357219)
XLA Ops:
  12.9 3.7 %collective-permute-start.1 = (bf16[256,512]{1,0:T(8,128)(2,1)S(1)}, bf16[256,512]{1,0:T(8,128)(2,1)S(1)}, u32[]{:S(2)}, u32[]{:S(2)}) collective-permute-start(bf16[256,512]{1,0:T(8,128)(2,1)S(1)} %maximum_select_fusion.2.n0), channel_id=1, source_target_pairs={{0,2},{1,3},{2,0},{3,1},{4,6},{5,7},{6,4},{7,5},{8,10},{9,11},{10,... | collective-permute-start | bytes 786440 | tf_op jit(solution)/shard_map/attn_weights/ppermute | solution.py:32
  25.0 7.4 %collective-permute-done.2.t2 = bf16[128,1024]{1,0:T(8,128)(2,1)S(1)} collective-permute-done((bf16[128,1024]{1,0:T(8,128)(2,1)S(1)}, bf16[128,1024]{1,0:T(8,128)(2,1)S(1)}, u32[]{:S(2)}, u32[]{:S(2)}) %collective-permute-start.2) | collective-permute-done | bytes 262176 | tf_op jit(solution)/shard_map/token_rows/ppermute | solution.py:27
  32.4 4.7 %all-to-all-start = ((bf16[32,16,128]{2,1,0:T(8,128)(2,1)}), bf16[32,16,128]{2,1,0:T(8,128)(2,1)S(1)}, u32[]{:S(2)}, u32[]{:S(2)}) async-start(bf16[32,16,128]{2,1,0:T(8,128)(2,1)} %pack_rows.1), calls=%async_computation | async-start | bytes 262144 | tf_op jit(solution)/shard_map/vectors/all_to_all | solution.py:536
  37.2 2.7 %collective-permute-start.10 = (bf16[256,512]{1,0:T(8,128)(2,1)S(1)}, bf16[256,512]{1,0:T(8,128)(2,1)S(1)}, u32[]{:S(2)}, u32[]{:S(2)}) collective-permute-start(bf16[256,512]{1,0:T(8,128)(2,1)S(1)} %collective-permute-done.1.f0), channel_id=1, source_target_pairs={{0,24},{4,28},{8,16},{12,20},{16,8},{20,12},{24,0},{28,4},{1,25},{... | collective-permute-start | bytes 786440 | tf_op jit(solution)/shard_map/attn_weights/ppermute | solution.py:66
  41.3 4.3 %all-to-all-done.every = bf16[32,16,128]{2,1,0:T(8,128)(2,1)S(1)} async-done(((bf16[32,16,128]{2,1,0:T(8,128)(2,1)}), bf16[32,16,128]{2,1,0:T(8,128)(2,1)S(1)}, u32[]{:S(2)}, u32[]{:S(2)}) %all-to-all-start) | async-done | bytes 131104 | tf_op jit(solution)/shard_map/vectors/all_to_all | solution.py:536
  48.4 4.9 %collective-permute-done.8.f1 = bf16[256,512]{1,0:T(8,128)(2,1)S(1)} collective-permute-done((bf16[256,512]{1,0:T(8,128)(2,1)S(1)}, bf16[256,512]{1,0:T(8,128)(2,1)S(1)}, u32[]{:S(2)}, u32[]{:S(2)}) %collective-permute-start.8) | collective-permute-done | bytes 262176 | tf_op jit(solution)/shard_map/attn_weights/ppermute | solution.py:66
  54.1 9.4 %attn_forward.1 = (bf16[512,1024]{1,0:T(8,128)(2,1)}, bf16[512,768]{1,0:T(8,128)(2,1)}, f32[4,4,128,128]{3,2,1,0:T(8,128)}, bf16[512,256]{1,0:T(8,128)(2,1)}, f3...) custom-call(s32[4]{0:T(128)} %pad_add_fusion.place, f32[8,1024]{1,0:T(8,128)} %reshape.131.vec, ...), custom_call_target="tpu_custom_call" | custom-call | bytes 10649616 | tf_op jit(solution)/shard_map/attn_forward/pallas_call | solution.py:154
  68.6 6.8 %collective-permute-done.12.across = bf16[128,1024]{1,0:T(8,128)(2,1)S(1)} collective-permute-done((bf16[128,1024]{1,0:T(8,128)(2,1)S(1)}, bf16[128,1024]{1,0:T(8,128)(2,1)S(1)}, u32[]{:S(2)}, u32[]{:S(2)}) %collective-permute-start.12) | collective-permute-done | bytes 262176 | tf_op jit(solution)/shard_map/attn_return/ppermute | solution.py:27
  83.1 8.0 %collective-permute-done.13.a1 = bf16[128,1024]{1,0:T(8,128)(2,1)S(1)} collective-permute-done((bf16[128,1024]{1,0:T(8,128)(2,1)}, bf16[128,1024]{1,0:T(8,128)(2,1)S(1)}, u32[]{:S(2)}, u32[]{:S(2)}) %collective-permute-start.13) | collective-permute-done | bytes 262176 | tf_op jit(solution)/shard_map/mlp_inputs/ppermute | solution.py:73
  91.1 10.7 %collective-permute-done.14.a2 = bf16[128,1024]{1,0:T(8,128)(2,1)S(1)} collective-permute-done((bf16[128,1024]{1,0:T(8,128)(2,1)}, bf16[128,1024]{1,0:T(8,128)(2,1)S(1)}, u32[]{:S(2)}, u32[]{:S(2)}) %collective-permute-start.14) | collective-permute-done | bytes 262176 | tf_op jit(solution)/shard_map/mlp_inputs/ppermute | solution.py:73
  102.6 9.3 %mlp_forward.1 = (bf16[512,1024]{1,0:T(8,128)(2,1)}, bf16[512,1024]{1,0:T(8,128)(2,1)}, f32[1,4096]{1,0:T(1,128)}, f32[128,1024]{1,0:T(8,128)}, bf16[128,1024]{1...) custom-call(s32[4]{0:T(128)} %pad_add_fusion.place, f32[1,4096]{1,0:T(1,128)} %bitcast.87, ...), custom_call_target="tpu_custom_call" | custom-call | bytes 12615696 | tf_op jit(solution)/shard_map/mlp_forward/pallas_call | solution.py:154
  112.0 4.2 %collective-permute-start.16 = (bf16[128,1024]{1,0:T(8,128)(2,1)}, bf16[128,1024]{1,0:T(8,128)(2,1)S(1)}, u32[]{:S(2)}, u32[]{:S(2)}) collective-permute-start(bf16[128,1024]{1,0:T(8,128)(2,1)} %get-tuple-element.165), channel_id=1, source_target_pairs={{0,1},{1,0},{2,3},{3,2},{4,5},{5,4},{6,7},{7,6},{8,9},{9,8},{10,11... | collective-permute-start | bytes 786440 | tf_op jit(solution)/shard_map/normed_return/ppermute | solution.py:73
  118.6 8.2 %unit_grads.1 = (bf16[1024,1024]{1,0:T(8,128)(2,1)}, bf16[512,1024]{1,0:T(8,128)(2,1)}, bf16[512,1024]{1,0:T(8,128)(2,1)}, f32[128,1024]{1,0:T(8,128)}, bf16[128...) custom-call(s32[4]{0:T(128)} %pad_add_fusion.place, ...), custom_call_target="tpu_custom_call" | custom-call | bytes 18874384 | tf_op jit(solution)/shard_map/unit_grads/pallas_call | solution.py:154
  126.9 10.7 %collective-permute-done.17.r2 = bf16[128,1024]{1,0:T(8,128)(2,1)S(1)} collective-permute-done((bf16[128,1024]{1,0:T(8,128)(2,1)}, bf16[128,1024]{1,0:T(8,128)(2,1)S(1)}, u32[]{:S(2)}, u32[]{:S(2)}) %collective-permute-start.17) | collective-permute-done | bytes 262176 | tf_op jit(solution)/shard_map/normed_return/ppermute | solution.py:73
  138.4 3.0 %norm_back.1 = (f32[128,1024]{1,0:T(8,128)}, bf16[128,1024]{1,0:T(8,128)(2,1)}, f32[4,1024]{1,0:T(4,128)}) custom-call(s32[4]{0:T(128)} %pad_add_fusion.place, f32[8,1024]{1,0:T(8,128)} %reshape.131.vec, f32[128,1024]{1,0:T(8,128)} %get-tuple-element.175.hidden, f32[128,1024]{1,0:T(8,128)} %get-tuple-element.350.grad_out, ...), custom_call_target="tpu_custom_call" | custom-call | bytes 3457040 | tf_op jit(solution)/shard_map/norm_back/pallas_call | solution.py:154
  141.4 3.3 %collective-permute-start.22 = (bf16[128,1024]{1,0:T(8,128)(2,1)}, bf16[128,1024]{1,0:T(8,128)(2,1)S(1)}, u32[]{:S(2)}, u32[]{:S(2)}) collective-permute-start(bf16[128,1024]{1,0:T(8,128)(2,1)} %get-tuple-element.180.h0), channel_id=1, source_target_pairs={{0,1},{1,0},{2,3},{3,2},{4,5},{5,4},{6,7},{7,6},{8,9},{9,8},{10,11... | collective-permute-start | bytes 786440 | tf_op jit(solution)/shard_map/hidden_rows/ppermute | solution.py:27
  145.1 6.1 %collective-permute-done.22.h2 = bf16[128,1024]{1,0:T(8,128)(2,1)S(1)} collective-permute-done((bf16[128,1024]{1,0:T(8,128)(2,1)}, bf16[128,1024]{1,0:T(8,128)(2,1)S(1)}, u32[]{:S(2)}, u32[]{:S(2)}) %collective-permute-start.22) | collective-permute-done | bytes 262176 | tf_op jit(solution)/shard_map/hidden_rows/ppermute | solution.py:27
  157.8 10.6 %attn_backward.1 = (bf16[256,512]{1,0:T(8,128)(2,1)}, bf16[256,512]{1,0:T(8,128)(2,1)}, bf16[256,512]{1,0:T(8,128)(2,1)}, bf16[256,512]{1,0:T(8,128)(2,1)}, bf16...) custom-call(s32[4]{0:T(128)} %pad_add_fusion.place, ...), custom_call_target="tpu_custom_call" | custom-call | bytes 12066832 | tf_op jit(solution)/shard_map/attn_backward/pallas_call | solution.py:154
  168.4 4.2 %attn_return.1 = (f32[128,1024]{1,0:T(8,128)}, f32[128,1024]{1,0:T(8,128)}, bf16[256,1024]{1,0:T(8,128)(2,1)}) custom-call(s32[4]{0:T(128)} %pad_add_fusion.place, bf16[512,768]{1,0:T(8,128)(2,1)} %get-tuple-element.184.low, bf16[256,512]{1,0:T(8,128)(2,1)} %copy-done, bf16[256,512]{1,0:T(8,128)(2,1)} %copy-done.3, bf16[256,512]{1,0:T(8,128)(2,1)} %copy-done.4, ...), custom_call_target="tpu_custom_call" | custom-call | bytes 4980752 | tf_op jit(solution)/shard_map/attn_return/pallas_call | solution.py:154
  184.4 3.4 %collective-permute-done.28 = bf16[256,512]{1,0:T(8,128)(2,1)S(1)} collective-permute-done((bf16[256,512]{1,0:T(8,128)(2,1)}, bf16[256,512]{1,0:T(8,128)(2,1)S(1)}, u32[]{:S(2)}, u32[]{:S(2)}) %collective-permute-start.28) | collective-permute-done | bytes 262176 | tf_op jit(solution)/shard_map/attn_grads/ppermute | solution.py:66
  187.7 6.7 %collective-permute-done.29 = bf16[256,512]{1,0:T(8,128)(2,1)S(1)} collective-permute-done((bf16[256,512]{1,0:T(8,128)(2,1)}, bf16[256,512]{1,0:T(8,128)(2,1)S(1)}, u32[]{:S(2)}, u32[]{:S(2)}) %collective-permute-start.29) | collective-permute-done | bytes 262176 | tf_op jit(solution)/shard_map/attn_grads/ppermute | solution.py:66
  195.3 2.8 %input_back.1 = (f32[128,1024]{1,0:T(8,128)}, f32[2,1024]{1,0:T(2,128)}) custom-call(s32[4]{0:T(128)} %pad_add_fusion.place, f32[8,1024]{1,0:T(8,128)} %reshape.131.vec, bf16[128,1024]{1,0:T(8,128)(2,1)} %copy-done.1, f32[128,1024]{1,0:T(8,128)} %get-tuple-element.214.grad_hidden, f32[128,1024]{1,0:T(8,128)} %get-tuple-element.215.own, ...), custom_call_target="tpu_custom_call" | custom-call | bytes 2662416 | tf_op jit(solution)/shard_map/input_back/pallas_call | solution.py:154
  211.2 3.7 %all-to-all-start.1 = ((f32[32,1,384]{2,1,0:T(1,128)}), f32[32,1,384]{2,1,0:T(1,128)S(1)}, u32[]{:S(2)}, u32[]{:S(2)}) async-start(f32[32,1,384]{2,1,0:T(1,128)} %copy.83), calls=%async_computation.2 | async-start | bytes 98304 | tf_op jit(solution)/shard_map/small_grads/all_to_all | solution.py:692
  218.3 4.0 %all-to-all-done.1 = f32[32,1,384]{2,1,0:T(1,128)S(1)} async-done(((f32[32,1,384]{2,1,0:T(1,128)}), f32[32,1,384]{2,1,0:T(1,128)S(1)}, u32[]{:S(2)}, u32[]{:S(2)}) %all-to-all-start.1) | async-done | bytes 49184 | tf_op jit(solution)/shard_map/small_grads/all_to_all | solution.py:692
  (218 shorter events, 73.7 us)
Async XLA Ops:
  7.2 94.7 %all-gather.5.cloned.1.call-start = ((), (), s32[]{:S(2)}) async-start(), calls=%async_computation.4 | async-start | bytes 1310720 | tf_op jit(solution)/shard_map/grad_rows/all_gather | solution.py:530
  12.9 19.5 %collective-permute-start.1 = (bf16[256,512]{1,0:T(8,128)(2,1)S(1)}, bf16[256,512]{1,0:T(8,128)(2,1)S(1)}, u32[]{:S(2)}, u32[]{:S(2)}) collective-permute-start(bf16[256,512]{1,0:T(8,128)(2,1)S(1)} %maximum_select_fusion.2.n0), channel_id=1, source_target_pairs={{0,2},{1,3},{2,0},{3,1},{4,6},{5,7},{6,4},{7,5},{8,10},{9,11},{10,... | collective-permute-start | bytes 786440 | tf_op jit(solution)/shard_map/attn_weights/ppermute | solution.py:32
  16.6 15.8 %collective-permute-start.3 = (bf16[256,512]{1,0:T(8,128)(2,1)S(1)}, bf16[256,512]{1,0:T(8,128)(2,1)S(1)}, u32[]{:S(2)}, u32[]{:S(2)}) collective-permute-start(bf16[256,512]{1,0:T(8,128)(2,1)S(1)} %maximum_select_fusion.2.n0), channel_id=1, source_target_pairs={{0,8},{4,12},{8,0},{12,4},{16,24},{20,28},{24,16},{28,20},{1,9},{5... | collective-permute-start | bytes 786440 | tf_op jit(solution)/shard_map/attn_weights/ppermute | solution.py:66
  18.1 14.3 %collective-permute-start.4 = (bf16[256,512]{1,0:T(8,128)(2,1)S(1)}, bf16[256,512]{1,0:T(8,128)(2,1)S(1)}, u32[]{:S(2)}, u32[]{:S(2)}) collective-permute-start(bf16[256,512]{1,0:T(8,128)(2,1)S(1)} %maximum_select_fusion.2.n0), channel_id=1, source_target_pairs={{0,16},{4,20},{8,24},{12,28},{16,0},{20,4},{24,8},{28,12},{1,17},{... | collective-permute-start | bytes 786440 | tf_op jit(solution)/shard_map/attn_weights/ppermute | solution.py:66
  32.4 13.2 %all-to-all-start = ((bf16[32,16,128]{2,1,0:T(8,128)(2,1)}), bf16[32,16,128]{2,1,0:T(8,128)(2,1)S(1)}, u32[]{:S(2)}, u32[]{:S(2)}) async-start(bf16[32,16,128]{2,1,0:T(8,128)(2,1)} %pack_rows.1), calls=%async_computation | async-start | bytes 262144 | tf_op jit(solution)/shard_map/vectors/all_to_all | solution.py:536
  37.1 64.7 %all-gather.3.cloned.1.call-start = ((), (), s32[]{:S(2)}) async-start(), calls=%async_computation.3 | async-start | bytes 4718592 | tf_op jit(solution)/shard_map/mlp_weights/all_gather | solution.py:547
  39.9 13.4 %collective-permute-start.8 = (bf16[256,512]{1,0:T(8,128)(2,1)S(1)}, bf16[256,512]{1,0:T(8,128)(2,1)S(1)}, u32[]{:S(2)}, u32[]{:S(2)}) collective-permute-start(bf16[256,512]{1,0:T(8,128)(2,1)S(1)} %collective-permute-done.1.f0), channel_id=1, source_target_pairs={{0,8},{4,12},{8,0},{12,4},{16,24},{20,28},{24,16},{28,20},{1,9},{5... | collective-permute-start | bytes 786440 | tf_op jit(solution)/shard_map/attn_weights/ppermute | solution.py:66
  53.5 141.2 %reduce-scatter.2.cloned.1.call-start = ((), (), s32[]{:S(2)}) async-start(), calls=%async_computation.5 | async-start | bytes 2359296 | tf_op jit(solution)/shard_map/down_grads/reduce_scatter | solution.py:605
  80.3 21.6 %collective-permute-start.14 = (bf16[128,1024]{1,0:T(8,128)(2,1)}, bf16[128,1024]{1,0:T(8,128)(2,1)S(1)}, u32[]{:S(2)}, u32[]{:S(2)}) collective-permute-start(bf16[128,1024]{1,0:T(8,128)(2,1)} %get-tuple-element.153.a0), channel_id=1, source_target_pairs={{0,2},{1,3},{2,0},{3,1},{4,6},{5,7},{6,4},{7,5},{8,10},{9,11},{10,... | collective-permute-start | bytes 786440 | tf_op jit(solution)/shard_map/mlp_inputs/ppermute | solution.py:73
  82.6 19.2 %collective-permute-start.15 = (bf16[128,1024]{1,0:T(8,128)(2,1)}, bf16[128,1024]{1,0:T(8,128)(2,1)S(1)}, u32[]{:S(2)}, u32[]{:S(2)}) collective-permute-start(bf16[128,1024]{1,0:T(8,128)(2,1)} %get-tuple-element.153.a0), channel_id=1, source_target_pairs={{0,3},{1,2},{2,1},{3,0},{4,7},{5,6},{6,5},{7,4},{8,11},{9,10},{10,... | collective-permute-start | bytes 786440 | tf_op jit(solution)/shard_map/mlp_inputs/ppermute | solution.py:73
  112.0 14.9 %collective-permute-start.16 = (bf16[128,1024]{1,0:T(8,128)(2,1)}, bf16[128,1024]{1,0:T(8,128)(2,1)S(1)}, u32[]{:S(2)}, u32[]{:S(2)}) collective-permute-start(bf16[128,1024]{1,0:T(8,128)(2,1)} %get-tuple-element.165), channel_id=1, source_target_pairs={{0,1},{1,0},{2,3},{3,2},{4,5},{5,4},{6,7},{7,6},{8,9},{9,8},{10,11... | collective-permute-start | bytes 786440 | tf_op jit(solution)/shard_map/normed_return/ppermute | solution.py:73
  116.2 21.3 %collective-permute-start.17 = (bf16[128,1024]{1,0:T(8,128)(2,1)}, bf16[128,1024]{1,0:T(8,128)(2,1)S(1)}, u32[]{:S(2)}, u32[]{:S(2)}) collective-permute-start(bf16[128,1024]{1,0:T(8,128)(2,1)} %get-tuple-element.166), channel_id=1, source_target_pairs={{0,2},{1,3},{2,0},{3,1},{4,6},{5,7},{6,4},{7,5},{8,10},{9,11},{10,... | collective-permute-start | bytes 786440 | tf_op jit(solution)/shard_map/normed_return/ppermute | solution.py:73
  117.0 20.5 %collective-permute-start.18 = (bf16[128,1024]{1,0:T(8,128)(2,1)}, bf16[128,1024]{1,0:T(8,128)(2,1)S(1)}, u32[]{:S(2)}, u32[]{:S(2)}) collective-permute-start(bf16[128,1024]{1,0:T(8,128)(2,1)} %get-tuple-element.167), channel_id=1, source_target_pairs={{0,3},{1,2},{2,1},{3,0},{4,7},{5,6},{6,5},{7,4},{8,11},{9,10},{10,... | collective-permute-start | bytes 786440 | tf_op jit(solution)/shard_map/normed_return/ppermute | solution.py:73
  151.3 21.3 %collective-permute-start.19 = (bf16[128,1024]{1,0:T(8,128)(2,1)}, bf16[128,1024]{1,0:T(8,128)(2,1)S(1)}, u32[]{:S(2)}, u32[]{:S(2)}) collective-permute-start(bf16[128,1024]{1,0:T(8,128)(2,1)} %get-tuple-element.169), channel_id=1, source_target_pairs={{0,1},{1,0},{2,3},{3,2},{4,5},{5,4},{6,7},{7,6},{8,9},{9,8},{10,11... | collective-permute-start | bytes 786440 | tf_op jit(solution)/shard_map/mlp_return/ppermute | solution.py:73
  153.0 19.6 %collective-permute-start.20 = (bf16[128,1024]{1,0:T(8,128)(2,1)}, bf16[128,1024]{1,0:T(8,128)(2,1)S(1)}, u32[]{:S(2)}, u32[]{:S(2)}) collective-permute-start(bf16[128,1024]{1,0:T(8,128)(2,1)} %get-tuple-element.170), channel_id=1, source_target_pairs={{0,2},{1,3},{2,0},{3,1},{4,6},{5,7},{6,4},{7,5},{8,10},{9,11},{10,... | collective-permute-start | bytes 786440 | tf_op jit(solution)/shard_map/mlp_return/ppermute | solution.py:73
  154.2 18.4 %collective-permute-start.25 = (bf16[128,1024]{1,0:T(8,128)(2,1)S(1)}, bf16[128,1024]{1,0:T(8,128)(2,1)S(1)}, u32[]{:S(2)}, u32[]{:S(2)}) collective-permute-start(bf16[128,1024]{1,0:T(8,128)(2,1)S(1)} %get-tuple-element.312), channel_id=1, source_target_pairs={{0,8},{4,12},{8,0},{12,4},{16,24},{20,28},{24,16},{28,20},{1,9},{5... | collective-permute-start | bytes 786440 | tf_op jit(solution)/shard_map/up_grads/ppermute | solution.py:66
  155.5 17.1 %collective-permute-start.26 = (bf16[128,1024]{1,0:T(8,128)(2,1)S(1)}, bf16[128,1024]{1,0:T(8,128)(2,1)S(1)}, u32[]{:S(2)}, u32[]{:S(2)}) collective-permute-start(bf16[128,1024]{1,0:T(8,128)(2,1)S(1)} %get-tuple-element.311), channel_id=1, source_target_pairs={{0,16},{4,20},{8,24},{12,28},{16,0},{20,4},{24,8},{28,12},{1,17},{... | collective-permute-start | bytes 786440 | tf_op jit(solution)/shard_map/up_grads/ppermute | solution.py:66
  156.7 17.5 %collective-permute-start.27 = (bf16[128,1024]{1,0:T(8,128)(2,1)S(1)}, bf16[128,1024]{1,0:T(8,128)(2,1)}, u32[]{:S(2)}, u32[]{:S(2)}) collective-permute-start(bf16[128,1024]{1,0:T(8,128)(2,1)S(1)} %get-tuple-element.310), channel_id=1, source_target_pairs={{0,24},{4,28},{8,16},{12,20},{16,8},{20,12},{24,0},{28,4},{1,25},{... | collective-permute-start | bytes 786440 | tf_op jit(solution)/shard_map/up_grads/ppermute | solution.py:66
  175.0 19.6 %collective-permute-start.33 = (bf16[128,1024]{1,0:T(8,128)(2,1)}, bf16[128,1024]{1,0:T(8,128)(2,1)S(1)}, u32[]{:S(2)}, u32[]{:S(2)}) collective-permute-start(bf16[128,1024]{1,0:T(8,128)(2,1)} %get-tuple-element.210), channel_id=1, source_target_pairs={{0,3},{1,2},{2,1},{3,0},{4,7},{5,6},{6,5},{7,4},{8,11},{9,10},{10,... | collective-permute-start | bytes 786440 | tf_op jit(solution)/shard_map/mlp_return/ppermute | solution.py:73
  177.7 16.8 %collective-permute-start.29 = (bf16[256,512]{1,0:T(8,128)(2,1)}, bf16[256,512]{1,0:T(8,128)(2,1)S(1)}, u32[]{:S(2)}, u32[]{:S(2)}) collective-permute-start(bf16[256,512]{1,0:T(8,128)(2,1)} %get-tuple-element.199), channel_id=1, source_target_pairs={{0,16},{4,20},{8,24},{12,28},{16,0},{20,4},{24,8},{28,12},{1,17},{... | collective-permute-start | bytes 786440 | tf_op jit(solution)/shard_map/attn_grads/ppermute | solution.py:66
  179.1 15.3 %collective-permute-start.30 = (bf16[256,512]{1,0:T(8,128)(2,1)S(1)}, bf16[256,512]{1,0:T(8,128)(2,1)S(1)}, u32[]{:S(2)}, u32[]{:S(2)}) collective-permute-start(bf16[256,512]{1,0:T(8,128)(2,1)S(1)} %copy-done.40), channel_id=1, source_target_pairs={{0,24},{4,28},{8,16},{12,20},{16,8},{20,12},{24,0},{28,4},{1,25},{... | collective-permute-start | bytes 786440 | tf_op jit(solution)/shard_map/attn_grads/ppermute | solution.py:66
  180.5 14.2 %collective-permute-start.32 = (bf16[128,1024]{1,0:T(8,128)(2,1)S(1)}, bf16[128,1024]{1,0:T(8,128)(2,1)S(1)}, u32[]{:S(2)}, u32[]{:S(2)}) collective-permute-start(bf16[128,1024]{1,0:T(8,128)(2,1)S(1)} %add_convert_fusion.2), channel_id=1, source_target_pairs={{0,1},{1,0},{2,3},{3,2},{4,5},{5,4},{6,7},{7,6},{8,9},{9,8},{10,11... | collective-permute-start | bytes 786440 | tf_op jit(solution)/shard_map/attn_back/ppermute | solution.py:27
  201.3 13.5 %collective-permute-start.35 = (bf16[256,512]{1,0:T(8,128)(2,1)}, bf16[256,512]{1,0:T(8,128)(2,1)S(1)}, u32[]{:S(2)}, u32[]{:S(2)}) collective-permute-start(bf16[256,512]{1,0:T(8,128)(2,1)} %get-tuple-element.226), channel_id=1, source_target_pairs={{0,8},{4,12},{8,0},{12,4},{16,24},{20,28},{24,16},{28,20},{1,9},{5... | collective-permute-start | bytes 786440 | tf_op jit(solution)/shard_map/attn_grads/ppermute | solution.py:66
  203.6 13.4 %collective-permute-start.37 = (bf16[256,512]{1,0:T(8,128)(2,1)S(1)}, bf16[256,512]{1,0:T(8,128)(2,1)}, u32[]{:S(2)}, u32[]{:S(2)}) collective-permute-start(bf16[256,512]{1,0:T(8,128)(2,1)S(1)} %add_convert_fusion.3), channel_id=1, source_target_pairs={{0,2},{1,3},{2,0},{3,1},{4,6},{5,7},{6,4},{7,5},{8,10},{9,11},{10,... | collective-permute-start | bytes 786440 | tf_op jit(solution)/shard_map/attn_grads/ppermute | solution.py:32
  (61 other events, 548.1 us)
Sparse Core Ops, SparseCore 0:
  32.6 28.0 all-gather.4
  62.5 36.1 all-gather.2
  137.8 50.3 reduce-scatter.1

commit v4 on v3

--- a/solution.py
+++ b/solution.py
@@ -616,18 +616,21 @@
     )
     with jax.named_scope("up_grads"):
         if swap:
-            g_up_half = (g_up.astype(F32) + core(g_up_sent).astype(F32)).astype(BF16)
+            others = core(g_up_sent)
+            g_up_half = []
+            for k in range(PLANE):
+                piece = slice(k * rows, (k + 1) * rows)
+                g_up_half.append((g_up[piece].astype(F32) + others[piece].astype(F32)).astype(BF16))
         else:
-            g_up_half = jnp.concatenate([g_up, g_up_sent], axis=0)
+            g_up_half = [jnp.concatenate([g_up, g_up_sent], axis=0)]
     with jax.named_scope("hidden_rows"):
-        across, g_up_half = hold(pair(hidden_low), g_up_half)
+        across, *g_up_half = hold(pair(hidden_low), *g_up_half)
         hidden_rows = [hidden_low, core(hidden_low), across, core(across)]
     with jax.named_scope("up_grads"):
         if swap:
-            g_up_parts = [g_up_half[k * rows : (k + 1) * rows] for k in range(PLANE)]
-            g_up_parts = g_up_parts[:1] + [plane(g_up_parts[k], k) for k in range(1, PLANE)]
+            g_up_parts = g_up_half[:1] + [plane(g_up_half[k], k) for k in range(1, PLANE)]
         else:
-            g_up_parts = [lax.psum_scatter(g_up_half, "fsdp", scatter_dimension=0, tiled=True)]
+            g_up_parts = [lax.psum_scatter(g_up_half[0], "fsdp", scatter_dimension=0, tiled=True)]
     with jax.named_scope("mlp_return"):
         mlp_own, *mlp_others = return_ring(*mlp_parts)
     side = ((width // PLANE, 4 * half), BF16)
@@ -657,10 +660,10 @@
     with jax.named_scope("attn_back"):
         grad_attn = return_blocks(*back_parts)
     g_attn_far, g_down_own, *held = hold(
-        g_attn_far, g_down_own, *g_attn_near, *grad_attn, *mlp_others
+        g_attn_far, g_down_own, *g_attn_near, *grad_attn, *mlp_others[:2]
     )
     g_attn_near, held = held[:PLANE], held[PLANE:]
-    grad_attn, mlp_others = held[:3], held[3:]
+    grad_attn, mlp_others = held[:3], [*held[3:], mlp_others[2]]
     with jax.named_scope("up_grads"):
         g_up = sum(part.astype(F32) for part in g_up_parts)
     with jax.named_scope("attn_grads"):

time: 233 us -> 231 us (level)
  other arithmetic: 14 us -> 18.6 us
  waiting for transfers between devices: 81.1 us -> 76.6 us
  starting transfers between devices: 55.9 us -> 53.4 us
    ppermute x15, waiting for transfers between devices: 18.8 us -> 15.3 us  [plane(): lax.ppermute(array, 'fsdp', [(index, index ^ 2 * distance) for index in r...]
    unnamed x86 -> x76, local copies, waits for them, and re-layouts: 6.69 us -> 7.59 us
  transfers between devices with their start and end apart: 44 -> 44, of which waited for: 17 -> 15; matrix products, arithmetic and copies ran while one was open for 8% -> 11% of each run, Pallas kernels for 17% -> 18%
where the time goes in v4:
time: 231 us; the launch traced here: 230 us
  waiting for transfers between devices  76.6 us (33%)
  starting transfers between devices  53.4 us (23%)
  Pallas kernels  51.6 us (22%)
  other arithmetic  18.6 us (8%)
  between operations  15.1 us (7%)
  local copies, waits for them, and re-layouts  14.6 us (6%)
    pallas_call x8, Pallas kernels, run(): pl.pallas_call(kernel, out_shape=[jax.ShapeDtypeStruct(shape, kind) for s...  50.1 us
    ppermute x9, waiting for transfers between devices, ring(): lax.ppermute(array, 'shard', [(index, index ^ distance) for index in rang...  29.4 us
    ppermute x4, waiting for transfers between devices, pair(): lax.ppermute(array, 'shard', [(index, index ^ 1) for index in range(count)])  19.5 us
    ppermute x15, starting transfers between devices, plane(): lax.ppermute(array, 'fsdp', [(index, index ^ 2 * distance) for index in r...  17.6 us
    ppermute x9, starting transfers between devices, ring(): lax.ppermute(array, 'shard', [(index, index ^ distance) for index in rang...  15.5 us
    ppermute x15, waiting for transfers between devices, plane(): lax.ppermute(array, 'fsdp', [(index, index ^ 2 * distance) for index in r...  15.3 us
    unnamed x76, local copies, waits for them, and re-layouts  7.59 us
    ppermute x4, starting transfers between devices, pair(): lax.ppermute(array, 'shard', [(index, index ^ 1) for index in range(count)])  7.41 us
  transfers between devices with their start and end apart: 44, of which 15 were waited for; matrix products, arithmetic and copies ran while one was open for 11% of the time, Pallas kernels for 18%

profile of v4, /device:TPU:0, one launch (start us, length us, event | category | flops | bytes accessed | tf_op | source)
XLA Modules:
  0.0 229.8 jit_solution(3954266067801691264)
XLA Ops:
  15.6 3.7 %collective-permute-start.1 = (bf16[256,512]{1,0:T(8,128)(2,1)S(1)}, bf16[256,512]{1,0:T(8,128)(2,1)S(1)}, u32[]{:S(2)}, u32[]{:S(2)}) collective-permute-start(bf16[256,512]{1,0:T(8,128)(2,1)S(1)} %maximum_select_fusion.2.n0), channel_id=1, source_target_pairs={{0,2},{1,3},{2,0},{3,1},{4,6},{5,7},{6,4},{7,5},{8,10},{9,11},{10,... | collective-permute-start | bytes 786440 | tf_op jit(solution)/shard_map/attn_weights/ppermute | solution.py:32
  27.7 7.4 %collective-permute-done.2.t2 = bf16[128,1024]{1,0:T(8,128)(2,1)S(1)} collective-permute-done((bf16[128,1024]{1,0:T(8,128)(2,1)S(1)}, bf16[128,1024]{1,0:T(8,128)(2,1)S(1)}, u32[]{:S(2)}, u32[]{:S(2)}) %collective-permute-start.2) | collective-permute-done | bytes 262176 | tf_op jit(solution)/shard_map/token_rows/ppermute | solution.py:27
  35.2 3.8 %all-to-all-start = ((bf16[32,16,128]{2,1,0:T(8,128)(2,1)}), bf16[32,16,128]{2,1,0:T(8,128)(2,1)S(1)}, u32[]{:S(2)}, u32[]{:S(2)}) async-start(bf16[32,16,128]{2,1,0:T(8,128)(2,1)} %pack_rows.1), calls=%async_computation | async-start | bytes 262144 | tf_op jit(solution)/shard_map/vectors/all_to_all | solution.py:536
  39.0 2.7 %collective-permute-start.10 = (bf16[256,512]{1,0:T(8,128)(2,1)S(1)}, bf16[256,512]{1,0:T(8,128)(2,1)S(1)}, u32[]{:S(2)}, u32[]{:S(2)}) collective-permute-start(bf16[256,512]{1,0:T(8,128)(2,1)S(1)} %collective-permute-done.1.f0), channel_id=1, source_target_pairs={{0,24},{4,28},{8,16},{12,20},{16,8},{20,12},{24,0},{28,4},{1,25},{... | collective-permute-start | bytes 786440 | tf_op jit(solution)/shard_map/attn_weights/ppermute | solution.py:66
  43.1 4.3 %all-to-all-done.every = bf16[32,16,128]{2,1,0:T(8,128)(2,1)S(1)} async-done(((bf16[32,16,128]{2,1,0:T(8,128)(2,1)}), bf16[32,16,128]{2,1,0:T(8,128)(2,1)S(1)}, u32[]{:S(2)}, u32[]{:S(2)}) %all-to-all-start) | async-done | bytes 131104 | tf_op jit(solution)/shard_map/vectors/all_to_all | solution.py:536
  50.3 4.9 %collective-permute-done.8.f1 = bf16[256,512]{1,0:T(8,128)(2,1)S(1)} collective-permute-done((bf16[256,512]{1,0:T(8,128)(2,1)S(1)}, bf16[256,512]{1,0:T(8,128)(2,1)S(1)}, u32[]{:S(2)}, u32[]{:S(2)}) %collective-permute-start.8) | collective-permute-done | bytes 262176 | tf_op jit(solution)/shard_map/attn_weights/ppermute | solution.py:66
  56.0 9.4 %attn_forward.1 = (bf16[512,1024]{1,0:T(8,128)(2,1)}, bf16[512,768]{1,0:T(8,128)(2,1)}, f32[4,4,128,128]{3,2,1,0:T(8,128)}, bf16[512,256]{1,0:T(8,128)(2,1)}, f3...) custom-call(s32[4]{0:T(128)} %pad_add_fusion.place, f32[8,1024]{1,0:T(8,128)} %reshape.131.vec, ...), custom_call_target="tpu_custom_call" | custom-call | bytes 10649616 | tf_op jit(solution)/shard_map/attn_forward/pallas_call | solution.py:154
  70.5 6.8 %collective-permute-done.12.across = bf16[128,1024]{1,0:T(8,128)(2,1)S(1)} collective-permute-done((bf16[128,1024]{1,0:T(8,128)(2,1)S(1)}, bf16[128,1024]{1,0:T(8,128)(2,1)S(1)}, u32[]{:S(2)}, u32[]{:S(2)}) %collective-permute-start.12) | collective-permute-done | bytes 262176 | tf_op jit(solution)/shard_map/attn_return/ppermute | solution.py:27
  84.9 8.0 %collective-permute-done.13.a1 = bf16[128,1024]{1,0:T(8,128)(2,1)S(1)} collective-permute-done((bf16[128,1024]{1,0:T(8,128)(2,1)}, bf16[128,1024]{1,0:T(8,128)(2,1)S(1)}, u32[]{:S(2)}, u32[]{:S(2)}) %collective-permute-start.13) | collective-permute-done | bytes 262176 | tf_op jit(solution)/shard_map/mlp_inputs/ppermute | solution.py:73
  92.9 10.8 %collective-permute-done.14.a2 = bf16[128,1024]{1,0:T(8,128)(2,1)S(1)} collective-permute-done((bf16[128,1024]{1,0:T(8,128)(2,1)}, bf16[128,1024]{1,0:T(8,128)(2,1)S(1)}, u32[]{:S(2)}, u32[]{:S(2)}) %collective-permute-start.14) | collective-permute-done | bytes 262176 | tf_op jit(solution)/shard_map/mlp_inputs/ppermute | solution.py:73
  104.5 9.4 %mlp_forward.1 = (bf16[512,1024]{1,0:T(8,128)(2,1)}, bf16[512,1024]{1,0:T(8,128)(2,1)}, f32[1,4096]{1,0:T(1,128)}, f32[128,1024]{1,0:T(8,128)}, bf16[128,1024]{1...) custom-call(s32[4]{0:T(128)} %pad_add_fusion.place, f32[1,4096]{1,0:T(1,128)} %bitcast.87, ...), custom_call_target="tpu_custom_call" | custom-call | bytes 12615696 | tf_op jit(solution)/shard_map/mlp_forward/pallas_call | solution.py:154
  113.8 4.2 %collective-permute-start.16 = (bf16[128,1024]{1,0:T(8,128)(2,1)}, bf16[128,1024]{1,0:T(8,128)(2,1)S(1)}, u32[]{:S(2)}, u32[]{:S(2)}) collective-permute-start(bf16[128,1024]{1,0:T(8,128)(2,1)} %get-tuple-element.167), channel_id=1, source_target_pairs={{0,1},{1,0},{2,3},{3,2},{4,5},{5,4},{6,7},{7,6},{8,9},{9,8},{10,11... | collective-permute-start | bytes 786440 | tf_op jit(solution)/shard_map/normed_return/ppermute | solution.py:73
  120.4 8.2 %unit_grads.1 = (bf16[1024,1024]{1,0:T(8,128)(2,1)}, bf16[512,1024]{1,0:T(8,128)(2,1)}, bf16[512,1024]{1,0:T(8,128)(2,1)}, f32[128,1024]{1,0:T(8,128)}, bf16[128...) custom-call(s32[4]{0:T(128)} %pad_add_fusion.place, ...), custom_call_target="tpu_custom_call" | custom-call | bytes 18874384 | tf_op jit(solution)/shard_map/unit_grads/pallas_call | solution.py:154
  128.7 10.7 %collective-permute-done.17.r2 = bf16[128,1024]{1,0:T(8,128)(2,1)S(1)} collective-permute-done((bf16[128,1024]{1,0:T(8,128)(2,1)}, bf16[128,1024]{1,0:T(8,128)(2,1)S(1)}, u32[]{:S(2)}, u32[]{:S(2)}) %collective-permute-start.17) | collective-permute-done | bytes 262176 | tf_op jit(solution)/shard_map/normed_return/ppermute | solution.py:73
  140.2 3.1 %norm_back.1 = (f32[128,1024]{1,0:T(8,128)}, bf16[128,1024]{1,0:T(8,128)(2,1)}, f32[4,1024]{1,0:T(4,128)}) custom-call(s32[4]{0:T(128)} %pad_add_fusion.place, f32[8,1024]{1,0:T(8,128)} %reshape.131.vec, f32[128,1024]{1,0:T(8,128)} %get-tuple-element.177.hidden, f32[128,1024]{1,0:T(8,128)} %get-tuple-element.354.grad_out, ...), custom_call_target="tpu_custom_call" | custom-call | bytes 3457040 | tf_op jit(solution)/shard_map/norm_back/pallas_call | solution.py:154
  143.3 3.3 %collective-permute-start.22 = (bf16[128,1024]{1,0:T(8,128)(2,1)}, bf16[128,1024]{1,0:T(8,128)(2,1)S(1)}, u32[]{:S(2)}, u32[]{:S(2)}) collective-permute-start(bf16[128,1024]{1,0:T(8,128)(2,1)} %get-tuple-element.182.h0), channel_id=1, source_target_pairs={{0,1},{1,0},{2,3},{3,2},{4,5},{5,4},{6,7},{7,6},{8,9},{9,8},{10,11... | collective-permute-start | bytes 786440 | tf_op jit(solution)/shard_map/hidden_rows/ppermute | solution.py:27
  147.7 5.4 %collective-permute-done.22.h2 = bf16[128,1024]{1,0:T(8,128)(2,1)S(1)} collective-permute-done((bf16[128,1024]{1,0:T(8,128)(2,1)}, bf16[128,1024]{1,0:T(8,128)(2,1)S(1)}, u32[]{:S(2)}, u32[]{:S(2)}) %collective-permute-start.22) | collective-permute-done | bytes 262176 | tf_op jit(solution)/shard_map/hidden_rows/ppermute | solution.py:27
  159.4 10.4 %attn_backward.1 = (bf16[256,512]{1,0:T(8,128)(2,1)}, bf16[256,512]{1,0:T(8,128)(2,1)}, bf16[256,512]{1,0:T(8,128)(2,1)}, bf16[256,512]{1,0:T(8,128)(2,1)}, bf16...) custom-call(s32[4]{0:T(128)} %pad_add_fusion.place, ...), custom_call_target="tpu_custom_call" | custom-call | bytes 12066832 | tf_op jit(solution)/shard_map/attn_backward/pallas_call | solution.py:154
  169.8 4.1 %attn_return.1 = (f32[128,1024]{1,0:T(8,128)}, f32[128,1024]{1,0:T(8,128)}, bf16[256,1024]{1,0:T(8,128)(2,1)}) custom-call(s32[4]{0:T(128)} %pad_add_fusion.place, bf16[512,768]{1,0:T(8,128)(2,1)} %get-tuple-element.186.low, bf16[256,512]{1,0:T(8,128)(2,1)} %copy-done, bf16[256,512]{1,0:T(8,128)(2,1)} %copy-done.3, bf16[256,512]{1,0:T(8,128)(2,1)} %copy-done.4, ...), custom_call_target="tpu_custom_call" | custom-call | bytes 4980752 | tf_op jit(solution)/shard_map/attn_return/pallas_call | solution.py:154
  183.1 2.7 %collective-permute-done.28 = bf16[256,512]{1,0:T(8,128)(2,1)S(1)} collective-permute-done((bf16[256,512]{1,0:T(8,128)(2,1)}, bf16[256,512]{1,0:T(8,128)(2,1)S(1)}, u32[]{:S(2)}, u32[]{:S(2)}) %collective-permute-start.28) | collective-permute-done | bytes 262176 | tf_op jit(solution)/shard_map/attn_grads/ppermute | solution.py:66
  185.9 6.1 %collective-permute-done.29 = bf16[256,512]{1,0:T(8,128)(2,1)S(1)} collective-permute-done((bf16[256,512]{1,0:T(8,128)(2,1)}, bf16[256,512]{1,0:T(8,128)(2,1)S(1)}, u32[]{:S(2)}, u32[]{:S(2)}) %collective-permute-start.29) | collective-permute-done | bytes 262176 | tf_op jit(solution)/shard_map/attn_grads/ppermute | solution.py:66
  193.8 2.9 %input_back.1 = (f32[128,1024]{1,0:T(8,128)}, f32[2,1024]{1,0:T(2,128)}) custom-call(s32[4]{0:T(128)} %pad_add_fusion.place, f32[8,1024]{1,0:T(8,128)} %reshape.131.vec, bf16[128,1024]{1,0:T(8,128)(2,1)} %copy-done.1, f32[128,1024]{1,0:T(8,128)} %get-tuple-element.218.grad_hidden, f32[128,1024]{1,0:T(8,128)} %get-tuple-element.219.own, ...), custom_call_target="tpu_custom_call" | custom-call | bytes 2662416 | tf_op jit(solution)/shard_map/input_back/pallas_call | solution.py:154
  210.1 2.6 %all-to-all-start.1 = ((f32[32,1,384]{2,1,0:T(1,128)}), f32[32,1,384]{2,1,0:T(1,128)S(1)}, u32[]{:S(2)}, u32[]{:S(2)}) async-start(f32[32,1,384]{2,1,0:T(1,128)} %copy.83), calls=%async_computation.2 | async-start | bytes 98304 | tf_op jit(solution)/shard_map/small_grads/all_to_all | solution.py:695
  216.1 4.0 %all-to-all-done.1 = f32[32,1,384]{2,1,0:T(1,128)S(1)} async-done(((f32[32,1,384]{2,1,0:T(1,128)}), f32[32,1,384]{2,1,0:T(1,128)S(1)}, u32[]{:S(2)}, u32[]{:S(2)}) %all-to-all-start.1) | async-done | bytes 49184 | tf_op jit(solution)/shard_map/small_grads/all_to_all | solution.py:695
  (207 shorter events, 75.8 us)
Async XLA Ops:
  7.2 96.5 %all-gather.5.cloned.1.call-start = ((), (), s32[]{:S(2)}) async-start(), calls=%async_computation.4 | async-start | bytes 1310720 | tf_op jit(solution)/shard_map/grad_rows/all_gather | solution.py:530
  15.6 19.5 %collective-permute-start.1 = (bf16[256,512]{1,0:T(8,128)(2,1)S(1)}, bf16[256,512]{1,0:T(8,128)(2,1)S(1)}, u32[]{:S(2)}, u32[]{:S(2)}) collective-permute-start(bf16[256,512]{1,0:T(8,128)(2,1)S(1)} %maximum_select_fusion.2.n0), channel_id=1, source_target_pairs={{0,2},{1,3},{2,0},{3,1},{4,6},{5,7},{6,4},{7,5},{8,10},{9,11},{10,... | collective-permute-start | bytes 786440 | tf_op jit(solution)/shard_map/attn_weights/ppermute | solution.py:32
  19.3 15.8 %collective-permute-start.3 = (bf16[256,512]{1,0:T(8,128)(2,1)S(1)}, bf16[256,512]{1,0:T(8,128)(2,1)S(1)}, u32[]{:S(2)}, u32[]{:S(2)}) collective-permute-start(bf16[256,512]{1,0:T(8,128)(2,1)S(1)} %maximum_select_fusion.2.n0), channel_id=1, source_target_pairs={{0,8},{4,12},{8,0},{12,4},{16,24},{20,28},{24,16},{28,20},{1,9},{5... | collective-permute-start | bytes 786440 | tf_op jit(solution)/shard_map/attn_weights/ppermute | solution.py:66
  19.9 15.3 %collective-permute-start.4 = (bf16[256,512]{1,0:T(8,128)(2,1)S(1)}, bf16[256,512]{1,0:T(8,128)(2,1)S(1)}, u32[]{:S(2)}, u32[]{:S(2)}) collective-permute-start(bf16[256,512]{1,0:T(8,128)(2,1)S(1)} %maximum_select_fusion.2.n0), channel_id=1, source_target_pairs={{0,16},{4,20},{8,24},{12,28},{16,0},{20,4},{24,8},{28,12},{1,17},{... | collective-permute-start | bytes 786440 | tf_op jit(solution)/shard_map/attn_weights/ppermute | solution.py:66
  21.4 13.8 %collective-permute-start.5 = (bf16[256,512]{1,0:T(8,128)(2,1)S(1)}, bf16[256,512]{1,0:T(8,128)(2,1)S(1)}, u32[]{:S(2)}, u32[]{:S(2)}) collective-permute-start(bf16[256,512]{1,0:T(8,128)(2,1)S(1)} %maximum_select_fusion.2.n0), channel_id=1, source_target_pairs={{0,24},{4,28},{8,16},{12,20},{16,8},{20,12},{24,0},{28,4},{1,25},{... | collective-permute-start | bytes 786440 | tf_op jit(solution)/shard_map/attn_weights/ppermute | solution.py:66
  39.0 64.7 %all-gather.3.cloned.1.call-start = ((), (), s32[]{:S(2)}) async-start(), calls=%async_computation.3 | async-start | bytes 4718592 | tf_op jit(solution)/shard_map/mlp_weights/all_gather | solution.py:547
  41.8 13.4 %collective-permute-start.8 = (bf16[256,512]{1,0:T(8,128)(2,1)S(1)}, bf16[256,512]{1,0:T(8,128)(2,1)S(1)}, u32[]{:S(2)}, u32[]{:S(2)}) collective-permute-start(bf16[256,512]{1,0:T(8,128)(2,1)S(1)} %collective-permute-done.1.f0), channel_id=1, source_target_pairs={{0,8},{4,12},{8,0},{12,4},{16,24},{20,28},{24,16},{28,20},{1,9},{5... | collective-permute-start | bytes 786440 | tf_op jit(solution)/shard_map/attn_weights/ppermute | solution.py:66
  42.3 12.9 %collective-permute-start.9 = (bf16[256,512]{1,0:T(8,128)(2,1)S(1)}, bf16[256,512]{1,0:T(8,128)(2,1)S(1)}, u32[]{:S(2)}, u32[]{:S(2)}) collective-permute-start(bf16[256,512]{1,0:T(8,128)(2,1)S(1)} %collective-permute-done.1.f0), channel_id=1, source_target_pairs={{0,16},{4,20},{8,24},{12,28},{16,0},{20,4},{24,8},{28,12},{1,17},{... | collective-permute-start | bytes 786440 | tf_op jit(solution)/shard_map/attn_weights/ppermute | solution.py:66
  55.3 137.8 %reduce-scatter.2.cloned.1.call-start = ((), (), s32[]{:S(2)}) async-start(), calls=%async_computation.5 | async-start | bytes 2359296 | tf_op jit(solution)/shard_map/down_grads/reduce_scatter | solution.py:605
  82.1 21.6 %collective-permute-start.14 = (bf16[128,1024]{1,0:T(8,128)(2,1)}, bf16[128,1024]{1,0:T(8,128)(2,1)S(1)}, u32[]{:S(2)}, u32[]{:S(2)}) collective-permute-start(bf16[128,1024]{1,0:T(8,128)(2,1)} %get-tuple-element.155.a0), channel_id=1, source_target_pairs={{0,2},{1,3},{2,0},{3,1},{4,6},{5,7},{6,4},{7,5},{8,10},{9,11},{10,... | collective-permute-start | bytes 786440 | tf_op jit(solution)/shard_map/mlp_inputs/ppermute | solution.py:73
  84.4 19.2 %collective-permute-start.15 = (bf16[128,1024]{1,0:T(8,128)(2,1)}, bf16[128,1024]{1,0:T(8,128)(2,1)S(1)}, u32[]{:S(2)}, u32[]{:S(2)}) collective-permute-start(bf16[128,1024]{1,0:T(8,128)(2,1)} %get-tuple-element.155.a0), channel_id=1, source_target_pairs={{0,3},{1,2},{2,1},{3,0},{4,7},{5,6},{6,5},{7,4},{8,11},{9,10},{10,... | collective-permute-start | bytes 786440 | tf_op jit(solution)/shard_map/mlp_inputs/ppermute | solution.py:73
  113.8 14.9 %collective-permute-start.16 = (bf16[128,1024]{1,0:T(8,128)(2,1)}, bf16[128,1024]{1,0:T(8,128)(2,1)S(1)}, u32[]{:S(2)}, u32[]{:S(2)}) collective-permute-start(bf16[128,1024]{1,0:T(8,128)(2,1)} %get-tuple-element.167), channel_id=1, source_target_pairs={{0,1},{1,0},{2,3},{3,2},{4,5},{5,4},{6,7},{7,6},{8,9},{9,8},{10,11... | collective-permute-start | bytes 786440 | tf_op jit(solution)/shard_map/normed_return/ppermute | solution.py:73
  118.0 21.3 %collective-permute-start.17 = (bf16[128,1024]{1,0:T(8,128)(2,1)}, bf16[128,1024]{1,0:T(8,128)(2,1)S(1)}, u32[]{:S(2)}, u32[]{:S(2)}) collective-permute-start(bf16[128,1024]{1,0:T(8,128)(2,1)} %get-tuple-element.168), channel_id=1, source_target_pairs={{0,2},{1,3},{2,0},{3,1},{4,6},{5,7},{6,4},{7,5},{8,10},{9,11},{10,... | collective-permute-start | bytes 786440 | tf_op jit(solution)/shard_map/normed_return/ppermute | solution.py:73
  118.9 20.5 %collective-permute-start.18 = (bf16[128,1024]{1,0:T(8,128)(2,1)}, bf16[128,1024]{1,0:T(8,128)(2,1)S(1)}, u32[]{:S(2)}, u32[]{:S(2)}) collective-permute-start(bf16[128,1024]{1,0:T(8,128)(2,1)} %get-tuple-element.169), channel_id=1, source_target_pairs={{0,3},{1,2},{2,1},{3,0},{4,7},{5,6},{6,5},{7,4},{8,11},{9,10},{10,... | collective-permute-start | bytes 786440 | tf_op jit(solution)/shard_map/normed_return/ppermute | solution.py:73
  153.1 20.9 %collective-permute-start.19 = (bf16[128,1024]{1,0:T(8,128)(2,1)}, bf16[128,1024]{1,0:T(8,128)(2,1)S(1)}, u32[]{:S(2)}, u32[]{:S(2)}) collective-permute-start(bf16[128,1024]{1,0:T(8,128)(2,1)} %get-tuple-element.171), channel_id=1, source_target_pairs={{0,1},{1,0},{2,3},{3,2},{4,5},{5,4},{6,7},{7,6},{8,9},{9,8},{10,11... | collective-permute-start | bytes 786440 | tf_op jit(solution)/shard_map/mlp_return/ppermute | solution.py:73
  154.8 19.2 %collective-permute-start.20 = (bf16[128,1024]{1,0:T(8,128)(2,1)}, bf16[128,1024]{1,0:T(8,128)(2,1)S(1)}, u32[]{:S(2)}, u32[]{:S(2)}) collective-permute-start(bf16[128,1024]{1,0:T(8,128)(2,1)} %get-tuple-element.172), channel_id=1, source_target_pairs={{0,2},{1,3},{2,0},{3,1},{4,6},{5,7},{6,4},{7,5},{8,10},{9,11},{10,... | collective-permute-start | bytes 786440 | tf_op jit(solution)/shard_map/mlp_return/ppermute | solution.py:73
  155.9 18.1 %collective-permute-start.25 = (bf16[128,1024]{1,0:T(8,128)(2,1)}, bf16[128,1024]{1,0:T(8,128)(2,1)S(1)}, u32[]{:S(2)}, u32[]{:S(2)}) collective-permute-start(bf16[128,1024]{1,0:T(8,128)(2,1)} %get-tuple-element.191), channel_id=1, source_target_pairs={{0,8},{4,12},{8,0},{12,4},{16,24},{20,28},{24,16},{28,20},{1,9},{5... | collective-permute-start | bytes 786440 | tf_op jit(solution)/shard_map/up_grads/ppermute | solution.py:66
  157.2 16.8 %collective-permute-start.26 = (bf16[128,1024]{1,0:T(8,128)(2,1)S(1)}, bf16[128,1024]{1,0:T(8,128)(2,1)S(1)}, u32[]{:S(2)}, u32[]{:S(2)}) collective-permute-start(bf16[128,1024]{1,0:T(8,128)(2,1)S(1)} %get-tuple-element.192), channel_id=1, source_target_pairs={{0,16},{4,20},{8,24},{12,28},{16,0},{20,4},{24,8},{28,12},{1,17},{... | collective-permute-start | bytes 786440 | tf_op jit(solution)/shard_map/up_grads/ppermute | solution.py:66
  158.4 15.6 %collective-permute-start.27 = (bf16[128,1024]{1,0:T(8,128)(2,1)S(1)}, bf16[128,1024]{1,0:T(8,128)(2,1)S(1)}, u32[]{:S(2)}, u32[]{:S(2)}) collective-permute-start(bf16[128,1024]{1,0:T(8,128)(2,1)S(1)} %get-tuple-element.193), channel_id=1, source_target_pairs={{0,24},{4,28},{8,16},{12,20},{16,8},{20,12},{24,0},{28,4},{1,25},{... | collective-permute-start | bytes 786440 | tf_op jit(solution)/shard_map/up_grads/ppermute | solution.py:66
  174.9 30.8 %collective-permute-start.33 = (bf16[128,1024]{1,0:T(8,128)(2,1)}, bf16[128,1024]{1,0:T(8,128)(2,1)}, u32[]{:S(2)}, u32[]{:S(2)}) collective-permute-start(bf16[128,1024]{1,0:T(8,128)(2,1)} %get-tuple-element.217), channel_id=1, source_target_pairs={{0,3},{1,2},{2,1},{3,0},{4,7},{5,6},{6,5},{7,4},{8,11},{9,10},{10,... | collective-permute-start | bytes 786440 | tf_op jit(solution)/shard_map/mlp_return/ppermute | solution.py:73
  178.0 14.0 %collective-permute-start.29 = (bf16[256,512]{1,0:T(8,128)(2,1)}, bf16[256,512]{1,0:T(8,128)(2,1)S(1)}, u32[]{:S(2)}, u32[]{:S(2)}) collective-permute-start(bf16[256,512]{1,0:T(8,128)(2,1)} %get-tuple-element.204), channel_id=1, source_target_pairs={{0,16},{4,20},{8,24},{12,28},{16,0},{20,4},{24,8},{28,12},{1,17},{... | collective-permute-start | bytes 786440 | tf_op jit(solution)/shard_map/attn_grads/ppermute | solution.py:66
  179.1 13.0 %collective-permute-start.30 = (bf16[256,512]{1,0:T(8,128)(2,1)}, bf16[256,512]{1,0:T(8,128)(2,1)S(1)}, u32[]{:S(2)}, u32[]{:S(2)}) collective-permute-start(bf16[256,512]{1,0:T(8,128)(2,1)} %get-tuple-element.205), channel_id=1, source_target_pairs={{0,24},{4,28},{8,16},{12,20},{16,8},{20,12},{24,0},{28,4},{1,25},{... | collective-permute-start | bytes 786440 | tf_op jit(solution)/shard_map/attn_grads/ppermute | solution.py:66
  199.4 13.4 %collective-permute-start.35 = (bf16[256,512]{1,0:T(8,128)(2,1)}, bf16[256,512]{1,0:T(8,128)(2,1)}, u32[]{:S(2)}, u32[]{:S(2)}) collective-permute-start(bf16[256,512]{1,0:T(8,128)(2,1)} %get-tuple-element.230), channel_id=1, source_target_pairs={{0,8},{4,12},{8,0},{12,4},{16,24},{20,28},{24,16},{28,20},{1,9},{5... | collective-permute-start | bytes 786440 | tf_op jit(solution)/shard_map/attn_grads/ppermute | solution.py:66
  201.7 12.9 %collective-permute-start.37 = (bf16[256,512]{1,0:T(8,128)(2,1)}, bf16[256,512]{1,0:T(8,128)(2,1)}, u32[]{:S(2)}, u32[]{:S(2)}) collective-permute-start(bf16[256,512]{1,0:T(8,128)(2,1)} %add_convert_fusion.2), channel_id=1, source_target_pairs={{0,2},{1,3},{2,0},{3,1},{4,6},{5,7},{6,4},{7,5},{8,10},{9,11},{10,... | collective-permute-start | bytes 786440 | tf_op jit(solution)/shard_map/attn_grads/ppermute | solution.py:32
  (56 other events, 633.4 us)
Sparse Core Ops, SparseCore 0:
  35.3 27.0 all-gather.4
  64.3 36.1 all-gather.2
  128.8 45.6 reduce-scatter.1
